TPU v7x, 32 devices: a whole 2x2x4 slice. The times are simulated.
32 devices in a mesh: dp: 16 (over z, y, core), tensor: 2 (over x).
Axes of the slice: x: 2, y: 2, z: 4, core: 2. Of those that a mesh axis runs over, the one named last changes fastest.
Arguments:
- inputs: bfloat16 [16, 1024, 768], P('dp', 'tensor'), may hold values from -6 to 6
- lengths: int32 [16], P('dp'), may hold values from 256 to 1024, as said below
- w_qkv: bfloat16 [3, 768, 768], P(None, 'dp', 'tensor'), may hold values from -0.21875 to 0.21875
- b_qv: float32 [2, 768], P(None, 'tensor'), may hold values from -2 to 2
- w_out: bfloat16 [768, 768], P('tensor', 'dp'), may hold values from -1.75 to 1.75
- b_out: float32 [768], replicated, may hold values from -2 to 2
- ln1_gain: float32 [768], replicated, may hold values from 0.5 to 1.5
- ln1_bias: float32 [768], replicated, may hold values from -2 to 2
- w_in: bfloat16 [768, 3072], P('dp', 'tensor'), may hold values from -0.21875 to 0.21875
- b_in: float32 [3072], P('tensor'), may hold values from -2 to 2
- w_hid: bfloat16 [3072, 768], P('tensor', 'dp'), may hold values from -0.109375 to 0.109375
- b_hid: float32 [768], replicated, may hold values from -2 to 2
- ln2_gain: float32 [768], replicated, may hold values from 0.5 to 1.5
- ln2_bias: float32 [768], replicated, may hold values from -2 to 2
- mask_logits: float32 [12, 1024, 1024], P('tensor', 'dp'), may hold values from -6 to 6
- noise: float32 [12, 1024, 1024], P('tensor', 'dp'), may hold values from -6 to 6
- cotangent: float32 [16, 1024, 768], P('dp', 'tensor'), may hold values from -6 to 6
Outputs:
- outputs: bfloat16 [16, 1024, 768], P('dp', 'tensor')
- input_grad: float32 [16, 1024, 768], P('dp', 'tensor')
- grad_w_qkv: float32 [3, 768, 768], P(None, 'dp', 'tensor')
- grad_b_qv: float32 [2, 768], P(None, 'tensor')
- grad_w_out: float32 [768, 768], P('tensor', 'dp')
- grad_b_out: float32 [768], replicated
- grad_ln1_gain: float32 [768], replicated
- grad_ln1_bias: float32 [768], replicated
- grad_w_in: float32 [768, 3072], P('dp', 'tensor')
- grad_b_in: float32 [3072], P('tensor')
- grad_w_hid: float32 [3072, 768], P('tensor', 'dp')
- grad_b_hid: float32 [768], replicated
- grad_ln2_gain: float32 [768], replicated
- grad_ln2_bias: float32 [768], replicated
- grad_mask_logits: float32 [12, 1024, 1024], P('tensor', 'dp')
Inputs may be any that keep to these rules, and one draw needn't show every extreme that they name: `lengths`: some sequence fills all 1024 slots and some has exactly 256 valid tokens.
All inputs are finite; a program needn't handle non-finite values.
Results may differ from a plain program's by a relative error of at most 0.014.
Values may be sent and summed in bfloat16 or wider, within the bound.
A program may use at most 192 MiB of HBM per device.

v0:
```python
import jax
import jax.numpy as jnp
from jax import lax
from jax.sharding import PartitionSpec as P

NEG = -1e30
EPS = 1e-12


def layer_norm(value_rows, scale_vec, shift_vec):
    centre = value_rows - jnp.mean(value_rows, axis=-1, keepdims=True)
    spread = jnp.mean(centre * centre, axis=-1, keepdims=True)
    return centre * lax.rsqrt(spread + EPS) * scale_vec + shift_vec


def gelu_exact(value_rows):
    return jax.nn.gelu(value_rows, approximate=False)


def matmul(left, right):
    return jnp.dot(left, right, preferred_element_type=jnp.float32)


def times_transposed(left, right):
    return lax.dot_general(
        left, right, (((1,), (1,)), ((), ())), preferred_element_type=jnp.float32
    )


def over_rows(left, right):
    return lax.dot_general(
        left, right, (((0,), (0,)), ((), ())), preferred_element_type=jnp.float32
    )


def body(
    inputs,
    lengths,
    w_qkv,
    b_qv,
    w_out,
    b_out,
    ln1_gain,
    ln1_bias,
    w_in,
    b_in,
    w_hid,
    b_hid,
    ln2_gain,
    ln2_bias,
    mask_logits,
    noise,
    cotangent,
):
    seq_count, half_rows, width = inputs.shape
    slot_len = half_rows * lax.axis_size("tensor")
    tensor_rank = lax.axis_index("tensor")
    head_count = mask_logits.shape[0]
    head_dim = w_qkv.shape[2] // head_count
    scale = head_dim ** (-0.5)
    token_count = seq_count * slot_len
    mixed_logits = mask_logits + noise
    local_mask = jax.nn.log_sigmoid(mixed_logits).astype(jnp.bfloat16)
    full_qkv, full_out, full_in, full_hid, full_mask = (
        lax.all_gather(w_qkv, "dp", axis=1, tiled=True),
        lax.all_gather(w_out, "dp", axis=1, tiled=True),
        lax.all_gather(w_in, "dp", axis=0, tiled=True),
        lax.all_gather(w_hid, "dp", axis=1, tiled=True),
        lax.all_gather(local_mask, "dp", axis=1, tiled=True),
    )
    key_valid = jnp.arange(slot_len, dtype=jnp.int32)[None, :] < lengths[:, None]
    own_rows = tensor_rank * half_rows + jnp.arange(half_rows, dtype=jnp.int32)
    row_valid = (own_rows[None, :] < lengths[:, None]).astype(jnp.float32)
    gathered = lax.all_gather(inputs, "tensor", axis=1, tiled=True)
    flat_rows = gathered.reshape(token_count, width)
    query_rows = (matmul(flat_rows, full_qkv[0]) + b_qv[0]).astype(jnp.bfloat16)
    key_rows = matmul(flat_rows, full_qkv[1]).astype(jnp.bfloat16)
    value_rows = (matmul(flat_rows, full_qkv[2]) + b_qv[1]).astype(jnp.bfloat16)

    def split_heads(matrix):
        return matrix.reshape(seq_count, slot_len, head_count, head_dim).transpose(0, 2, 1, 3)

    def join_heads(stacked):
        return stacked.transpose(0, 2, 1, 3).reshape(token_count, head_count * head_dim)

    def masked_scores(query_h, keys_h, mask_h, valid_keys):
        score_matrix = (
            jnp.einsum("qd,kd->qk", query_h, keys_h, preferred_element_type=jnp.float32) * scale
        )
        score_matrix = score_matrix + mask_h.astype(jnp.float32)
        return jnp.where(valid_keys[None, :], score_matrix, NEG)

    def attend_sequence(operands):
        query_s, keys_s, values_s, valid_keys = operands

        def attend_head(head_ops):
            query_h, keys_h, values_h, mask_h = head_ops
            score_matrix = masked_scores(query_h, keys_h, mask_h, valid_keys)
            top_score = jnp.max(score_matrix, axis=-1, keepdims=True)
            expo = jnp.exp(score_matrix - top_score)
            row_total = jnp.sum(expo, axis=-1, keepdims=True)
            attention_probabilities = (expo / row_total).astype(jnp.bfloat16)
            result = jnp.einsum(
                "qk,kd->qd", attention_probabilities, values_h, preferred_element_type=jnp.float32
            )
            return (result.astype(jnp.bfloat16), (top_score + jnp.log(row_total))[:, 0])

        return lax.map(attend_head, (query_s, keys_s, values_s, full_mask))

    head_out, log_total = lax.map(
        attend_sequence,
        (split_heads(query_rows), split_heads(key_rows), split_heads(value_rows), key_valid),
    )
    attn = join_heads(head_out)
    attn_terms = matmul(attn, full_out).reshape(seq_count, slot_len, width)
    attn_part = lax.psum_scatter(attn_terms, "tensor", scatter_dimension=1, tiled=True)
    first_sum = inputs.astype(jnp.float32) + attn_part + b_out
    hidden_one = layer_norm(first_sum, ln1_gain, ln1_bias)
    hidden_rows = lax.all_gather(
        hidden_one.astype(jnp.bfloat16), "tensor", axis=1, tiled=True
    ).reshape(token_count, width)
    pre_act = matmul(hidden_rows, full_in) + b_in
    activated = gelu_exact(pre_act).astype(jnp.bfloat16)
    ffn_terms = matmul(activated, full_hid).reshape(seq_count, slot_len, width)
    ffn_part = lax.psum_scatter(ffn_terms, "tensor", scatter_dimension=1, tiled=True)
    second_sum = hidden_one + ffn_part + b_hid
    outputs = layer_norm(second_sum, ln2_gain, ln2_bias).astype(jnp.bfloat16)
    back_qkv, back_out, back_in, back_hid, back_mask = (
        lax.all_gather(w_qkv, "dp", axis=1, tiled=True),
        lax.all_gather(w_out, "dp", axis=1, tiled=True),
        lax.all_gather(w_in, "dp", axis=0, tiled=True),
        lax.all_gather(w_hid, "dp", axis=1, tiled=True),
        lax.all_gather(local_mask, "dp", axis=1, tiled=True),
    )
    grad_output = cotangent * row_valid[:, :, None]
    _, pull_second = jax.vjp(layer_norm, second_sum, ln2_gain, ln2_bias)
    grad_second, ln2_gain_part, ln2_bias_part = pull_second(grad_output)
    b_hid_part = jnp.sum(grad_second, axis=(0, 1))
    second_rows = lax.all_gather(
        grad_second.astype(jnp.bfloat16), "tensor", axis=1, tiled=True
    ).reshape(token_count, width)
    w_hid_grad = over_rows(activated, second_rows)
    grad_act = times_transposed(second_rows, back_hid)
    _, pull_gelu = jax.vjp(gelu_exact, pre_act)
    grad_pre = pull_gelu(grad_act)[0].astype(jnp.bfloat16)
    b_in_part = jnp.sum(grad_pre.astype(jnp.float32), axis=0)
    w_in_grad = over_rows(hidden_rows, grad_pre)
    hidden_terms = times_transposed(grad_pre, back_in).reshape(seq_count, slot_len, width)
    grad_hidden = grad_second + lax.psum_scatter(
        hidden_terms, "tensor", scatter_dimension=1, tiled=True
    )
    _, pull_first = jax.vjp(layer_norm, first_sum, ln1_gain, ln1_bias)
    grad_first, ln1_gain_part, ln1_bias_part = pull_first(grad_hidden)
    b_out_part = jnp.sum(grad_first, axis=(0, 1))
    first_rows = lax.all_gather(
        grad_first.astype(jnp.bfloat16), "tensor", axis=1, tiled=True
    ).reshape(token_count, width)
    w_out_grad = over_rows(attn, first_rows)
    grad_attn = times_transposed(first_rows, back_out).astype(jnp.bfloat16)

    def sequence_back(mask_acc, operands):
        query_s, keys_s, values_s, grad_s, total_s, valid_keys = operands

        def head_back(head_ops):
            query_h, keys_h, values_h, mask_h, grad_h, total_h = head_ops
            score_matrix = masked_scores(query_h, keys_h, mask_h, valid_keys)
            attention_probabilities = jnp.exp(score_matrix - total_h[:, None])
            grad_probs = jnp.einsum(
                "qd,kd->qk", grad_h, values_h, preferred_element_type=jnp.float32
            )
            centre = jnp.sum(attention_probabilities * grad_probs, axis=-1, keepdims=True)
            grad_scores = (attention_probabilities * (grad_probs - centre)).astype(jnp.bfloat16)
            grad_q = (
                jnp.einsum("qk,kd->qd", grad_scores, keys_h, preferred_element_type=jnp.float32)
                * scale
            ).astype(jnp.bfloat16)
            grad_k = (
                jnp.einsum("qk,qd->kd", grad_scores, query_h, preferred_element_type=jnp.float32)
                * scale
            ).astype(jnp.bfloat16)
            grad_v = jnp.einsum(
                "qk,qd->kd",
                attention_probabilities.astype(jnp.bfloat16),
                grad_h,
                preferred_element_type=jnp.float32,
            ).astype(jnp.bfloat16)
            return (grad_q, grad_k, grad_v, grad_scores)

        grad_q, grad_k, grad_v, grad_sc = lax.map(
            head_back, (query_s, keys_s, values_s, back_mask, grad_s, total_s)
        )
        return (mask_acc + grad_sc.astype(jnp.float32), (grad_q, grad_k, grad_v))

    mask_zero = jnp.zeros(back_mask.shape, jnp.float32)
    mask_grad, (heads_q, heads_k, heads_v) = lax.scan(
        sequence_back,
        mask_zero,
        (
            split_heads(query_rows),
            split_heads(key_rows),
            split_heads(value_rows),
            split_heads(grad_attn),
            log_total,
            key_valid,
        ),
    )
    query_grad = join_heads(heads_q)
    keys_grad = join_heads(heads_k)
    values_grad = join_heads(heads_v)
    b_qv_part = jnp.stack(
        [
            jnp.sum(query_grad.astype(jnp.float32), axis=0),
            jnp.sum(values_grad.astype(jnp.float32), axis=0),
        ]
    )
    w_qkv_grad = jnp.stack(
        [
            over_rows(flat_rows, query_grad),
            over_rows(flat_rows, keys_grad),
            over_rows(flat_rows, values_grad),
        ]
    )
    input_terms = (
        times_transposed(query_grad, back_qkv[0])
        + times_transposed(keys_grad, back_qkv[1])
        + times_transposed(values_grad, back_qkv[2])
    ).reshape(seq_count, slot_len, width)
    input_grad = grad_first + lax.psum_scatter(
        input_terms.astype(jnp.bfloat16), "tensor", scatter_dimension=1, tiled=True
    ).astype(jnp.float32)
    qkv_total, out_total, in_total, hid_total, mask_total = (
        lax.psum_scatter(w_qkv_grad, "dp", scatter_dimension=1, tiled=True),
        lax.psum_scatter(w_out_grad, "dp", scatter_dimension=1, tiled=True),
        lax.psum_scatter(w_in_grad, "dp", scatter_dimension=0, tiled=True),
        lax.psum_scatter(w_hid_grad, "dp", scatter_dimension=1, tiled=True),
        lax.psum_scatter(mask_grad, "dp", scatter_dimension=1, tiled=True),
    )
    mask_logit_grad = mask_total * jax.nn.sigmoid(-mixed_logits)
    ln1_gain_total, ln1_bias_total, ln2_gain_total, ln2_bias_total, b_out_total, b_hid_total = (
        lax.psum(
            (ln1_gain_part, ln1_bias_part, ln2_gain_part, ln2_bias_part, b_out_part, b_hid_part),
            ("dp", "tensor"),
        )
    )
    b_qv_total, b_in_total = lax.psum((b_qv_part, b_in_part), "dp")
    return (
        outputs,
        input_grad,
        qkv_total,
        b_qv_total,
        out_total,
        b_out_total,
        ln1_gain_total,
        ln1_bias_total,
        in_total,
        b_in_total,
        hid_total,
        b_hid_total,
        ln2_gain_total,
        ln2_bias_total,
        mask_logit_grad,
    )


def solution(mesh):
    placed = (
        P("dp", "tensor", None),
        P("dp"),
        P(None, "dp", "tensor"),
        P(None, "tensor"),
        P("tensor", "dp"),
        P(),
        P(),
        P(),
        P("dp", "tensor"),
        P("tensor"),
        P("tensor", "dp"),
        P(),
        P(),
        P(),
        P("tensor", "dp", None),
        P("tensor", "dp", None),
        P("dp", "tensor", None),
    )
    return jax.shard_map(
        body,
        mesh=mesh,
        in_specs=placed,
        out_specs=(
            P("dp", "tensor", None),
            P("dp", "tensor", None),
            P(None, "dp", "tensor"),
            P(None, "tensor"),
            P("tensor", "dp"),
            P(),
            P(),
            P(),
            P("dp", "tensor"),
            P("tensor"),
            P("tensor", "dp"),
            P(),
            P(),
            P(),
            P("tensor", "dp", None),
        ),
        check_vma=False,
    )
```

profile of v0, /device:TPU:0, one launch (start us, length us, event | category | flops | bytes accessed | tf_op | source)
XLA Modules:
  0.0 1337.9 jit_solution(16423183789566875789)
XLA Ops:
  8.7 3.8 fusion.65
  12.6 26.2 %all_gather.35 = bf16[384,768]{0,1:T(8,128)(2,1)} all-gather(bf16[384,48]{0,1:T(8,128)(2,1)S(1)} %copy-done.21), channel_id=1, replica_groups=mesh['dp'=16,'tensor'=2] {'dp'}, dimensions={1}, use_global_device_ids=true | all-gather | bytes 626688 | tf_op jit(solution)/shard_map/all_gather | solution.py:66
  39.5 42.8 %all-gather.11.cloned.1.call-done = bf16[3,768,384]{2,1,0:T(8,128)(2,1)} async-done(((bf16[3,48,384]{2,1,0:T(8,128)(2,1)}), bf16[3,768,384]{2,1,0:T(8,128)(2,1)}) %all-gather.11.cloned.1.call-update) | async-done | bytes 1769488 | tf_op jit(solution)/shard_map/all_gather | solution.py:65
  85.5 3.2 fusion.97
  90.5 3.5 add_convert_fusion.3
  96.4 88.4 %all-gather.13.cloned.1.call-done = bf16[6,1024,1024]{2,1,0:T(8,128)(2,1)} async-done(((bf16[6,64,1024]{2,1,0:T(8,128)(2,1)}), bf16[6,1024,1024]{2,1,0:T(8,128)(2,1)}) %all-gather.13.cloned.1.call-update) | async-done | bytes 12582928 | tf_op jit(solution)/shard_map/all_gather | solution.py:69
  184.8 16.6 %copy.43 = bf16[6,1024,1024]{1,2,0:T(8,128)(2,1)} copy(bf16[6,1024,1024]{2,1,0:T(8,128)(2,1)} %all-gather.13.cloned.1.call-done) | data formatting | bytes 25165824
  202.4 38.2 %while.52 = (s32[]{:T(128)}, bf16[6,1024,64]{1,2,0:T(8,128)(2,1)}, f32[6,1024]{1,0:T(8,128)S(1)}, bf16[6,1024,64]{2,1,0:T(8,128)(2,1)S(1)}, bf16[6,1024,64]{2,1,...) while((s32[]{:T(128)}, bf16[6,1024,64]{1,2,0:T(8,128)(2,1)}, ...), condition=%wide.region_3.4_spmd.clone, body=%wide.region_0.3_spmd.clone.sunk | while | flops 278986752 | bytes 15643253 | solution.py:108
  240.6 4.5 convolution_bitcast_fusion.2
  245.8 41.0 %reduce-scatter.9.cloned.1.call-done = f32[1,512,768]{2,1,0:T(8,128)} async-done(((f32[1,1024,768]{2,1,0:T(8,128)}), f32[1,512,768]{2,1,0:T(8,128)}) %reduce-scatter.9.cloned.1.call-update) | async-done | bytes 1572880 | tf_op jit(solution)/shard_map/reduce_scatter | solution.py:116
  291.2 40.2 %all-gather.17.cloned.1.call-done = bf16[768,1536]{1,0:T(8,128)(2,1)} async-done(((bf16[48,1536]{1,0:T(8,128)(2,1)}), bf16[768,1536]{1,0:T(8,128)(2,1)}) %all-gather.17.cloned.1.call-update) | async-done | bytes 2359312 | tf_op jit(solution)/shard_map/all_gather | solution.py:67
  331.5 28.1 %all-gather.15.cloned.1.call-done = bf16[1,1024,768]{2,1,0:T(8,128)(2,1)} async-done(((bf16[1,512,768]{2,1,0:T(8,128)(2,1)}), bf16[1,1024,768]{2,1,0:T(8,128)(2,1)}) %all-gather.15.cloned.1.call-update) | async-done | bytes 1572880 | tf_op jit(solution)/shard_map/all_gather | solution.py:119
  359.5 20.0 %multiply_convert_fusion.1 = (bf16[1024,1536]{1,0:T(8,128)(2,1)}, f32[1024,1536]{1,0:T(8,128)}, f32[1024,1536]{1,0:T(8,128)}) fusion(f32[1536]{0:T(1024)S(1)} %copy-done.35, bf16[768,1536]{1,0:T(8,128)(2,1)} %all-gather.17.cloned.1.call-done, bf16[1,1024,768]{2,1,0:T(8,128)(2,1)} %all-gather.15.cloned.1.call-done), kind=kOutput, calls=%fused_computation.67 | convolution fusion | flops 2519728128 | bytes 19666944 | tf_op jit(solution)/shard_map/dot_general | solution.py:21
  379.5 24.8 %all-gather.19.cloned.1.call-done = bf16[1536,768]{0,1:T(8,128)(2,1)} async-done(((bf16[1536,48]{0,1:T(8,128)(2,1)}), bf16[1536,768]{0,1:T(8,128)(2,1)}) %all-gather.19.cloned.1.call-update) | async-done | bytes 2359312 | tf_op jit(solution)/shard_map/all_gather | solution.py:68
  404.3 7.0 convolution_bitcast_fusion.1
  412.1 41.5 %reduce-scatter.11.cloned.1.call-done = f32[1,512,768]{2,1,0:T(8,128)} async-done(((f32[1,1024,768]{2,1,0:T(8,128)}), f32[1,512,768]{2,1,0:T(8,128)}) %reduce-scatter.11.cloned.1.call-update) | async-done | bytes 1572880 | tf_op jit(solution)/shard_map/reduce_scatter | solution.py:125
  460.9 27.3 %all-gather.21.cloned.1.call-done = bf16[1,1024,768]{2,1,0:T(8,128)(2,1)} async-done(((bf16[1,512,768]{2,1,0:T(8,128)(2,1)}), bf16[1,1024,768]{2,1,0:T(8,128)(2,1)}) %all-gather.21.cloned.1.call-update) | async-done | bytes 1572880 | tf_op jit(solution)/shard_map/all_gather | solution.py:139
  488.2 10.9 convert_reduce_fusion
  500.8 4.3 convolution_bitcast_fusion
  505.1 43.5 %reduce-scatter.13.cloned.1.call-done = f32[1,512,768]{2,1,0:T(8,128)} async-done(((f32[1,1024,768]{2,1,0:T(8,128)}), f32[1,512,768]{2,1,0:T(8,128)}) %reduce-scatter.13.cloned.1.call-update) | async-done | bytes 1572880 | tf_op jit(solution)/shard_map/reduce_scatter | solution.py:149
  548.6 3.3 multiply_reduce_fusion.2
  555.6 27.1 %all-gather.23.cloned.1.call-done = bf16[1,1024,768]{2,1,0:T(8,128)(2,1)} async-done(((bf16[1,512,768]{2,1,0:T(8,128)(2,1)}), bf16[1,1024,768]{2,1,0:T(8,128)(2,1)}) %all-gather.23.cloned.1.call-update) | async-done | bytes 1572880 | tf_op jit(solution)/shard_map/all_gather | solution.py:155
  582.7 3.1 fusion.100
  590.6 117.2 %while.53 = (s32[]{:T(128)}, bf16[6,1024,64]{1,2,0:T(8,128)(2,1)}, bf16[6,1024,64]{1,2,0:T(8,128)(2,1)}, bf16[6,1024,64]{1,2,0:T(8,128)(2,1)}, bf16[6,1024,1024]...) while((s32[]{:T(128)}, bf16[6,1024,64]{1,2,0:T(8,128)(2,1)}, ...), condition=%wide.region_17.18_spmd.clone, body=%wide.region_15.17_spmd.clone.sunk | while | flops 682950656 | bytes 56782592 | solution.py:189
  593.1 3.2 multiply_reduce_fusion.9
  606.9 3.3 constant_dynamic-update-slice_fusion.2
  612.7 3.2 multiply_reduce_fusion.9
  626.4 3.2 constant_dynamic-update-slice_fusion.2
  632.2 3.2 multiply_reduce_fusion.9
  645.9 3.2 constant_dynamic-update-slice_fusion.2
  651.8 3.2 multiply_reduce_fusion.9
  665.5 3.2 constant_dynamic-update-slice_fusion.2
  671.2 3.2 multiply_reduce_fusion.9
  685.0 3.3 constant_dynamic-update-slice_fusion.2
  690.8 3.2 multiply_reduce_fusion.9
  704.5 3.3 constant_dynamic-update-slice_fusion.2
  712.6 3.9 copy.46
  723.5 14.4 %convert_element_type.121 = f32[6,1024,1024]{2,1,0:T(8,128)} convert(bf16[6,1024,1024]{2,1,0:T(8,128)(2,1)} %get-tuple-element.188) | non-fusion elementwise | flops 6291456 | bytes 37748736 | tf_op jit(solution)/shard_map/while/body/eval_jaxpr/convert_element_type | solution.py:192
  739.3 6.2 fusion.76
  747.0 6.2 fusion.70
  754.3 3.5 fusion.66
  759.1 40.1 %all-reduce.1 = (f32[768]{0:T(1024)}, f32[768]{0:T(1024)}, f32[768]{0:T(1024)}, f32[768]{0:T(1024)}, f32[768]{0:T(1024)}, /*index=5*/f32[768]{0:T(1024)}) all-reduce(f32[768]{0:T(1024)S(1)} %copy-done.23, f32[768]{0:T(1024)S(1)} %copy-done.25, f32[768]{0:T(1024)S(1)} %copy-done.26, ...), channel_id=1, replica_groups=mesh['dp'=16,'tensor'=2] {'dp','tensor'}, use_global_device_ids=true, to_apply=%region_25.26 | all-reduce | flops 4608 | bytes 36864 | tf_op jit(solution)/shard_map/psum | solution.py:240
  799.7 61.5 %all-reduce.2 = (f32[2,384]{1,0:T(2,128)}, f32[1536]{0:T(1024)}) all-reduce(f32[2,384]{1,0:T(2,128)S(1)} %pad_maximum_fusion.1, f32[1536]{0:T(1024)S(1)} %copy-done.27), channel_id=1, replica_groups=mesh['dp'=16,'tensor'=2] {'dp'}, use_global_device_ids=true, to_apply=%region_22.23 | all-reduce | flops 2304 | bytes 18432 | tf_op jit(solution)/shard_map/psum | solution.py:245
  866.0 245.4 %reduce-scatter.23.cloned.1.call-done = f32[6,64,1024]{2,1,0:T(8,128)} async-done(((f32[6,1024,1024]{2,1,0:T(8,128)}), f32[6,64,1024]{2,1,0:T(8,128)}) %reduce-scatter.23.cloned.1.call-update) | async-done | bytes 1572880 | tf_op jit(solution)/shard_map/reduce_scatter | solution.py:236
  1111.4 3.6 divide_multiply_fusion
  1115.0 75.4 %reduce-scatter.19.cloned.1.call-done = f32[48,1536]{1,0:T(8,128)} async-done(((f32[768,1536]{1,0:T(8,128)}), f32[48,1536]{1,0:T(8,128)}) %reduce-scatter.19.cloned.1.call-update) | async-done | bytes 294928 | tf_op jit(solution)/shard_map/reduce_scatter | solution.py:234
  1190.4 79.4 %reduce-scatter.21.cloned.1.call-done = f32[1536,48]{0,1:T(8,128)} async-done(((f32[1536,768]{0,1:T(8,128)}), f32[1536,48]{0,1:T(8,128)}) %reduce-scatter.21.cloned.1.call-update) | async-done | bytes 294928 | tf_op jit(solution)/shard_map/reduce_scatter | solution.py:235
  1269.8 61.2 %reduce-scatter.17.cloned.1.call-done = f32[384,48]{0,1:T(8,128)} async-done(((f32[384,768]{0,1:T(8,128)}), f32[384,48]{0,1:T(8,128)}) %reduce-scatter.17.cloned.1.call-update) | async-done | bytes 73744 | tf_op jit(solution)/shard_map/reduce_scatter | solution.py:233
  (281 shorter events, 170.6 us)
Async XLA Ops:
  7.2 32.3 %all-gather.9.cloned.1.call-start = ((), (), s32[]{:S(2)}) async-start(), calls=%async_computation.8 | async-start | bytes 2359296 | tf_op jit(solution)/shard_map/all_gather | solution.py:74
  7.9 74.4 %all-gather.11.cloned.1.call-start = ((), (), s32[]{:S(2)}) async-start(), calls=%async_computation.9 | async-start | bytes 1880064 | tf_op jit(solution)/shard_map/all_gather | solution.py:65
  8.7 3.9 copy-start.31
  8.7 3.9 copy-start.21
  8.7 176.1 %all-gather.13.cloned.1.call-start = ((), (), s32[]{:S(2)}) async-start(), calls=%async_computation.10 | async-start | bytes 13369344 | tf_op jit(solution)/shard_map/all_gather | solution.py:69
  12.5 274.3 %reduce-scatter.9.cloned.1.call-start = ((), (), s32[]{:S(2)}) async-start(), calls=%async_computation.11 | async-start | bytes 4718592 | tf_op jit(solution)/shard_map/reduce_scatter | solution.py:116
  240.6 5.2 copy-start.2
  245.1 41.7 %copy-start.29 = (f32[768]{0:T(1024)S(1)}, f32[768]{0:T(1024)}, u32[]{:S(2)}) copy-start(f32[768]{0:T(1024)} %param.26) | copy-start | bytes 9220
  245.1 86.3 %all-gather.17.cloned.1.call-start = ((), (), s32[]{:S(2)}) async-start(), calls=%async_computation.13 | async-start | bytes 2506752 | tf_op jit(solution)/shard_map/all_gather | solution.py:67
  245.7 43.3 %copy-start.20 = (f32[768]{0:T(1024)S(1)}, f32[768]{0:T(1024)}, u32[]{:S(2)}) copy-start(f32[768]{0:T(1024)} %param.27) | copy-start | bytes 9220
  245.7 43.3 %copy-start.24 = (f32[768]{0:T(1024)S(1)}, f32[768]{0:T(1024)}, u32[]{:S(2)}) copy-start(f32[768]{0:T(1024)} %param.28) | copy-start | bytes 9220
  245.8 113.8 %all-gather.15.cloned.1.call-start = ((), (), s32[]{:S(2)}) async-start(), calls=%async_computation.12 | async-start | bytes 2359296 | tf_op jit(solution)/shard_map/all_gather | solution.py:119
  288.7 70.8 %copy-start.35 = (f32[1536]{0:T(1024)S(1)}, f32[1536]{0:T(1024)}, u32[]{:S(2)}) copy-start(f32[1536]{0:T(1024)} %param.30) | copy-start | bytes 18436
  290.3 114.1 %all-gather.19.cloned.1.call-start = ((), (), s32[]{:S(2)}) async-start(), calls=%async_computation.14 | async-start | bytes 2506752 | tf_op jit(solution)/shard_map/all_gather | solution.py:68
  291.0 162.6 %reduce-scatter.11.cloned.1.call-start = ((), (), s32[]{:S(2)}) async-start(), calls=%async_computation.15 | async-start | bytes 4718592 | tf_op jit(solution)/shard_map/reduce_scatter | solution.py:125
  411.3 42.3 %copy-start.30 = (f32[768]{0:T(1024)S(1)}, f32[768]{0:T(1024)}, u32[]{:S(2)}) copy-start(f32[768]{0:T(1024)} %param.32) | copy-start | bytes 9220
  411.3 76.9 %all-gather.21.cloned.1.call-start = ((), (), s32[]{:S(2)}) async-start(), calls=%async_computation.16 | async-start | bytes 2359296 | tf_op jit(solution)/shard_map/all_gather | solution.py:139
  412.0 44.0 %copy-start.22 = (f32[768]{0:T(1024)S(1)}, f32[768]{0:T(1024)}, u32[]{:S(2)}) copy-start(f32[768]{0:T(1024)} %param.33) | copy-start | bytes 9220
  460.8 87.7 %reduce-scatter.13.cloned.1.call-start = ((), (), s32[]{:S(2)}) async-start(), calls=%async_computation.17 | async-start | bytes 4718592 | tf_op jit(solution)/shard_map/reduce_scatter | solution.py:149
  488.2 12.6 copy-start.32
  505.1 77.7 %all-gather.23.cloned.1.call-start = ((), (), s32[]{:S(2)}) async-start(), calls=%async_computation.18 | async-start | bytes 2359296 | tf_op jit(solution)/shard_map/all_gather | solution.py:155
  552.5 30.2 %copy-start.17 = (bf16[384,768]{0,1:T(8,128)(2,1)S(1)}, bf16[384,768]{0,1:T(8,128)(2,1)}, u32[]{:S(2)}) copy-start(bf16[384,768]{0,1:T(8,128)(2,1)} %all_gather.35) | copy-start | bytes 1769476
  555.3 305.8 %all-reduce.5.cloned.1.call-start = ((), (), s32[]{:S(2)}) async-start(), calls=%async_computation.24 | async-start | bytes 9437184
  606.8 3.3 copy-start.1
  606.9 3.3 copy-start.7
  626.4 3.3 copy-start.1
  626.4 3.3 copy-start.7
  645.9 3.2 copy-start.1
  645.9 3.2 copy-start.7
  665.5 3.2 copy-start.1
  665.5 3.2 copy-start.7
  685.0 3.3 copy-start.1
  685.0 3.3 copy-start.7
  704.5 3.3 copy-start.1
  704.5 3.3 copy-start.7
  716.5 3.3 copy-start.15
  716.6 146.9 %reduce-scatter.15.cloned.1.call-start = ((), (), s32[]{:S(2)}) async-start(), calls=%async_computation.19 | async-start | bytes 2359296 | tf_op jit(solution)/shard_map/reduce_scatter | solution.py:228
  723.2 388.2 %reduce-scatter.23.cloned.1.call-start = ((), (), s32[]{:S(2)}) async-start(), calls=%async_computation.23 | async-start | bytes 26738688 | tf_op jit(solution)/shard_map/reduce_scatter | solution.py:236
  737.9 452.4 %reduce-scatter.19.cloned.1.call-start = ((), (), s32[]{:S(2)}) async-start(), calls=%async_computation.21 | async-start | bytes 5013504 | tf_op jit(solution)/shard_map/reduce_scatter | solution.py:234
  745.6 524.2 %reduce-scatter.21.cloned.1.call-start = ((), (), s32[]{:S(2)}) async-start(), calls=%async_computation.22 | async-start | bytes 5013504 | tf_op jit(solution)/shard_map/reduce_scatter | solution.py:235
  753.2 4.6 copy-start.36
  753.2 5.9 copy-start.23
  753.2 5.9 copy-start.25
  753.2 5.9 copy-start.26
  753.2 577.7 %reduce-scatter.17.cloned.1.call-start = ((), (), s32[]{:S(2)}) async-start(), calls=%async_computation.20 | async-start | bytes 1253376 | tf_op jit(solution)/shard_map/reduce_scatter | solution.py:233
  757.8 41.8 %copy-start.27 = (f32[1536]{0:T(1024)S(1)}, f32[1536]{0:T(1024)}, u32[]{:S(2)}) copy-start(f32[1536]{0:T(1024)} %get-tuple-element.382) | copy-start | bytes 18436
  757.8 105.7 %copy-start.4 = (f32[1,512,768]{2,1,0:T(8,128)S(1)}, f32[1,512,768]{2,1,0:T(8,128)}, u32[]{:S(2)}) copy-start(f32[1,512,768]{2,1,0:T(8,128)} %copy-done.3) | copy-start | bytes 4718596
  862.2 249.2 %copy-start.12 = (f32[6,64,1024]{2,1,0:T(8,128)S(1)}, f32[6,64,1024]{2,1,0:T(8,128)}, u32[]{:S(2)}) copy-start(f32[6,64,1024]{2,1,0:T(8,128)} %param.35) | copy-start | bytes 4718596
  (26 other events, 48.8 us)
Sparse Core Ops, SparseCore 0:
  9.6 29.8 all-gather.8
  41.8 40.4 all-gather.10
  85.0 99.6 all-gather.12
  245.3 41.4 reduce-scatter.8
  289.2 42.2 all-gather.16
  333.5 25.9 all-gather.14
  362.1 42.2 all-gather.18
  411.5 42.0 reduce-scatter.10
  460.9 27.2 all-gather.20
  505.2 43.3 reduce-scatter.12
  555.5 27.2 all-gather.22
  716.7 118.0 all-reduce.4
  837.7 25.7 reduce-scatter.14
  867.4 243.9 reduce-scatter.22
  1115.7 74.6 reduce-scatter.18
  1195.2 74.5 reduce-scatter.20
  1273.8 57.0 reduce-scatter.16
where the time goes:
time: 1350 us; the launch traced here: 1340 us
  waiting for transfers between devices  870 us (64%)
  matrix products  185 us (14%)
  blocking collectives  128 us (9%)
  local copies, waits for them, and re-layouts  78.4 us (6%)
  other arithmetic  58 us (4%)
  between operations  16.2 us (1%)
    reduce_scatter x1, waiting for transfers between devices, body(): lax.psum_scatter(mask_grad, 'dp', scatter_dimension=1, tiled=True)  245 us
    all_gather x1, waiting for transfers between devices, body(): lax.all_gather(local_mask, 'dp', axis=1, tiled=True)  88.4 us
    reduce_scatter x1, waiting for transfers between devices, body(): lax.psum_scatter(w_hid_grad, 'dp', scatter_dimension=1, tiled=True)  79.4 us
    reduce_scatter x1, waiting for transfers between devices, body(): lax.psum_scatter(w_in_grad, 'dp', scatter_dimension=0, tiled=True)  75.4 us
    psum x1, blocking collectives, body(): b_qv_total, b_in_total = lax.psum((b_qv_part, b_in_part), 'dp')  61.5 us
    reduce_scatter x1, waiting for transfers between devices, body(): lax.psum_scatter(w_out_grad, 'dp', scatter_dimension=1, tiled=True)  61.2 us
    reduce_scatter x1, waiting for transfers between devices, body(): lax.psum_scatter(hidden_terms, 'tensor', scatter_dimension=1, tiled=True)  43.5 us
    all_gather x1, waiting for transfers between devices, body(): lax.all_gather(w_qkv, 'dp', axis=1, tiled=True)  42.8 us
  transfers between devices with their start and end apart: 17, of which 16 were waited for; matrix products, arithmetic and copies ran while one was open for 6% of the time, Pallas kernels for 0%

commit v1 on v0

--- a/solution.py
+++ b/solution.py
@@ -1,7 +1,804 @@
+import functools
+
 import jax
 import jax.numpy as jnp
 from jax import lax
+from jax.experimental import pallas as pl
+from jax.experimental.pallas import tpu as pltpu
 from jax.sharding import PartitionSpec as P
+
+MESH = pl.DeviceIdType.MESH
+BF, F32 = jnp.bfloat16, jnp.float32
+ANY = pl.BlockSpec(memory_space=pl.ANY)
+VM = pl.BlockSpec(memory_space=pltpu.VMEM)
+
+
+class Place:
+    def __init__(self, deep):
+        self.Z, self.Y, self.C = deep // 4, 2, 2
+        i = lax.axis_index("dp")
+        self.t = lax.axis_index("tensor")
+        self.c = lax.rem(i, 2)
+        self.y = lax.rem(i // 2, 2)
+        self.z = i // 4
+
+    def dev(self, z=None, y=None, c=None, t=None):
+        z = self.z if z is None else z
+        y = self.y if y is None else y
+        c = self.c if c is None else c
+        t = self.t if t is None else t
+        return ((z * self.Y + y) * self.C + c, t)
+
+    def along_z(self, d):
+        return self.dev(z=lax.rem(self.z + d, self.Z))
+
+    def source_z(self, d):
+        return lax.rem(self.z - d + self.Z, self.Z)
+
+    @property
+    def over_y(self):
+        return self.dev(y=1 - self.y)
+
+    @property
+    def over_c(self):
+        return self.dev(c=1 - self.c)
+
+    @property
+    def over_t(self):
+        return self.dev(t=1 - self.t)
+
+    def greet(self):
+        bar = pltpu.get_barrier_semaphore()
+        peers = [self.along_z(d) for d in range(1, self.Z)] + [self.over_y, self.over_c, self.over_t]
+        for p in peers:
+            pl.semaphore_signal(bar, inc=1, device_id=p, device_id_type=MESH)
+        pl.semaphore_wait(bar, len(peers))
+
+
+def rcopy(src, dst, ssem, rsem, dev):
+    return pltpu.make_async_remote_copy(src_ref=src, dst_ref=dst, send_sem=ssem, recv_sem=rsem, device_id=dev, device_id_type=MESH)
+
+
+def dot(a, b):
+    return jnp.dot(a, b, preferred_element_type=F32)
+
+
+def dot_t(a, b):
+    return lax.dot_general(a, b, (((1,), (1,)), ((), ())), preferred_element_type=F32)
+
+
+def dot_0(a, b):
+    return lax.dot_general(a, b, (((0,), (0,)), ((), ())), preferred_element_type=F32)
+
+
+def fwd_kernel(deep, x_sh, mask_sh, qkv_sh, out_sh, in_sh, hid_sh, bin_sh, bias, bqv,
+               attn_o, q_o, k_o, v_o, lse_o, x_o, mask_o, qkv_o, out_o, in_o, hid_o, bin_o,
+               x_v, w_v, m_v, q_v, k_v, v_v, a_v, lse_v,
+               loc, xs, xr, qz_s, qz_r, q1_s, q1_r, mz_s, mz_r, m1_s, m1_r, wz_s, wz_r, w1_s, w1_r, as_, ar):
+    me = Place(deep)
+    Z = me.Z
+    y, c, z, t = me.y, me.c, me.z, me.t
+    half = x_sh.shape[0]
+    seq, width = x_v.shape
+    pairs = q_v.shape[0]
+    heads = 2 * pairs
+    shards = (out_sh, in_sh, hid_sh)
+    wholes = (out_o, in_o, hid_o)
+
+    def cols(k):
+        n = shards[k].shape[1]
+        return pl.ds(pl.multiple_of(t * n, 128), n)
+
+    rows_own = pl.ds(pl.multiple_of(t * half, 128), half)
+    rows_other = pl.ds(pl.multiple_of((1 - t) * half, 128), half)
+
+    locals_ = [
+        pltpu.make_async_copy(qkv_sh, w_v.at[z, y, c], loc.at[0]),
+        pltpu.make_async_copy(x_sh, x_v.at[rows_own], loc.at[1]),
+        pltpu.make_async_copy(mask_sh, m_v.at[:, z, y, c], loc.at[2]),
+        pltpu.make_async_copy(bin_sh, bin_o.at[t], loc.at[3]),
+    ] + [pltpu.make_async_copy(shards[k], wholes[k].at[z, y, c, :, cols(k)], loc.at[4 + k]) for k in range(3)]
+    for cp in locals_:
+        cp.start()
+
+    me.greet()
+
+    def x_copy():
+        return rcopy(x_sh, x_v.at[rows_own], xs.at[0], xr.at[0], me.over_t)
+
+    def b_copy():
+        return rcopy(bin_sh, bin_o.at[t], xs.at[1], xr.at[1], me.over_t)
+
+    def qkv_z(d):
+        return rcopy(qkv_sh, w_v.at[z, y, c], qz_s.at[d - 1], qz_r.at[d - 1], me.along_z(d))
+
+    def qkv_y():
+        return rcopy(w_v.at[:, y, c], w_v.at[:, y, c], q1_s.at[0], q1_r.at[0], me.over_y)
+
+    def qkv_c():
+        return rcopy(w_v.at[:, :, c], w_v.at[:, :, c], q1_s.at[1], q1_r.at[1], me.over_c)
+
+    def mask_z(h, d):
+        return rcopy(mask_sh.at[h], m_v.at[h, z, y, c], mz_s.at[h, d - 1], mz_r.at[h, d - 1], me.along_z(d))
+
+    def mask_y(h):
+        return rcopy(m_v.at[h, :, y, c], m_v.at[h, :, y, c], m1_s.at[h, 0], m1_r.at[h, 0], me.over_y)
+
+    def mask_c(h):
+        return rcopy(m_v.at[h, :, :, c], m_v.at[h, :, :, c], m1_s.at[h, 1], m1_r.at[h, 1], me.over_c)
+
+    def w_z(k, d):
+        return rcopy(shards[k], wholes[k].at[z, y, c, :, cols(k)], wz_s.at[k, d - 1], wz_r.at[k, d - 1], me.along_z(d))
+
+    def w_y(k):
+        part = wholes[k].at[:, y, c, :, cols(k)]
+        return rcopy(part, part, w1_s.at[k, 0], w1_r.at[k, 0], me.over_y)
+
+    def w_x(k):
+        part = wholes[k].at[:, :, c, :, cols(k)]
+        return rcopy(part, part, w1_s.at[k, 1], w1_r.at[k, 1], me.over_t)
+
+    def w_c(k):
+        part = wholes[k].at[:, :, c]
+        return rcopy(part, part, w1_s.at[k, 2], w1_r.at[k, 2], me.over_c)
+
+    def a_copy(p):
+        n = 128
+        at = pl.ds(pl.multiple_of(t * (pairs * n) + p * n, 128), n)
+        return rcopy(a_v.at[p, rows_other], attn_o.at[:, at], as_.at[p], ar.at[p], me.over_t)
+
+    def a_local(p):
+        n = 128
+        at = pl.ds(pl.multiple_of(t * (pairs * n) + p * n, 128), n)
+        return pltpu.make_async_copy(a_v.at[p, rows_own], attn_o.at[:, at], loc.at[7 + p])
+
+    zs = range(1, Z)
+
+    def start_z(make, *k):
+        for d in zs:
+            make(*k, d).start()
+
+    def wait_z(make, *k):
+        for d in zs:
+            make(*k, d).wait_recv()
+
+    x_copy().start()
+    b_copy().start()
+    start_z(qkv_z)
+    start_z(mask_z, 0)
+    start_z(mask_z, 1)
+    start_z(w_z, 2)
+    for cp in locals_:
+        cp.wait()
+    wait_z(qkv_z)
+    qkv_y().start()
+    wait_z(mask_z, 0)
+    mask_y(0).start()
+    qkv_y().wait_recv()
+    qkv_c().start()
+    x_copy().wait_recv()
+    qkv_c().wait_recv()
+
+    step = half // 2
+
+    def project(r, carry):
+        rows = pl.ds(pl.multiple_of(r * step, step), step)
+        xb = x_v[rows, :]
+        for j, dst in enumerate((q_v, k_v, v_v)):
+            w = w_v[:, :, :, j].reshape(width, pairs * 128)
+            acc = dot(xb, w)
+            if j == 0:
+                acc = acc + bqv[0:1, :]
+            elif j == 2:
+                acc = acc + bqv[1:2, :]
+            out = acc.astype(BF)
+            if j == 0:
+                out = out * jnp.asarray(0.125, BF)
+            for p in range(pairs):
+                dst[p, rows, :] = out[:, p * 128:(p + 1) * 128]
+        return carry
+
+    lax.fori_loop(0, seq // step, project, 0)
+    outs = [
+        pltpu.make_async_copy(q_v, q_o, loc.at[0]),
+        pltpu.make_async_copy(k_v, k_o, loc.at[1]),
+        pltpu.make_async_copy(v_v, v_o, loc.at[2]),
+        pltpu.make_async_copy(x_v, x_o, loc.at[3]),
+        pltpu.make_async_copy(w_v, qkv_o, loc.at[4]),
+    ]
+    for cp in outs:
+        cp.start()
+
+    blk = seq // Z
+
+    def attend(p, u):
+        h = 2 * p + u
+        sl = slice(64 * u, 64 * u + 64)
+
+        def rows_of(b, carry):
+            rows = pl.ds(pl.multiple_of(b * blk, blk), blk)
+            s = dot_t(q_v[p, rows, sl], k_v[p, :, sl])
+            s = s + m_v[h, b].reshape(blk, seq).astype(F32) + bias[...]
+            top = jnp.max(s, axis=-1, keepdims=True)
+            e = jnp.exp(s - top)
+            total = jnp.sum(e, axis=-1, keepdims=True)
+            o = dot(e.astype(BF), v_v[p, :, sl])
+            a_v[p, rows, sl] = (o / total).astype(BF)
+            lse_v[p, rows, u:u + 1] = top + jnp.log(total)
+            return carry
+
+        lax.fori_loop(0, Z, rows_of, 0)
+
+    def mask_save(h):
+        return pltpu.make_async_copy(m_v.at[h], mask_o.at[h], loc.at[10 + h])
+
+    order = (2, 1, 0)
+
+    def pair_step(p, carry):
+        a, b = 2 * p, 2 * p + 1
+        wait_z(mask_z, b)
+        mask_y(b).start()
+
+        @pl.when(p < pairs - 1)
+        def _():
+            start_z(mask_z, a + 2)
+
+        mask_y(a).wait_recv()
+        mask_c(a).start()
+        for n, k in enumerate(order):
+            @pl.when(p == n)
+            def _():
+                wait_z(w_z, k)
+                w_y(k).start()
+
+        @pl.when(p < pairs - 1)
+        def _():
+            start_z(mask_z, a + 3)
+
+        mask_c(a).wait_recv()
+        mask_save(a).start()
+        attend(p, 0)
+        mask_y(b).wait_recv()
+        mask_c(b).start()
+        for n, k in enumerate(order[1:]):
+            @pl.when(p == n)
+            def _():
+                start_z(w_z, k)
+
+        @pl.when(p < pairs - 1)
+        def _():
+            wait_z(mask_z, a + 2)
+            mask_y(a + 2).start()
+
+        mask_c(b).wait_recv()
+        mask_save(b).start()
+        attend(p, 1)
+        for n, k in enumerate(order):
+            @pl.when(p == n)
+            def _():
+                w_y(k).wait_recv()
+                w_x(k).start()
+                if n > 0:
+                    w_x(order[n - 1]).wait_recv()
+                    w_c(order[n - 1]).start()
+
+        a_copy(p).start()
+        a_local(p).start()
+        return carry
+
+    lax.fori_loop(0, pairs, pair_step, 0)
+    lse_out = pltpu.make_async_copy(lse_v, lse_o, loc.at[5])
+    lse_out.start()
+    w_x(order[-1]).wait_recv()
+    w_c(order[-1]).start()
+    for cp in outs + [lse_out]:
+        cp.wait()
+    for p in range(pairs):
+        a_local(p).wait()
+        a_copy(p).wait()
+    b_copy().wait()
+    x_copy().wait_send()
+    for d in zs:
+        qkv_z(d).wait_send()
+    qkv_y().wait_send()
+    qkv_c().wait_send()
+    for h in range(heads):
+        for d in zs:
+            mask_z(h, d).wait_send()
+        mask_y(h).wait_send()
+        mask_c(h).wait_send()
+        mask_save(h).wait()
+    for k in range(3):
+        for d in zs:
+            w_z(k, d).wait_send()
+        w_y(k).wait_send()
+        w_x(k).wait_send()
+        w_c(k).wait()
+
+
+def forward(deep, x, mask, qkv, w_out_t, w_in, w_hid_t, b_in, bias, b_qv):
+    half, width = x.shape
+    seq = 2 * half
+    heads, blk, _ = mask.shape
+    pairs = heads // 2
+    Z, Y, C = deep // 4, 2, 2
+    n_out, n_in = w_out_t.shape[1], w_in.shape[1]
+    r = w_in.shape[0]
+    sd = jax.ShapeDtypeStruct
+    dma = pltpu.SemaphoreType.DMA
+    out_shape = (
+        sd((half, 2 * pairs * 128), BF),
+        sd((pairs, seq, 128), BF), sd((pairs, seq, 128), BF), sd((pairs, seq, 128), BF),
+        sd((pairs, seq, 128), F32),
+        sd((seq, width), BF),
+        sd((heads, Z, Y, C, blk, seq), BF),
+        sd((Z, Y, C) + qkv.shape, BF),
+        sd((Z, Y, C, r, 2 * n_out), BF), sd((Z, Y, C, r, 2 * n_in), BF), sd((Z, Y, C, r, 2 * n_in), BF),
+        sd((2,) + b_in.shape, F32),
+    )
+    return pl.pallas_call(
+        functools.partial(fwd_kernel, deep),
+        out_shape=out_shape,
+        in_specs=[ANY] * 7 + [VM, VM],
+        out_specs=[ANY] * len(out_shape),
+        scratch_shapes=[
+            pltpu.VMEM((seq, width), BF),
+            pltpu.VMEM((Z, Y, C) + qkv.shape, BF),
+            pltpu.VMEM((heads, Z, Y, C, blk, seq), BF),
+            pltpu.VMEM((pairs, seq, 128), BF), pltpu.VMEM((pairs, seq, 128), BF), pltpu.VMEM((pairs, seq, 128), BF),
+            pltpu.VMEM((pairs, seq, 128), BF),
+            pltpu.VMEM((pairs, seq, 128), F32),
+            dma((16,)), dma((2,)), dma((2,)),
+            dma((Z - 1,)), dma((Z - 1,)), dma((2,)), dma((2,)),
+            dma((heads, Z - 1)), dma((heads, Z - 1)), dma((heads, 2)), dma((heads, 2)),
+            dma((3, Z - 1)), dma((3, Z - 1)), dma((3, 3)), dma((3, 3)),
+            dma((pairs,)), dma((pairs,)),
+        ],
+        compiler_params=pltpu.CompilerParams(collective_id=1, has_side_effects=True, vmem_limit_bytes=58 << 20),
+        name="forward_attention",
+    )(x, mask, qkv, w_out_t, w_in, w_hid_t, b_in, bias, b_qv)
+
+
+def bwd_kernel(deep, dat, q_h, k_h, v_h, mask_h, lse_h, x_h, qkv_h, hid_h, in_h, out_h, dz1_h, sg_h, small_h, bias,
+               dx_o, gqkv_o, ghid_o, gin_o, gout_o, gmask_o, small_o,
+               q_v, k_v, v_v, do_v, lse_v, m_v, p_v, dq_v, dk_v, dv_v, acck, accv,
+               lc_m, ly_m, lz_m, gm_v,
+               own_w, lc_hid, lx_hid, ly_hid, lz_hid, lc_in, lx_in, ly_in, lz_in, lc_out, lx_out, ly_out, lz_out, fin_hid, fin_in, fin_out,
+               p_q, lc_q, ly_q, lz_q, fin_q,
+               x_v, w_v, sx_v, lx_x, dx_v, dz_v,
+               s_v, sc_v, sy_v, sz_v, sx2_v,
+               loc, msem, ds_, dr, wl, w1s, w1r, wzs, wzr, m1s, m1r, mzs, mzr, q1s, q1r, qzs, qzr, xs, xr, s1s, s1r, szs, szr):
+    me = Place(deep)
+    Z, y, c, z, t = me.Z, me.y, me.c, me.z, me.t
+    pairs, seq, _ = q_v.shape
+    heads = 2 * pairs
+    half = seq // 2
+    width = x_v.shape[1]
+    zs = range(1, Z)
+    rows_own = pl.ds(pl.multiple_of(t * half, 128), half)
+    rows_other = pl.ds(pl.multiple_of((1 - t) * half, 128), half)
+    parts = (hid_h, in_h, out_h)
+    lcs, lxs, lys, lzs, fins = (lc_hid, lc_in, lc_out), (lx_hid, lx_in, lx_out), (ly_hid, ly_in, ly_out), (lz_hid, lz_in, lz_out), (fin_hid, fin_in, fin_out)
+    w_outs = (ghid_o, gin_o, gout_o)
+
+    def cols(k, who):
+        n = lxs[k].shape[-1]
+        return pl.ds(pl.multiple_of(who * n, 128), n)
+
+    def dat_cols(p, who):
+        return pl.ds(pl.multiple_of(who * (pairs * 128) + p * 128, 128), 128)
+
+    def dat_local(p):
+        return pltpu.make_async_copy(dat.at[:, dat_cols(p, t)], do_v.at[p, rows_own], loc.at[p])
+
+    def dat_copy(p):
+        return rcopy(dat.at[:, dat_cols(p, 1 - t)], do_v.at[p, rows_own], ds_.at[p], dr.at[p], me.over_t)
+
+    loads = [pltpu.make_async_copy(a, b, loc.at[3 + n]) for n, (a, b) in enumerate((
+        (q_h, q_v), (k_h, k_v), (v_h, v_v), (lse_h, lse_v), (x_h, x_v), (qkv_h, w_v), (dz1_h, dz_v), (small_h, s_v.at[pl.ds(0, small_h.shape[0])])))]
+
+    def m_load(h, slot):
+        return pltpu.make_async_copy(mask_h.at[h], m_v.at[slot], msem.at[slot])
+
+    def sg_load(h):
+        return pltpu.make_async_copy(sg_h.at[h], gm_v.at[h], loc.at[11 + h])
+
+    def gm_save(h):
+        return pltpu.make_async_copy(gm_v.at[h], gmask_o.at[h], loc.at[17 + h])
+
+    def own_at(k):
+        n = lcs[k].shape[-1]
+        return own_w.at[:, :, :, pl.ds(0, n)]
+
+    def own_load(k):
+        return pltpu.make_async_copy(parts[k].at[:, :, c], own_at(k), wl.at[k])
+
+    def w_c(k):
+        return rcopy(parts[k].at[:, :, 1 - c], lcs[k], w1s.at[k, 0], w1r.at[k, 0], me.over_c)
+
+    def w_x(k):
+        return rcopy(lcs[k].at[:, :, :, cols(k, 1 - t)], lxs[k], w1s.at[k, 1], w1r.at[k, 1], me.over_t)
+
+    def w_y(k):
+        return rcopy(lxs[k].at[:, 1 - y], lys[k], w1s.at[k, 2], w1r.at[k, 2], me.over_y)
+
+    def w_z(k, d):
+        return rcopy(lys[k].at[lax.rem(z + d, Z)], lzs[k].at[d - 1], wzs.at[k, d - 1], wzr.at[k, d - 1], me.along_z(d))
+
+    def m_c(h, slot):
+        return rcopy(p_v.at[slot, :, :, 1 - c], lc_m.at[h], m1s.at[h, 0], m1r.at[h, 0], me.over_c)
+
+    def m_y(h):
+        return rcopy(lc_m.at[h, :, 1 - y], ly_m.at[h], m1s.at[h, 1], m1r.at[h, 1], me.over_y)
+
+    def m_z(h, d):
+        return rcopy(ly_m.at[h, lax.rem(z + d, Z)], lz_m.at[h, d - 1], mzs.at[h, d - 1], mzr.at[h, d - 1], me.along_z(d))
+
+    def q_c():
+        return rcopy(p_q.at[:, :, 1 - c], lc_q, q1s.at[0], q1r.at[0], me.over_c)
+
+    def q_y():
+        return rcopy(lc_q.at[:, 1 - y], ly_q, q1s.at[1], q1r.at[1], me.over_y)
+
+    def q_z(d):
+        return rcopy(ly_q.at[lax.rem(z + d, Z)], lz_q.at[d - 1], qzs.at[d - 1], qzr.at[d - 1], me.along_z(d))
+
+    def x_copy():
+        return rcopy(sx_v, lx_x, xs, xr, me.over_t)
+
+    def s_c():
+        return rcopy(s_v, sc_v, s1s.at[0], s1r.at[0], me.over_c)
+
+    def s_y():
+        return rcopy(sc_v, sy_v, s1s.at[1], s1r.at[1], me.over_y)
+
+    def s_z(d):
+        return rcopy(sy_v, sz_v.at[z], szs.at[d - 1], szr.at[d - 1], me.along_z(d))
+
+    def s_z_in(d):
+        return rcopy(sy_v, sz_v.at[me.source_z(d)], szs.at[d - 1], szr.at[d - 1], me.along_z(d))
+
+    def s_x():
+        return rcopy(s_v, sx2_v, s1s.at[2], s1r.at[2], me.over_t)
+
+    for p in range(pairs):
+        dat_local(p).start()
+    for cp in loads:
+        cp.start()
+    own_load(0).start()
+    m_load(0, 0).start()
+    me.greet()
+    for p in range(pairs):
+        dat_copy(p).start()
+    for k in range(3):
+        w_c(k).start()
+    for h in range(heads):
+        sg_load(h).start()
+
+    def add_own(k):
+        own_load(k).wait()
+        w_c(k).wait_recv()
+        n = lcs[k].shape[-1]
+
+        def one(i, carry):
+            for j in range(me.Y):
+                lcs[k][i, j] = lcs[k][i, j] + own_w[i, j, :, 0:n]
+            return carry
+
+        lax.fori_loop(0, Z, one, 0)
+
+    for k in range(3):
+        add_own(k)
+        if k < 2:
+            own_load(k + 1).start()
+        w_x(k).start()
+    for cp in loads:
+        cp.wait()
+
+    blk = seq // Z
+    shape4 = p_v.shape[2:]
+
+    def attend(p, u, slot):
+        sl = slice(64 * u, 64 * u + 64)
+        acck[...] = jnp.zeros_like(acck)
+        accv[...] = jnp.zeros_like(accv)
+
+        def rows_of(b, carry):
+            rows = pl.ds(pl.multiple_of(b * blk, blk), blk)
+            qb, dob = q_v[p, rows, sl], do_v[p, rows, sl]
+            kk, vv = k_v[p, :, sl], v_v[p, :, sl]
+            s = dot_t(qb, kk) + m_v[u, b].reshape(blk, seq).astype(F32) + bias[...]
+            pr = jnp.exp(s - lse_v[p, rows, u:u + 1])
+            dp = dot_t(dob, vv)
+            tt = pr * dp
+            delta = jnp.sum(tt, axis=-1, keepdims=True)
+            dsb = (tt - pr * delta).astype(BF)
+            p_v[slot, b] = dsb.reshape(shape4)
+            dq_v[p, rows, sl] = (dot(dsb, kk) * 0.125).astype(BF)
+            acck[...] += dot_0(dsb, qb)
+            accv[...] += dot_0(pr.astype(BF), dob)
+            return carry
+
+        lax.fori_loop(0, Z, rows_of, 0)
+        dk_v[p, :, sl] = acck[...].astype(BF)
+        dv_v[p, :, sl] = accv[...].astype(BF)
+
+    def m_add_c(h, slot):
+        m_c(h, slot).wait_recv()
+
+        def one(i, carry):
+            for j in range(me.Y):
+                lc_m[h, i, j] = lc_m[h, i, j] + p_v[slot, i, j, c]
+            return carry
+
+        lax.fori_loop(0, Z, one, 0)
+        m_y(h).start()
+
+    def m_add_y(h):
+        m_y(h).wait_recv()
+
+        def one(i, carry):
+            ly_m[h, i] = ly_m[h, i] + lc_m[h, i, y]
+            return carry
+
+        lax.fori_loop(0, Z, one, 0)
+        for d in zs:
+            m_z(h, d).start()
+
+    def m_end(h):
+        total = ly_m[h, z].astype(F32)
+        for d in zs:
+            m_z(h, d).wait_recv()
+            total = total + lz_m[h, d - 1].astype(F32)
+        sg_load(h).wait()
+        gm_v[h] = total * gm_v[h]
+        gm_save(h).start()
+
+    def head_step(p, u):
+        h = 2 * p + u
+        m_load(h, u).wait()
+        if u == 0:
+            m_load(h + 1, 1).start()
+        else:
+            @pl.when(p < pairs - 1)
+            def _():
+                m_load(h + 1, 0).start()
+
+        @pl.when(p > 0)
+        def _():
+            m_c(h - 2, u).wait_send()
+
+        attend(p, u, u)
+        m_c(h, u).start()
+        if u == 1:
+            m_add_c(h - 1, 0)
+        else:
+            @pl.when(p > 0)
+            def _():
+                m_add_c(h - 1, 1)
+
+        @pl.when(h >= 2)
+        def _():
+            m_add_y(h - 2)
+
+    def pair_step(p, carry):
+        dat_local(p).wait()
+        dat_copy(p).wait_recv()
+        head_step(p, 0)
+        head_step(p, 1)
+        return carry
+
+    lax.fori_loop(0, pairs, pair_step, 0)
+
+    def w_add_x(k):
+        w_x(k).wait_recv()
+
+        def one(i, carry):
+            for j in range(me.Y):
+                lxs[k][i, j] = lxs[k][i, j] + lcs[k][i, j, :, cols(k, t)]
+            return carry
+
+        lax.fori_loop(0, Z, one, 0)
+        w_y(k).start()
+
+    def w_add_y(k):
+        w_y(k).wait_recv()
+
+        def one(i, carry):
+            lys[k][i] = lys[k][i] + lxs[k][i, y]
+            return carry
+
+        lax.fori_loop(0, Z, one, 0)
+        for d in zs:
+            w_z(k, d).start()
+
+    def w_end(k):
+        total = lys[k][z].astype(F32)
+        for d in zs:
+            w_z(k, d).wait_recv()
+            total = total + lzs[k][d - 1].astype(F32)
+        fins[k][...] = total
+        pltpu.make_async_copy(fins[k], w_outs[k], wl.at[3 + k]).start()
+
+    m_add_c(heads - 1, 1)
+    w_add_x(0)
+
+    step = half // 2
+
+    def d_cat(ref, rows):
+        return jnp.concatenate([ref[p, rows, :] for p in range(pairs)], axis=1)
+
+    def weight(j):
+        return w_v[:, :, :, j].reshape(width, pairs * 128)
+
+    def terms(rows):
+        acc = dot_t(d_cat(dq_v, rows), weight(0))
+        acc = acc + dot_t(d_cat(dk_v, rows), weight(1))
+        return acc + dot_t(d_cat(dv_v, rows), weight(2))
+
+    def theirs(r, carry):
+        at = pl.ds(pl.multiple_of(r * step, step), step)
+        rows = pl.ds(pl.multiple_of((1 - t) * half + r * step, step), step)
+        sx_v[at, :] = terms(rows).astype(BF)
+        return carry
+
+    lax.fori_loop(0, 2, theirs, 0)
+    x_copy().start()
+
+    for j, ref in enumerate((dq_v, dk_v, dv_v)):
+        g = dot_0(x_v[...], d_cat(ref, slice(None)))
+        p_q[:, :, :, j] = g.astype(BF).reshape(p_q.shape[:3] + p_q.shape[4:])
+    q_c().start()
+    base = small_h.shape[0]
+    for n, ref in enumerate((dq_v, dv_v)):
+        for p in range(pairs):
+            at = base + n * pairs + p
+            s_v[at:at + 1, :] = jnp.sum(ref[p].astype(F32), axis=0, keepdims=True)
+    for at in range(base + 2 * pairs, s_v.shape[0]):
+        s_v[at:at + 1, :] = jnp.zeros((1, 128), F32)
+    s_c().start()
+
+    def mine(r, carry):
+        at = pl.ds(pl.multiple_of(r * step, step), step)
+        rows = pl.ds(pl.multiple_of(t * half + r * step, step), step)
+        dx_v[at, :] = terms(rows) + dz_v[at, :]
+        return carry
+
+    lax.fori_loop(0, 2, mine, 0)
+    q_c().wait_recv()
+    for i in range(Z):
+        lc_q[i] = lc_q[i] + p_q[i, :, c]
+    q_y().start()
+    s_c().wait_recv()
+    sc_v[...] = sc_v[...] + s_v[...]
+    s_y().start()
+    m_add_y(heads - 2)
+    w_add_x(1)
+    m_end(0)
+    m_end(1)
+    w_add_x(2)
+    m_end(2)
+    m_add_y(heads - 1)
+    m_end(3)
+    w_add_y(0)
+    m_end(4)
+    q_y().wait_recv()
+    for i in range(Z):
+        ly_q[i] = ly_q[i] + lc_q[i, y]
+    for d in zs:
+        q_z(d).start()
+    s_y().wait_recv()
+    sy_v[...] = sy_v[...] + sc_v[...]
+    sz_v[z] = sy_v[...]
+    for d in zs:
+        s_z(d).start()
+    m_end(5)
+    w_add_y(1)
+    w_end(0)
+    w_add_y(2)
+    x_copy().wait_recv()
+    dx_v[...] = dx_v[...] + lx_x[...].astype(F32)
+    dx_save = pltpu.make_async_copy(dx_v, dx_o, loc.at[23])
+    dx_save.start()
+    total = ly_q[z].astype(F32)
+    for d in zs:
+        q_z(d).wait_recv()
+        total = total + lz_q[d - 1].astype(F32)
+    fin_q[...] = total
+    q_save = pltpu.make_async_copy(fin_q, gqkv_o, loc.at[24])
+    q_save.start()
+    for d in zs:
+        s_z_in(d).wait_recv()
+    s_c().wait_send()
+    total = sz_v[0]
+    for i in range(1, Z):
+        total = total + sz_v[i]
+    s_v[...] = total
+    s_x().start()
+    w_end(1)
+    w_end(2)
+    s_x().wait_recv()
+    low = sx2_v[...] + s_v[...]
+    row = lax.broadcasted_iota(jnp.int32, low.shape, 0)
+    sy_done = s_y()
+    sy_done.wait_send()
+    sc_v[...] = jnp.where(row < base, low, s_v[...])
+    s_save = pltpu.make_async_copy(sc_v, small_o, loc.at[25])
+    s_save.start()
+
+    for p in range(pairs):
+        dat_copy(p).wait_send()
+    for k in range(3):
+        w_c(k).wait_send()
+        w_x(k).wait_send()
+        w_y(k).wait_send()
+        for d in zs:
+            w_z(k, d).wait_send()
+        pltpu.make_async_copy(fins[k], w_outs[k], wl.at[3 + k]).wait()
+    for h in range(heads):
+        if h >= heads - 2:
+            m_c(h, h % 2).wait_send()
+        m_y(h).wait_send()
+        for d in zs:
+            m_z(h, d).wait_send()
+        gm_save(h).wait()
+    q_c().wait_send()
+    q_y().wait_send()
+    for d in zs:
+        q_z(d).wait_send()
+        s_z(d).wait_send()
+    x_copy().wait_send()
+    s_x().wait_send()
+    dx_save.wait()
+    q_save.wait()
+    s_save.wait()
+
+
+def backward(deep, dat, q, k, v, mask, lse, x, qkv, g_hid, g_in, g_out, dz1, sg, small, bias):
+    pairs, seq, _ = q.shape
+    half, width = dz1.shape
+    heads, Z, Y, C, blk, _ = mask.shape
+    r, n2 = g_in.shape[3], g_in.shape[4]
+    n2o = g_out.shape[4]
+    n, no = n2 // 2, n2o // 2
+    base = small.shape[0]
+    rows_s = base + 8
+    sd = jax.ShapeDtypeStruct
+    dma = pltpu.SemaphoreType.DMA
+    vm = pltpu.VMEM
+    out_shape = (
+        sd((half, width), F32), sd(qkv.shape[3:], F32), sd((r, n), F32), sd((r, n), F32), sd((r, no), F32),
+        sd((heads, blk, seq), F32), sd((rows_s, 128), F32),
+    )
+    pair = vm((pairs, seq, 128), BF)
+
+    def chain(m):
+        return [vm((Z, Y, r, 2 * m), BF), vm((Z, Y, r, m), BF), vm((Z, r, m), BF), vm((Z - 1, r, m), BF)]
+
+    three, rq, nq = qkv.shape[3:]
+    return pl.pallas_call(
+        functools.partial(bwd_kernel, deep),
+        out_shape=out_shape,
+        in_specs=[ANY] * 14 + [VM],
+        out_specs=[ANY] * len(out_shape),
+        scratch_shapes=[
+            pair, pair, pair, pair, vm((pairs, seq, 128), F32), vm((2, Z, Y, C, blk, seq), BF), vm((2, Z, Y, C, blk, seq), BF),
+            pair, pair, pair, vm((seq, 64), F32), vm((seq, 64), F32),
+            vm((heads, Z, Y, blk, seq), BF), vm((heads, Z, blk, seq), BF), vm((heads, Z - 1, blk, seq), BF), vm((heads, blk, seq), F32),
+            vm((Z, Y, r, n2), BF), *chain(n), *chain(n), *chain(no), vm((r, n), F32), vm((r, n), F32), vm((r, no), F32),
+            vm((Z, Y, C, three, rq, nq), BF), vm((Z, Y, three, rq, nq), BF), vm((Z, three, rq, nq), BF), vm((Z - 1, three, rq, nq), BF), vm((three, rq, nq), F32),
+            vm((seq, width), BF), vm((Z, Y, C, three, rq, nq), BF), vm((half, width), BF), vm((half, width), BF), vm((half, width), F32), vm((half, width), F32),
+            vm((rows_s, 128), F32), vm((rows_s, 128), F32), vm((rows_s, 128), F32), vm((Z, rows_s, 128), F32), vm((rows_s, 128), F32),
+            dma((26,)), dma((2,)), dma((pairs,)), dma((pairs,)),
+            dma((6,)), dma((3, 3)), dma((3, 3)), dma((3, Z - 1)), dma((3, Z - 1)),
+            dma((heads, 2)), dma((heads, 2)), dma((heads, Z - 1)), dma((heads, Z - 1)),
+            dma((2,)), dma((2,)), dma((Z - 1,)), dma((Z - 1,)), dma, dma,
+            dma((3,)), dma((3,)), dma((Z - 1,)), dma((Z - 1,)),
+        ],
+        compiler_params=pltpu.CompilerParams(collective_id=2, has_side_effects=True, vmem_limit_bytes=62 << 20),
+        name="backward_attention",
+    )(dat, q, k, v, mask, lse, x, qkv, g_hid, g_in, g_out, dz1, sg, small, bias)
+
 
 NEG = -1e30
 EPS = 1e-12
@@ -33,7 +830,7 @@
     )
 
 
-def body(
+def plain_body(
     inputs,
     lengths,
     w_qkv,
@@ -262,6 +1059,80 @@
     )
 
 
+def norm_stats(rows):
+    centre = rows - jnp.mean(rows, axis=-1, keepdims=True)
+    scale = lax.rsqrt(jnp.mean(centre * centre, axis=-1, keepdims=True) + EPS)
+    return centre * scale, scale
+
+
+def norm_back(e, hat, scale):
+    return (e - jnp.mean(e, axis=-1, keepdims=True) - hat * jnp.mean(e * hat, axis=-1, keepdims=True)) * scale
+
+
+def body(
+    inputs, lengths, w_qkv, b_qv, w_out, b_out, ln1_gain, ln1_bias, w_in, b_in, w_hid, b_hid,
+    ln2_gain, ln2_bias, mask_logits, noise, cotangent,
+):
+    deep = lax.axis_size("dp")
+    x = inputs[0]
+    half, width = x.shape
+    seq = 2 * half
+    t = lax.axis_index("tensor")
+    length = lengths[0]
+    mixed = mask_logits + noise
+    mask = jax.nn.log_sigmoid(mixed).astype(BF)
+    gate = jax.nn.sigmoid(-mixed)
+    bias = jnp.where(jnp.arange(seq, dtype=jnp.int32) < length, 0.0, NEG).astype(F32)[None]
+    attn, q, k, v, lse, x_all, mask_all, qkv_all, out_all, in_all, hid_all, bin_all = forward(
+        deep, x, mask, w_qkv, w_out.T, w_in, w_hid.T, b_in[None], bias, b_qv)
+    w_out_t = out_all.reshape(width, -1)
+    w_in_all = in_all.reshape(width, -1)
+    w_hid_t = hid_all.reshape(width, -1)
+
+    z1 = x.astype(F32) + dot_t(attn, w_out_t) + b_out
+    hat1, scale1 = norm_stats(z1)
+    h1 = hat1 * ln1_gain + ln1_bias
+    h1b = h1.astype(BF)
+    pre = dot(h1b, w_in_all) + bin_all.reshape(-1)
+    act = gelu_exact(pre).astype(BF)
+    z2 = h1 + dot_t(act, w_hid_t) + b_hid
+    hat2, scale2 = norm_stats(z2)
+    outputs = (hat2 * ln2_gain + ln2_bias).astype(BF)
+
+    rows = t * half + jnp.arange(half, dtype=jnp.int32)
+    dy = cotangent[0] * (rows < length).astype(F32)[:, None]
+    dz2 = norm_back(dy * ln2_gain, hat2, scale2)
+    dz2b = dz2.astype(BF)
+    g_hid = dot_0(dz2b, act).astype(BF)
+    _, pull = jax.vjp(gelu_exact, pre)
+    dpre = pull(dot(dz2b, w_hid_t))[0].astype(BF)
+    g_in = dot_0(h1b, dpre).astype(BF)
+    dh1 = dz2 + dot_t(dpre, w_in_all)
+    dz1 = norm_back(dh1 * ln1_gain, hat1, scale1)
+    dz1b = dz1.astype(BF)
+    g_out = dot_0(dz1b, attn).astype(BF)
+    dattn = dot(dz1b, w_out_t).astype(BF)
+
+    sums = [
+        jnp.sum(dh1 * hat1, axis=0), jnp.sum(dh1, axis=0), jnp.sum(dy * hat2, axis=0), jnp.sum(dy, axis=0),
+        jnp.sum(dz1, axis=0), jnp.sum(dz2, axis=0), jnp.sum(dpre.astype(F32), axis=0),
+    ]
+    flat = jnp.concatenate(sums).reshape(-1, 128)
+    filled = flat.shape[0]
+    small = jnp.pad(flat, ((0, -filled % 8), (0, 0)))
+
+    dx, gqkv, ghid, gin, gout, gmask, total = backward(
+        deep, dattn, q, k, v, mask_all, lse, x_all, qkv_all,
+        g_hid.reshape(hid_all.shape), g_in.reshape(in_all.shape), g_out.reshape(out_all.shape), dz1, gate, small, bias)
+    vec = total[:6 * width // 128].reshape(6, width)
+    g_bin = lax.dynamic_slice_in_dim(total[6 * width // 128:filled].reshape(-1), t * b_in.shape[0], b_in.shape[0])
+    g_bqv = total[small.shape[0]:small.shape[0] + 2 * b_qv.shape[1] // 128].reshape(b_qv.shape)
+    return (
+        outputs[None], dx[None], gqkv, g_bqv, gout.T, vec[4], vec[0], vec[1], gin, g_bin, ghid.T, vec[5],
+        vec[2], vec[3], gmask,
+    )
+
+
 def solution(mesh):
     placed = (
         P("dp", "tensor", None),
@@ -282,8 +1153,14 @@
         P("tensor", "dp", None),
         P("dp", "tensor", None),
     )
+
+    def run(*args):
+        w_rows, m_rows = args[8].shape[0], args[14].shape[1]
+        tiled = w_rows % 16 == 0 and m_rows % 16 == 0 and args[0].shape[0] == 1
+        return (body if tiled else plain_body)(*args)
+
     return jax.shard_map(
-        body,
+        run,
         mesh=mesh,
         in_specs=placed,
         out_specs=(

time: 1350 us -> 377 us (0.28)
  waiting for transfers between devices: 870 us -> 0 us
  Pallas kernels: 0 us -> 304 us
  matrix products: 185 us -> 48.9 us
  blocking collectives: 128 us -> 0 us
  local copies, waits for them, and re-layouts: 78.4 us -> 11.8 us
  other arithmetic: 58 us -> 10.2 us
  between operations: 16.2 us -> 1.72 us
    reduce_scatter x8 -> x0, waiting for transfers between devices: 588 us -> none  [the longest x1 245 us: body(): lax.psum_scatter(mask_grad, 'dp', scatter_dimension=1, tiled=True)]
    pallas_call x0 -> x2, Pallas kernels: none -> 304 us  [the longest x1 159 us: backward(): pl.pallas_call(functools.partial(bwd_kernel, deep), out_shape=out_shape,...]
    all_gather x8 -> x0, waiting for transfers between devices: 279 us -> none  [the longest x1 88.4 us: body(): lax.all_gather(local_mask, 'dp', axis=1, tiled=True)]
    dot_general x60 -> x9, matrix products: 185 us -> 48.9 us  [the longest x3 29.3 us: dot(): return jnp.dot(a, b, preferred_element_type=F32)]
    psum x2 -> x0, blocking collectives: 102 us -> none  [the longest x1 61.5 us: body(): b_qv_total, b_in_total = lax.psum((b_qv_part, b_in_part), 'dp')]
    dynamic_update_slice x18 -> x0, local copies, waits for them, and re-layouts: 35.1 us -> none  [the longest x12 34.6 us: sequence_back(): lax.map(head_back, (query_s, keys_s, values_s, back_mask, grad_s, total_s))]
    all_gather x1 -> x0, blocking collectives: 26.2 us -> none  [body(): lax.all_gather(w_out, 'dp', axis=1, tiled=True)]
    convert_element_type x10 -> x1, other arithmetic: 26.1 us -> 0.01 us  [body(): dy = cotangent[0] * (rows < length).astype(F32)[:, None]]
  transfers between devices with their start and end apart: 17 -> 0, of which waited for: 16 -> 0; matrix products, arithmetic and copies ran while one was open for 6% -> 0% of each run, Pallas kernels for 0% -> 0%
where the time goes in v1:
time: 377 us
  Pallas kernels  304 us (81%)
  matrix products  48.9 us (13%)
  local copies, waits for them, and re-layouts  11.8 us (3%)
  other arithmetic  10.2 us (3%)
    pallas_call x1, Pallas kernels, backward(): pl.pallas_call(functools.partial(bwd_kernel, deep), out_shape=out_shape,...  159 us
    pallas_call x1, Pallas kernels, forward(): pl.pallas_call(functools.partial(fwd_kernel, deep), out_shape=out_shape,...  145 us
    dot_general x3, matrix products, dot(): return jnp.dot(a, b, preferred_element_type=F32)  29.3 us
    dot_general x3, matrix products, dot_0(): lax.dot_general(a, b, (((0,), (0,)), ((), ())), preferred_element_type=F32)  11.1 us
    dot_general x3, matrix products, dot_t(): lax.dot_general(a, b, (((1,), (1,)), ((), ())), preferred_element_type=F32)  8.51 us

profile of v1, /device:TPU:0, one launch (start us, length us, event | category | flops | bytes accessed | tf_op | source)
XLA Modules:
  0.0 377.1 jit_solution(15057382443129513047)
XLA Ops:
  1.3 0.6 compare_select_fusion.1.bias
  1.9 4.5 %add_divide_fusion = (f32[6,64,1024]{2,1,0:T(8,128)}, bf16[6,64,1024]{2,1,0:T(8,128)(2,1)}) fusion(f32[6,64,1024]{2,1,0:T(8,128)} %param.31, f32[6,64,1024]{2,1,0:T(8,128)} %param.32), kind=kLoop, calls=%fused_computation.26 | loop fusion | flops 4718592 | bytes 5505024 | tf_op jit(solution)/shard_map/div | solution.py:1084
  6.4 0.6 broadcast_in_dim.14.bin_sh
  7.0 145.0 %forward_attention.1 = (bf16[512,768]{1,0:T(8,128)(2,1)}, bf16[3,1024,128]{2,1,0:T(8,128)(2,1)}, bf16[3,1024,128]{2,1,0:T(8,128)(2,1)}, bf16[3,1024,128]{2,1,0:T...) custom-call(bf16[512,768]{1,0:T(8,128)(2,1)} %bitcast.65, ...), custom_call_target="tpu_custom_call" | custom-call | tf_op jit(solution)/shard_map/forward_attention/pallas_call | solution.py:339
  152.0 0.0 copy-start.13
  152.1 0.0 slice-start.2
  152.1 2.6 fusion.27
  154.7 0.3 multiply_reduce_fusion.5
  155.0 0.0 copy-done.21
  155.0 0.0 copy-done.13
  155.0 0.0 copy-done.15
  155.0 0.0 slice-start.3
  155.0 0.0 copy-start.20
  155.0 19.3 %multiply_convert_fusion = (bf16[512,3072]{1,0:T(8,128)(2,1)S(1)}, f32[512,3072]{1,0:T(8,128)}, f32[512,3072]{1,0:T(8,128)}) fusion(f32[3072]{0:T(1024)} %bitcast.81, bf16[768,3072]{1,0:T(8,128)(2,1)S(1)} %bitcast.71, f32[512,768]{1,0:T(8,128)S(1)} %get-tuple-element.78, f32[768]{0:T(1024)S(1)} %copy-done.21, f32[768]{0:T(1024)S(1)} %copy-done.13, ...), kind=kOutput, calls=%fused_computation.4 | convolution fusion | flops 2521694208 | bytes 22042624 | tf_op jit(solution)/shard_map/dot_general | solution.py:63
  174.3 0.0 copy-done.20
  174.3 0.0 copy-start.11
  174.3 2.8 fusion.28
  177.2 0.3 multiply_reduce_fusion.4
  177.5 0.0 copy-start.14
  177.5 0.0 copy-start.1
  177.5 0.0 copy-done.11
  177.6 0.0 copy-start.16
  177.6 0.0 copy-start.18
  177.6 2.4 multiply_reduce_fusion
  180.0 0.0 slice-start
  180.0 1.6 fusion.24
  181.6 8.4 %convert_reduce_fusion = (f32[3072]{0:T(1024)S(1)}, bf16[512,3072]{1,0:T(8,128)(2,1)S(1)}) fusion(f32[512,3072]{1,0:T(8,128)} %get-tuple-element.66, bf16[768,3072]{1,0:T(8,128)(2,1)S(1)} %bitcast.78, f32[512,768]{1,0:T(8,128)S(1)} %get-tuple-element.62, f32[512,3072]{1,0:T(8,128)} %get-tuple-element.79, f32[3072]{0:T(1024)S(1)} %bitcast.82), kind=kOutput, calls=%fused_computation.2 | convolution fusion | flops 2443047936 | bytes 22044672 | tf_op jit(solution)/shard_map/dot_general | solution.py:63
  190.0 3.1 multiply_reduce_fusion.1
  193.2 0.0 copy-done.24
  193.3 0.5 fusion.25
  193.8 0.0 copy-start
  193.8 0.7 pad.4.small_h
  194.5 1.9 convolution_convert_fusion.2
  196.4 0.3 copy-done.25
  196.7 4.8 %convolution_convert_fusion = bf16[768,3072]{1,0:T(8,128)(2,1)} fusion(bf16[512,3072]{1,0:T(8,128)(2,1)S(1)} %copy-done.25, f32[512,768]{1,0:T(8,128)S(1)} %get-tuple-element.78, f32[768]{0:T(1024)S(1)} %copy-done.21, f32[768]{0:T(1024)S(1)} %copy-done.13, f32[512]{0:T(512)S(1)} %add_rsqrt_fusion.1, f32[512]{0:T(512)S(1)} %broadcast_multiply_fusion.5), kind=kOutput, calls=%fused_computation.18 | convolution fusion | flops 2420244480 | bytes 9447424 | tf_op jit(solution)/shard_map/dot_general | solution.py:71
  201.5 4.4 %convolution_convert_fusion.1 = bf16[768,3072]{1,0:T(8,128)(2,1)} fusion(bf16[512,3072]{1,0:T(8,128)(2,1)S(1)} %copy-done.23, f32[512,768]{1,0:T(8,128)S(1)} %copy-done.4), kind=kOutput, calls=%fused_computation.19 | convolution fusion | flops 2418671616 | bytes 9437184 | tf_op jit(solution)/shard_map/dot_general | solution.py:71
  205.9 1.7 convolution_convert_fusion.3.dat
  207.6 159.3 %backward_attention.1 = (f32[512,768]{1,0:T(8,128)}, f32[3,48,384]{2,1,0:T(8,128)}, f32[48,1536]{1,0:T(8,128)}, f32[48,1536]{1,0:T(8,128)}, f32[48,384]{1,0:T(8,...) custom-call(bf16[512,768]{1,0:T(8,128)(2,1)} %convolution_convert_fusion.3.dat, ...), custom_call_target="tpu_custom_call" | custom-call | tf_op jit(solution)/shard_map/backward_attention/pallas_call | solution.py:779
  367.0 1.4 slice_bitcast_fusion.1
  368.4 0.6 reshape.140
  369.0 0.7 slice_bitcast_fusion
  369.7 0.7 dynamic_slice.3
  370.4 2.8 copy.46
  373.2 0.7 copy.47
  373.9 0.6 copy.48
  374.5 0.7 copy.49
  375.2 0.7 copy.50
  375.9 1.1 copy.51
  (60 shorter events, 0.2 us)
Async XLA Ops:
  1.9 4.5 %copy-start.12 = (f32[1536]{0:T(1024)S(1)}, f32[1536]{0:T(1024)}, u32[]{:S(2)}) copy-start(f32[1536]{0:T(1024)} %param.26) | copy-start | bytes 18436
  6.4 145.6 %copy-start.5 = (bf16[1,512,768]{2,1,0:T(8,128)(2,1)S(1)}, bf16[1,512,768]{2,1,0:T(8,128)(2,1)}, u32[]{:S(2)}) copy-start(bf16[1,512,768]{2,1,0:T(8,128)(2,1)} %param.17) | copy-start | bytes 2359300
  6.4 145.7 %copy-start.19 = (f32[768]{0:T(1024)S(1)}, f32[768]{0:T(1024)}, u32[]{:S(2)}) copy-start(f32[768]{0:T(1024)} %param.22) | copy-start | bytes 9220
  7.0 148.0 %copy-start.21 = (f32[768]{0:T(1024)S(1)}, f32[768]{0:T(1024)}, u32[]{:S(2)}) copy-start(f32[768]{0:T(1024)} %param.24) | copy-start | bytes 9220
  152.0 2.9 copy-start.13
  152.1 2.9 copy-start.15
  152.1 22.2 %slice-start.2 = ((s8[4718592]{0:T(1024)(128)(4,1)}), s8[4194304]{0:T(1024)(128)(4,1)S(1)}, s32[]{:S(2)}) async-start(s8[4718592]{0:T(1024)(128)(4,1)} %bitcast.75), calls=%async_computation.2 | async-start | bytes 8388608
  155.0 19.3 %slice-start.3 = ((s8[4718592]{0:T(1024)(128)(4,1)}), s8[524288]{0:T(1024)(128)(4,1)S(1)}, s32[]{:S(2)}) async-start(s8[4718592]{0:T(1024)(128)(4,1)} %bitcast.75), calls=%async_computation.3 | async-start | bytes 1048576
  155.0 19.3 %copy-start.20 = (f32[768]{0:T(1024)S(1)}, f32[768]{0:T(1024)}, u32[]{:S(2)}) copy-start(f32[768]{0:T(1024)} %param.28) | copy-start | bytes 9220
  174.3 2.9 copy-start.22
  174.3 3.2 copy-start.11
  177.5 2.5 copy-start.14
  177.5 2.5 copy-start.1
  177.6 4.1 %copy-start.16 = (bf16[4,2,2,48,3072]{4,3,2,1,0:T(8,128)(2,1)S(1)}, bf16[4,2,2,48,3072]{4,3,2,1,0:T(8,128)(2,1)}, u32[]{:S(2)}) copy-start(bf16[4,2,2,48,3072]{4,3,2,1,0:T(8,128)(2,1)} %get-tuple-element.38) | copy-start | bytes 14155780
  177.6 4.0 %copy-start.18 = (f32[2,1,1536]{2,1,0:T(1,128)S(1)}, f32[2,1,1536]{2,1,0:T(1,128)}, u32[]{:S(2)}) copy-start(f32[2,1,1536]{2,1,0:T(1,128)} %get-tuple-element.37) | copy-start | bytes 36868
  180.0 10.0 %slice-start = ((s8[4718592]{0:T(1024)(128)(4,1)}), s8[4194304]{0:T(1024)(128)(4,1)S(1)}, s32[]{:S(2)}) async-start(s8[4718592]{0:T(1024)(128)(4,1)} %bitcast.72), calls=%async_computation | async-start | bytes 8388608
  181.6 8.4 %copy-start.3 = (f32[512,768]{1,0:T(8,128)}, f32[512,768]{1,0:T(8,128)S(1)}, u32[]{:S(2)}) copy-start(f32[512,768]{1,0:T(8,128)S(1)} %get-tuple-element.62) | copy-start | bytes 4718596
  181.6 8.4 %slice-start.1 = ((s8[4718592]{0:T(1024)(128)(4,1)}), s8[524288]{0:T(1024)(128)(4,1)S(1)}, s32[]{:S(2)}) async-start(s8[4718592]{0:T(1024)(128)(4,1)} %bitcast.72), calls=%async_computation.1 | async-start | bytes 1048576
  190.0 3.2 copy-start.24
  193.2 1.3 copy-start.6
  193.8 12.2 %copy-start = (f32[512,768]{1,0:T(8,128)}, f32[512,768]{1,0:T(8,128)S(1)}, u32[]{:S(2)}) copy-start(f32[512,768]{1,0:T(8,128)S(1)} %get-tuple-element.64.dz1_h) | copy-start | bytes 4718596
  194.5 2.2 copy-start.25
  196.7 4.8 %copy-start.4 = (f32[512,768]{1,0:T(8,128)S(1)}, f32[512,768]{1,0:T(8,128)}, u32[]{:S(2)}) copy-start(f32[512,768]{1,0:T(8,128)} %copy-done.3) | copy-start | bytes 4718596
  196.7 4.8 %copy-start.23 = (bf16[512,3072]{1,0:T(8,128)(2,1)S(1)}, bf16[512,3072]{1,0:T(8,128)(2,1)}, u32[]{:S(2)}) copy-start(bf16[512,3072]{1,0:T(8,128)(2,1)} %copy-done.22) | copy-start | bytes 9437188
  201.5 4.4 %copy-start.17 = (bf16[4,2,2,48,768]{4,3,2,1,0:T(8,128)(2,1)S(1)}, bf16[4,2,2,48,768]{4,3,2,1,0:T(8,128)(2,1)}, u32[]{:S(2)}) copy-start(bf16[4,2,2,48,768]{4,3,2,1,0:T(8,128)(2,1)} %get-tuple-element.35) | copy-start | bytes 3538948
  367.0 6.2 %copy-start.9 = (f32[3,48,384]{2,1,0:T(8,128)S(1)}, f32[3,48,384]{2,1,0:T(8,128)}, u32[]{:S(2)}) copy-start(f32[3,48,384]{2,1,0:T(8,128)} %get-tuple-element.104) | copy-start | bytes 663556
  370.4 3.5 copy-start.10
  370.4 4.1 %copy-start.8 = (f32[48,1536]{1,0:T(8,128)S(1)}, f32[48,1536]{1,0:T(8,128)}, u32[]{:S(2)}) copy-start(f32[48,1536]{1,0:T(8,128)} %get-tuple-element.110) | copy-start | bytes 884740
  370.4 4.9 %copy-start.7 = (f32[48,1536]{1,0:T(8,128)S(1)}, f32[48,1536]{1,0:T(8,128)}, u32[]{:S(2)}) copy-start(f32[48,1536]{1,0:T(8,128)} %get-tuple-element.51) | copy-start | bytes 884740
  370.4 5.6 %copy-start.2 = (f32[6,64,1024]{2,1,0:T(8,128)S(1)}, f32[6,64,1024]{2,1,0:T(8,128)}, u32[]{:S(2)}) copy-start(f32[6,64,1024]{2,1,0:T(8,128)} %get-tuple-element.116) | copy-start | bytes 4718596

commit v2 on v1

--- a/solution.py
+++ b/solution.py
@@ -21,6 +21,11 @@
         self.c = lax.rem(i, 2)
         self.y = lax.rem(i // 2, 2)
         self.z = i // 4
+        far = self.z // 2
+        self.outer = 1 - lax.rem(self.z + far, 2)
+        self.z_near = self.z + 1 - 2 * lax.rem(self.z, 2)
+        self.z_far_inner = 2 - far
+        self.z_far_outer = 3 - 3 * far
 
     def dev(self, z=None, y=None, c=None, t=None):
         z = self.z if z is None else z
@@ -71,10 +76,87 @@
     return lax.dot_general(a, b, (((0,), (0,)), ((), ())), preferred_element_type=F32)
 
 
+class Pass:
+    def __init__(self, me, own, view, pair, sems, early=False, wide=False):
+        self.me, self.own, self.view, self.pair, self.early, self.wide = me, own, view, pair, early, wide
+        self.zs, self.zr, self.fs, self.ys, self.yr, self.xs, self.xr, self.cs, self.cr = sems
+
+    def held(self, z):
+        me = self.me
+        return self.view(z, slice(None) if self.early else me.y, me.t)
+
+    def source(self):
+        return self.held(self.me.z) if self.early else self.own
+
+    def near(self):
+        me = self.me
+        return rcopy(self.source(), self.held(me.z), self.zs.at[0], self.zr.at[0], me.dev(z=me.z_near))
+
+    def far(self):
+        me = self.me
+        return rcopy(self.source(), self.held(me.z), self.zs.at[1], self.zr.at[1 + me.outer], me.dev(z=me.z_far_inner))
+
+    def onward(self, n):
+        me = self.me
+        place = self.held(me.z_far_inner if n == 0 else me.z_far_outer)
+        return rcopy(place, place, self.fs.at[n], self.zr.at[1 + n], me.dev(z=me.z_near))
+
+    def z_start(self):
+        self.near().start()
+        self.far().start()
+
+    def relay(self):
+        @pl.when(self.me.outer == 0)
+        def _():
+            for n in range(2):
+                self.onward(n).wait_recv()
+                self.onward(n).start()
+
+    def z_wait(self):
+        @pl.when(self.me.outer == 1)
+        def _():
+            for n in range(2):
+                self.onward(n).wait_recv()
+
+        self.near().wait_recv()
+
+    def y_copy(self):
+        me = self.me
+        place = self.view(me.z if self.early else slice(None), me.y, me.t)
+        return rcopy(self.own if self.early else place, place, self.ys, self.yr, me.over_y)
+
+    def x_copy(self):
+        me = self.me
+        place = self.view(slice(None), slice(None), me.t)
+        return rcopy(place, place, self.xs, self.xr, me.over_t)
+
+    def c_copy(self):
+        return rcopy(self.pair(), self.pair(), self.cs, self.cr, self.me.over_c)
+
+    def finish(self):
+        self.near().wait_send()
+        self.far().wait_send()
+
+        @pl.when(self.me.outer == 0)
+        def _():
+            for n in range(2):
+                self.onward(n).wait_send()
+
+        self.y_copy().wait_send()
+        if self.wide:
+            self.x_copy().wait_send()
+        self.c_copy().wait_send()
+
+
+def pass_sems(*lead):
+    dma = pltpu.SemaphoreType.DMA
+    return [dma(lead + (2,)), dma(lead + (3,)), dma(lead + (2,))] + [dma(lead or (1,))] * 6
+
+
 def fwd_kernel(deep, x_sh, mask_sh, qkv_sh, out_sh, in_sh, hid_sh, bin_sh, bias, bqv,
                attn_o, q_o, k_o, v_o, lse_o, x_o, mask_o, qkv_o, out_o, in_o, hid_o, bin_o,
                x_v, w_v, m_v, q_v, k_v, v_v, a_v, lse_v,
-               loc, xs, xr, qz_s, qz_r, q1_s, q1_r, mz_s, mz_r, m1_s, m1_r, wz_s, wz_r, w1_s, w1_r, as_, ar):
+               loc, xs, xr, as_, ar, *sems):
     me = Place(deep)
     Z = me.Z
     y, c, z, t = me.y, me.c, me.z, me.t
@@ -82,25 +164,39 @@
     seq, width = x_v.shape
     pairs = q_v.shape[0]
     heads = 2 * pairs
-    shards = (out_sh, in_sh, hid_sh)
-    wholes = (out_o, in_o, hid_o)
-
-    def cols(k):
-        n = shards[k].shape[1]
+    q_sems, m_sems, w_sems = sems[0:9], sems[9:18], sems[18:27]
+
+    def cols(n):
         return pl.ds(pl.multiple_of(t * n, 128), n)
 
     rows_own = pl.ds(pl.multiple_of(t * half, 128), half)
     rows_other = pl.ds(pl.multiple_of((1 - t) * half, 128), half)
+
+    P_Q = Pass(me, qkv_sh, lambda zs, ys, ts: w_v.at[zs, ys, c], lambda: w_v.at[:, :, c],
+               list(q_sems[:3]) + [s.at[0] for s in q_sems[3:]])
+
+    def M(h):
+        return Pass(me, mask_sh.at[h], lambda zs, ys, ts: m_v.at[h, zs, ys, c], lambda: m_v.at[h, :, :, c],
+                    [s.at[h] for s in m_sems])
+
+    def W(k, shard, whole, early):
+        n = shard.shape[1]
+
+        def view(zs, ys, ts):
+            return whole.at[zs, ys, c, :, pl.ds(pl.multiple_of(ts * n, 128), n)]
+
+        return Pass(me, shard, view, lambda: whole.at[:, :, c], [s.at[k] for s in w_sems], early, True)
+
+    WO, WI, WH = W(0, out_sh, out_o, False), W(1, in_sh, in_o, True), W(2, hid_sh, hid_o, False)
 
     locals_ = [
         pltpu.make_async_copy(qkv_sh, w_v.at[z, y, c], loc.at[0]),
         pltpu.make_async_copy(x_sh, x_v.at[rows_own], loc.at[1]),
         pltpu.make_async_copy(mask_sh, m_v.at[:, z, y, c], loc.at[2]),
         pltpu.make_async_copy(bin_sh, bin_o.at[t], loc.at[3]),
-    ] + [pltpu.make_async_copy(shards[k], wholes[k].at[z, y, c, :, cols(k)], loc.at[4 + k]) for k in range(3)]
+    ] + [pltpu.make_async_copy(w.own, w.view(z, y, t), loc.at[4 + k]) for k, w in enumerate((WO, WI, WH))]
     for cp in locals_:
         cp.start()
-
     me.greet()
 
     def x_copy():
@@ -109,75 +205,42 @@
     def b_copy():
         return rcopy(bin_sh, bin_o.at[t], xs.at[1], xr.at[1], me.over_t)
 
-    def qkv_z(d):
-        return rcopy(qkv_sh, w_v.at[z, y, c], qz_s.at[d - 1], qz_r.at[d - 1], me.along_z(d))
-
-    def qkv_y():
-        return rcopy(w_v.at[:, y, c], w_v.at[:, y, c], q1_s.at[0], q1_r.at[0], me.over_y)
-
-    def qkv_c():
-        return rcopy(w_v.at[:, :, c], w_v.at[:, :, c], q1_s.at[1], q1_r.at[1], me.over_c)
-
-    def mask_z(h, d):
-        return rcopy(mask_sh.at[h], m_v.at[h, z, y, c], mz_s.at[h, d - 1], mz_r.at[h, d - 1], me.along_z(d))
-
-    def mask_y(h):
-        return rcopy(m_v.at[h, :, y, c], m_v.at[h, :, y, c], m1_s.at[h, 0], m1_r.at[h, 0], me.over_y)
-
-    def mask_c(h):
-        return rcopy(m_v.at[h, :, :, c], m_v.at[h, :, :, c], m1_s.at[h, 1], m1_r.at[h, 1], me.over_c)
-
-    def w_z(k, d):
-        return rcopy(shards[k], wholes[k].at[z, y, c, :, cols(k)], wz_s.at[k, d - 1], wz_r.at[k, d - 1], me.along_z(d))
-
-    def w_y(k):
-        part = wholes[k].at[:, y, c, :, cols(k)]
-        return rcopy(part, part, w1_s.at[k, 0], w1_r.at[k, 0], me.over_y)
-
-    def w_x(k):
-        part = wholes[k].at[:, :, c, :, cols(k)]
-        return rcopy(part, part, w1_s.at[k, 1], w1_r.at[k, 1], me.over_t)
-
-    def w_c(k):
-        part = wholes[k].at[:, :, c]
-        return rcopy(part, part, w1_s.at[k, 2], w1_r.at[k, 2], me.over_c)
+    def a_cols(p):
+        return pl.ds(pl.multiple_of(t * (pairs * 128) + p * 128, 128), 128)
 
     def a_copy(p):
-        n = 128
-        at = pl.ds(pl.multiple_of(t * (pairs * n) + p * n, 128), n)
-        return rcopy(a_v.at[p, rows_other], attn_o.at[:, at], as_.at[p], ar.at[p], me.over_t)
+        return rcopy(a_v.at[p, rows_other], attn_o.at[:, a_cols(p)], as_.at[p], ar.at[p], me.over_t)
 
     def a_local(p):
-        n = 128
-        at = pl.ds(pl.multiple_of(t * (pairs * n) + p * n, 128), n)
-        return pltpu.make_async_copy(a_v.at[p, rows_own], attn_o.at[:, at], loc.at[7 + p])
-
-    zs = range(1, Z)
-
-    def start_z(make, *k):
-        for d in zs:
-            make(*k, d).start()
-
-    def wait_z(make, *k):
-        for d in zs:
-            make(*k, d).wait_recv()
-
+        return pltpu.make_async_copy(a_v.at[p, rows_own], attn_o.at[:, a_cols(p)], loc.at[7 + p])
+
+    def mask_save(h):
+        return pltpu.make_async_copy(m_v.at[h], mask_o.at[h], loc.at[10 + h])
+
+    P_Q.z_start()
+    WI.y_copy().start()
     x_copy().start()
     b_copy().start()
-    start_z(qkv_z)
-    start_z(mask_z, 0)
-    start_z(mask_z, 1)
-    start_z(w_z, 2)
+    M(0).z_start()
     for cp in locals_:
         cp.wait()
-    wait_z(qkv_z)
-    qkv_y().start()
-    wait_z(mask_z, 0)
-    mask_y(0).start()
-    qkv_y().wait_recv()
-    qkv_c().start()
+    P_Q.relay()
+    P_Q.z_wait()
+    P_Q.y_copy().start()
+    WH.z_start()
+    M(0).relay()
+    M(0).z_wait()
+    M(0).y_copy().start()
+    WI.y_copy().wait_recv()
+    WI.z_start()
+    WH.relay()
+    WH.z_wait()
+    WH.y_copy().start()
+    M(1).z_start()
+    P_Q.y_copy().wait_recv()
+    P_Q.c_copy().start()
     x_copy().wait_recv()
-    qkv_c().wait_recv()
+    P_Q.c_copy().wait_recv()
 
     step = half // 2
 
@@ -208,7 +271,6 @@
     ]
     for cp in outs:
         cp.start()
-
     blk = seq // Z
 
     def attend(p, u):
@@ -229,59 +291,82 @@
 
         lax.fori_loop(0, Z, rows_of, 0)
 
-    def mask_save(h):
-        return pltpu.make_async_copy(m_v.at[h], mask_o.at[h], loc.at[10 + h])
-
-    order = (2, 1, 0)
+    def with_0():
+        M(1).relay()
+        M(1).z_wait()
+        M(1).y_copy().start()
+        M(2).z_start()
+
+    def with_1():
+        M(3).z_start()
+
+    def with_2():
+        pass
+
+    def with_3():
+        WI.x_copy().wait_recv()
+        WI.c_copy().start()
+
+    def with_4():
+        WH.x_copy().wait_recv()
+        WH.c_copy().start()
+
+    def with_5():
+        WO.y_copy().wait_recv()
+        WO.x_copy().start()
+
+    def ahead_0():
+        pass
+
+    def ahead_1():
+        WI.relay()
+        WI.z_wait()
+        WI.x_copy().start()
+        WH.y_copy().wait_recv()
+        WH.x_copy().start()
+        M(2).relay()
+        M(2).z_wait()
+        M(2).y_copy().start()
+
+    def ahead_2():
+        M(3).relay()
+        M(3).z_wait()
+        M(3).y_copy().start()
+        M(4).z_start()
+        WO.z_start()
+
+    def ahead_3():
+        M(4).relay()
+        M(4).z_wait()
+        M(4).y_copy().start()
+        M(5).z_start()
+
+    def ahead_4():
+        WO.relay()
+        WO.z_wait()
+        WO.y_copy().start()
+        M(5).relay()
+        M(5).z_wait()
+        M(5).y_copy().start()
+
+    def ahead_5():
+        pass
+
+    ahead = (ahead_0, ahead_1, ahead_2, ahead_3, ahead_4, ahead_5)
+    beside = (with_0, with_1, with_2, with_3, with_4, with_5)
 
     def pair_step(p, carry):
-        a, b = 2 * p, 2 * p + 1
-        wait_z(mask_z, b)
-        mask_y(b).start()
-
-        @pl.when(p < pairs - 1)
-        def _():
-            start_z(mask_z, a + 2)
-
-        mask_y(a).wait_recv()
-        mask_c(a).start()
-        for n, k in enumerate(order):
-            @pl.when(p == n)
-            def _():
-                wait_z(w_z, k)
-                w_y(k).start()
-
-        @pl.when(p < pairs - 1)
-        def _():
-            start_z(mask_z, a + 3)
-
-        mask_c(a).wait_recv()
-        mask_save(a).start()
-        attend(p, 0)
-        mask_y(b).wait_recv()
-        mask_c(b).start()
-        for n, k in enumerate(order[1:]):
-            @pl.when(p == n)
-            def _():
-                start_z(w_z, k)
-
-        @pl.when(p < pairs - 1)
-        def _():
-            wait_z(mask_z, a + 2)
-            mask_y(a + 2).start()
-
-        mask_c(b).wait_recv()
-        mask_save(b).start()
-        attend(p, 1)
-        for n, k in enumerate(order):
-            @pl.when(p == n)
-            def _():
-                w_y(k).wait_recv()
-                w_x(k).start()
-                if n > 0:
-                    w_x(order[n - 1]).wait_recv()
-                    w_c(order[n - 1]).start()
-
+        for u in range(2):
+            h = 2 * p + u
+            for n in range(pairs):
+                pl.when(p == n)(ahead[2 * n + u])
+            M(h).y_copy().wait_recv()
+            M(h).c_copy().start()
+            for n in range(pairs):
+                pl.when(p == n)(beside[2 * n + u])
+            M(h).c_copy().wait_recv()
+            mask_save(h).start()
+            attend(p, u)
         a_copy(p).start()
         a_local(p).start()
         return carry
@@ -289,8 +374,8 @@
     lax.fori_loop(0, pairs, pair_step, 0)
     lse_out = pltpu.make_async_copy(lse_v, lse_o, loc.at[5])
     lse_out.start()
-    w_x(order[-1]).wait_recv()
-    w_c(order[-1]).start()
+    WO.x_copy().wait_recv()
+    WO.c_copy().start()
     for cp in outs + [lse_out]:
         cp.wait()
     for p in range(pairs):
@@ -298,22 +383,13 @@
         a_copy(p).wait()
     b_copy().wait()
     x_copy().wait_send()
-    for d in zs:
-        qkv_z(d).wait_send()
-    qkv_y().wait_send()
-    qkv_c().wait_send()
+    P_Q.finish()
     for h in range(heads):
-        for d in zs:
-            mask_z(h, d).wait_send()
-        mask_y(h).wait_send()
-        mask_c(h).wait_send()
+        M(h).finish()
         mask_save(h).wait()
-    for k in range(3):
-        for d in zs:
-            w_z(k, d).wait_send()
-        w_y(k).wait_send()
-        w_x(k).wait_send()
-        w_c(k).wait()
+    for w in (WO, WI, WH):
+        w.finish()
+        w.c_copy().wait_recv()
 
 
 def forward(deep, x, mask, qkv, w_out_t, w_in, w_hid_t, b_in, bias, b_qv):
@@ -348,26 +424,149 @@
             pltpu.VMEM((pairs, seq, 128), BF), pltpu.VMEM((pairs, seq, 128), BF), pltpu.VMEM((pairs, seq, 128), BF),
             pltpu.VMEM((pairs, seq, 128), BF),
             pltpu.VMEM((pairs, seq, 128), F32),
-            dma((16,)), dma((2,)), dma((2,)),
-            dma((Z - 1,)), dma((Z - 1,)), dma((2,)), dma((2,)),
-            dma((heads, Z - 1)), dma((heads, Z - 1)), dma((heads, 2)), dma((heads, 2)),
-            dma((3, Z - 1)), dma((3, Z - 1)), dma((3, 3)), dma((3, 3)),
-            dma((pairs,)), dma((pairs,)),
+            dma((16,)), dma((2,)), dma((2,)), dma((pairs,)), dma((pairs,)),
+            *pass_sems(), *pass_sems(heads), *pass_sems(3),
         ],
         compiler_params=pltpu.CompilerParams(collective_id=1, has_side_effects=True, vmem_limit_bytes=58 << 20),
         name="forward_attention",
     )(x, mask, qkv, w_out_t, w_in, w_hid_t, b_in, bias, b_qv)
 
 
+class Fold:
+    def __init__(self, me, near_part, far_part, lc, bufs, sems, final, lx=None, early=False, cols=None):
+        self.me, self.own, self.away, self.lc = me, near_part, far_part, lc
+        self.ly, self.lz, self.lr = bufs
+        self.s, self.r = sems
+        self.final, self.lx, self.early, self.cols = final, lx, early, cols
+
+    def base(self):
+        return self.lc if self.lx is None else self.lx
+
+    def c_copy(self):
+        return rcopy(self.away, self.lc, self.s(0), self.r(0), self.me.over_c)
+
+    def c_add(self):
+        self.c_copy().wait_recv()
+
+        def one(i, carry):
+            for j in range(self.me.Y):
+                self.lc[i, j] = self.lc[i, j] + self.own(i, j)
+            return carry
+
+        lax.fori_loop(0, self.me.Z, one, 0)
+
+    def x_copy(self):
+        me = self.me
+        return rcopy(self.lc.at[:, :, :, self.cols(1 - me.t)], self.lx, self.s(1), self.r(1), me.over_t)
+
+    def x_add(self):
+        self.x_copy().wait_recv()
+        at = self.cols(self.me.t)
+
+        def one(i, carry):
+            for j in range(self.me.Y):
+                self.lx[i, j] = self.lx[i, j] + self.lc[i, j, :, at]
+            return carry
+
+        lax.fori_loop(0, self.me.Z, one, 0)
+
+    def y_copy(self):
+        me = self.me
+        src = self.base().at[me.z, 1 - me.y] if self.early else self.base().at[:, 1 - me.y]
+        return rcopy(src, self.ly, self.s(2), self.r(2), me.over_y)
+
+    def y_add(self):
+        self.y_copy().wait_recv()
+        base, y = self.base(), self.me.y
+
+        def one(i, carry):
+            self.ly[i] = self.ly[i] + base[i, y]
+            return carry
+
+        lax.fori_loop(0, self.me.Z, one, 0)
+
+    def along(self):
+        return self.base() if self.early else self.ly
+
+    def near(self):
+        me = self.me
+        return rcopy(self.along().at[me.z_near], self.lz.at[0], self.s(3), self.r(3), me.dev(z=me.z_near))
+
+    def through(self, n):
+        me = self.me
+        place = self.along().at[me.z_far_inner if n == 0 else me.z_far_outer]
+        return rcopy(place, self.lr.at[n], self.s(4 + n), self.r(4 + n), me.dev(z=me.z_near))
+
+    def onward(self, n):
+        me = self.me
+        z = me.z_far_inner if n == 0 else me.z_far_outer
+        return rcopy(self.along().at[z], self.lz.at[1], self.s(6 + n), self.r(6), me.dev(z=z))
+
+    def z_start(self):
+        @pl.when(self.me.outer == 1)
+        def _():
+            for n in range(2):
+                self.through(n).start()
+
+        self.near().start()
+
+    def relay(self):
+        me = self.me
+
+        @pl.when(me.outer == 0)
+        def _():
+            for n in range(2):
+                self.through(n).wait_recv()
+                z = me.z_far_inner if n == 0 else me.z_far_outer
+                self.along()[z] = self.along()[z] + self.lr[n]
+                self.onward(n).start()
+
+    def z_sum(self):
+        self.near().wait_recv()
+        self.onward(0).wait_recv()
+        total = self.along()[self.me.z].astype(F32) + self.lz[0].astype(F32)
+        return total + self.lz[1].astype(F32)
+
+    def z_end(self):
+        self.final(self.z_sum())
+
+    def early_z_end(self):
+        self.base()[self.me.z] = self.z_sum().astype(BF)
+        self.y_copy().start()
+
+    def early_y_end(self):
+        self.y_copy().wait_recv()
+        self.final(self.base()[self.me.z, self.me.y].astype(F32) + self.ly[...].astype(F32))
+
+    def finish(self, skip_c=False):
+        if not skip_c:
+            self.c_copy().wait_send()
+        if self.lx is not None:
+            self.x_copy().wait_send()
+        self.y_copy().wait_send()
+        self.near().wait_send()
+
+        @pl.when(self.me.outer == 1)
+        def _():
+            for n in range(2):
+                self.through(n).wait_send()
+
+        @pl.when(self.me.outer == 0)
+        def _():
+            for n in range(2):
+                self.onward(n).wait_send()
+
+
 def bwd_kernel(deep, dat, q_h, k_h, v_h, mask_h, lse_h, x_h, qkv_h, hid_h, in_h, out_h, dz1_h, sg_h, small_h, bias,
                dx_o, gqkv_o, ghid_o, gin_o, gout_o, gmask_o, small_o,
                q_v, k_v, v_v, do_v, lse_v, m_v, p_v, dq_v, dk_v, dv_v, acck, accv,
-               lc_m, ly_m, lz_m, gm_v,
-               own_w, lc_hid, lx_hid, ly_hid, lz_hid, lc_in, lx_in, ly_in, lz_in, lc_out, lx_out, ly_out, lz_out, fin_hid, fin_in, fin_out,
-               p_q, lc_q, ly_q, lz_q, fin_q,
+               lc_m, ly_m, lz_m, lr_m, gm_v,
+               own_w, lc_hid, lx_hid, ly_hid, lz_hid, lr_hid, lc_in, lx_in, ly_in, lz_in, lr_in, lc_out, lx_out, ly_out, lz_out, lr_out,
+               fin_hid, fin_in, fin_out,
+               p_q, lc_q, ly_q, lz_q, lr_q, fin_q,
                x_v, w_v, sx_v, lx_x, dx_v, dz_v,
                s_v, sc_v, sy_v, sz_v, sx2_v,
-               loc, msem, ds_, dr, wl, w1s, w1r, wzs, wzr, m1s, m1r, mzs, mzr, q1s, q1r, qzs, qzr, xs, xr, s1s, s1r, szs, szr):
+               loc, msem, ds_, dr, wl, w_s, w_r, m_s, m_r, q_s, q_r, xs, xr, s1s, s1r, szs, szr):
     me = Place(deep)
     Z, y, c, z, t = me.Z, me.y, me.c, me.z, me.t
     pairs, seq, _ = q_v.shape
@@ -376,14 +575,6 @@
     width = x_v.shape[1]
     zs = range(1, Z)
     rows_own = pl.ds(pl.multiple_of(t * half, 128), half)
-    rows_other = pl.ds(pl.multiple_of((1 - t) * half, 128), half)
-    parts = (hid_h, in_h, out_h)
-    lcs, lxs, lys, lzs, fins = (lc_hid, lc_in, lc_out), (lx_hid, lx_in, lx_out), (ly_hid, ly_in, ly_out), (lz_hid, lz_in, lz_out), (fin_hid, fin_in, fin_out)
-    w_outs = (ghid_o, gin_o, gout_o)
-
-    def cols(k, who):
-        n = lxs[k].shape[-1]
-        return pl.ds(pl.multiple_of(who * n, 128), n)
 
     def dat_cols(p, who):
         return pl.ds(pl.multiple_of(who * (pairs * 128) + p * 128, 128), 128)
@@ -406,42 +597,45 @@
     def gm_save(h):
         return pltpu.make_async_copy(gm_v.at[h], gmask_o.at[h], loc.at[17 + h])
 
-    def own_at(k):
-        n = lcs[k].shape[-1]
-        return own_w.at[:, :, :, pl.ds(0, n)]
-
-    def own_load(k):
-        return pltpu.make_async_copy(parts[k].at[:, :, c], own_at(k), wl.at[k])
-
-    def w_c(k):
-        return rcopy(parts[k].at[:, :, 1 - c], lcs[k], w1s.at[k, 0], w1r.at[k, 0], me.over_c)
-
-    def w_x(k):
-        return rcopy(lcs[k].at[:, :, :, cols(k, 1 - t)], lxs[k], w1s.at[k, 1], w1r.at[k, 1], me.over_t)
-
-    def w_y(k):
-        return rcopy(lxs[k].at[:, 1 - y], lys[k], w1s.at[k, 2], w1r.at[k, 2], me.over_y)
-
-    def w_z(k, d):
-        return rcopy(lys[k].at[lax.rem(z + d, Z)], lzs[k].at[d - 1], wzs.at[k, d - 1], wzr.at[k, d - 1], me.along_z(d))
-
-    def m_c(h, slot):
-        return rcopy(p_v.at[slot, :, :, 1 - c], lc_m.at[h], m1s.at[h, 0], m1r.at[h, 0], me.over_c)
-
-    def m_y(h):
-        return rcopy(lc_m.at[h, :, 1 - y], ly_m.at[h], m1s.at[h, 1], m1r.at[h, 1], me.over_y)
-
-    def m_z(h, d):
-        return rcopy(ly_m.at[h, lax.rem(z + d, Z)], lz_m.at[h, d - 1], mzs.at[h, d - 1], mzr.at[h, d - 1], me.along_z(d))
-
-    def q_c():
-        return rcopy(p_q.at[:, :, 1 - c], lc_q, q1s.at[0], q1r.at[0], me.over_c)
-
-    def q_y():
-        return rcopy(lc_q.at[:, 1 - y], ly_q, q1s.at[1], q1r.at[1], me.over_y)
-
-    def q_z(d):
-        return rcopy(ly_q.at[lax.rem(z + d, Z)], lz_q.at[d - 1], qzs.at[d - 1], qzr.at[d - 1], me.along_z(d))
+    def M(h, slot=None):
+        def own(i, j):
+            return p_v[slot, i, j, c]
+
+        def final(total):
+            sg_load(h).wait()
+            gm_v[h] = total * gm_v[h]
+            gm_save(h).start()
+
+        away = None if slot is None else p_v.at[slot, :, :, 1 - c]
+        return Fold(me, own, p_v.at[0, :, :, 1 - c] if away is None else away, lc_m.at[h],
+                    (ly_m.at[h], lz_m.at[h], lr_m.at[h]), (lambda n: m_s.at[h, n], lambda n: m_r.at[h, n]), final)
+
+    def W(k, part, lc, lx, ly, lz, lr, fin, out, early):
+        n = lx.shape[-1]
+
+        def own(i, j):
+            return own_w[i, j, :, 0:2 * n]
+
+        def final(total):
+            fin[...] = total
+            pltpu.make_async_copy(fin, out, wl.at[3 + k]).start()
+
+        fold = Fold(me, own, part.at[:, :, 1 - c], lc, (ly, lz, lr), (lambda i: w_s.at[k, i], lambda i: w_r.at[k, i]), final,
+                    lx, early, lambda who: pl.ds(pl.multiple_of(who * n, 128), n))
+        fold.own_load = lambda: pltpu.make_async_copy(part.at[:, :, c], own_w.at[:, :, :, pl.ds(0, 2 * n)], wl.at[k])
+        fold.saved = lambda: pltpu.make_async_copy(fin, out, wl.at[3 + k])
+        return fold
+
+    WH = W(0, hid_h, lc_hid, lx_hid, ly_hid, lz_hid, lr_hid, fin_hid, ghid_o, False)
+    WI = W(1, in_h, lc_in, lx_in, ly_in, lz_in, lr_in, fin_in, gin_o, True)
+    WO = W(2, out_h, lc_out, lx_out, ly_out, lz_out, lr_out, fin_out, gout_o, False)
+
+    def q_final(total):
+        fin_q[...] = total
+        pltpu.make_async_copy(fin_q, gqkv_o, loc.at[24]).start()
+
+    Q = Fold(me, lambda i, j: p_q[i, j, c], p_q.at[:, :, 1 - c], lc_q, (ly_q, lz_q, lr_q),
+             (lambda n: q_s.at[n], lambda n: q_r.at[n]), q_final)
 
     def x_copy():
         return rcopy(sx_v, lx_x, xs, xr, me.over_t)
@@ -461,37 +655,21 @@
     def s_x():
         return rcopy(s_v, sx2_v, s1s.at[2], s1r.at[2], me.over_t)
 
+    m_load(0, 0).start()
+    for cp in loads[:4]:
+        cp.start()
     for p in range(pairs):
         dat_local(p).start()
-    for cp in loads:
+    WH.own_load().start()
+    for cp in loads[4:]:
         cp.start()
-    own_load(0).start()
-    m_load(0, 0).start()
     me.greet()
     for p in range(pairs):
         dat_copy(p).start()
-    for k in range(3):
-        w_c(k).start()
+    for w in (WH, WI, WO):
+        w.c_copy().start()
     for h in range(heads):
         sg_load(h).start()
-
-    def add_own(k):
-        own_load(k).wait()
-        w_c(k).wait_recv()
-        n = lcs[k].shape[-1]
-
-        def one(i, carry):
-            for j in range(me.Y):
-                lcs[k][i, j] = lcs[k][i, j] + own_w[i, j, :, 0:n]
-            return carry
-
-        lax.fori_loop(0, Z, one, 0)
-
-    for k in range(3):
-        add_own(k)
-        if k < 2:
-            own_load(k + 1).start()
-        w_x(k).start()
     for cp in loads:
         cp.wait()
 
@@ -503,7 +681,13 @@
         acck[...] = jnp.zeros_like(acck)
         accv[...] = jnp.zeros_like(accv)
 
-        def rows_of(b, carry):
+        def rows_of(n, carry):
+            b = lax.rem(t * (Z // 2) + n, Z)
+            if u == 0:
+                @pl.when(n == Z // 2)
+                def _():
+                    dat_copy(p).wait_recv()
+
             rows = pl.ds(pl.multiple_of(b * blk, blk), blk)
             qb, dob = q_v[p, rows, sl], do_v[p, rows, sl]
             kk, vv = k_v[p, :, sl], v_v[p, :, sl]
@@ -523,105 +707,76 @@
         dk_v[p, :, sl] = acck[...].astype(BF)
         dv_v[p, :, sl] = accv[...].astype(BF)
 
-    def m_add_c(h, slot):
-        m_c(h, slot).wait_recv()
-
-        def one(i, carry):
-            for j in range(me.Y):
-                lc_m[h, i, j] = lc_m[h, i, j] + p_v[slot, i, j, c]
-            return carry
-
-        lax.fori_loop(0, Z, one, 0)
-        m_y(h).start()
-
-    def m_add_y(h):
-        m_y(h).wait_recv()
-
-        def one(i, carry):
-            ly_m[h, i] = ly_m[h, i] + lc_m[h, i, y]
-            return carry
-
-        lax.fori_loop(0, Z, one, 0)
-        for d in zs:
-            m_z(h, d).start()
-
-    def m_end(h):
-        total = ly_m[h, z].astype(F32)
-        for d in zs:
-            m_z(h, d).wait_recv()
-            total = total + lz_m[h, d - 1].astype(F32)
-        sg_load(h).wait()
-        gm_v[h] = total * gm_v[h]
-        gm_save(h).start()
-
-    def head_step(p, u):
-        h = 2 * p + u
-        m_load(h, u).wait()
-        if u == 0:
-            m_load(h + 1, 1).start()
-        else:
-            @pl.when(p < pairs - 1)
-            def _():
-                m_load(h + 1, 0).start()
-
-        @pl.when(p > 0)
-        def _():
-            m_c(h - 2, u).wait_send()
-
-        attend(p, u, u)
-        m_c(h, u).start()
-        if u == 1:
-            m_add_c(h - 1, 0)
-        else:
+    def after_0():
+        WH.own_load().wait()
+        WH.c_add()
+        WI.own_load().start()
+        WH.x_copy().start()
+        M(0, 0).c_add()
+        M(0).y_copy().start()
+
+    def after_1():
+        WI.own_load().wait()
+        WI.c_add()
+        WO.own_load().start()
+        WI.x_copy().start()
+        M(1, 1).c_add()
+        M(1).y_copy().start()
+
+    def after_2():
+        WO.own_load().wait()
+        WO.c_add()
+        WO.x_copy().start()
+        M(2, 0).c_add()
+        M(2).y_copy().start()
+        M(0).y_add()
+        M(0).z_start()
+
+    def after_3():
+        M(3, 1).c_add()
+        M(3).y_copy().start()
+        WH.x_add()
+        WH.y_copy().start()
+        M(0).relay()
+
+    def after_4():
+        M(1).y_add()
+        M(1).z_start()
+        M(4, 0).c_add()
+        M(4).y_copy().start()
+
+    def after_5():
+        M(1).relay()
+        M(2).y_add()
+        M(2).z_start()
+        M(5, 1).c_add()
+        M(5).y_copy().start()
+
+    after = (after_0, after_1, after_2, after_3, after_4, after_5)
+
+    def pair_step(p, carry):
+        dat_local(p).wait()
+        for u in range(2):
+            h = 2 * p + u
+            m_load(h, u).wait()
+            if u == 0:
+                m_load(h + 1, 1).start()
+            else:
+                @pl.when(p < pairs - 1)
+                def _():
+                    m_load(h + 1, 0).start()
+
             @pl.when(p > 0)
             def _():
-                m_add_c(h - 1, 1)
-
-        @pl.when(h >= 2)
-        def _():
-            m_add_y(h - 2)
-
-    def pair_step(p, carry):
-        dat_local(p).wait()
-        dat_copy(p).wait_recv()
-        head_step(p, 0)
-        head_step(p, 1)
+                M(h - 2, u).c_copy().wait_send()
+
+            attend(p, u, u)
+            M(h, u).c_copy().start()
+            for n in range(pairs):
+                pl.when(p == n)(after[2 * n + u])
         return carry
 
     lax.fori_loop(0, pairs, pair_step, 0)
-
-    def w_add_x(k):
-        w_x(k).wait_recv()
-
-        def one(i, carry):
-            for j in range(me.Y):
-                lxs[k][i, j] = lxs[k][i, j] + lcs[k][i, j, :, cols(k, t)]
-            return carry
-
-        lax.fori_loop(0, Z, one, 0)
-        w_y(k).start()
-
-    def w_add_y(k):
-        w_y(k).wait_recv()
-
-        def one(i, carry):
-            lys[k][i] = lys[k][i] + lxs[k][i, y]
-            return carry
-
-        lax.fori_loop(0, Z, one, 0)
-        for d in zs:
-            w_z(k, d).start()
-
-    def w_end(k):
-        total = lys[k][z].astype(F32)
-        for d in zs:
-            w_z(k, d).wait_recv()
-            total = total + lzs[k][d - 1].astype(F32)
-        fins[k][...] = total
-        pltpu.make_async_copy(fins[k], w_outs[k], wl.at[3 + k]).start()
-
-    m_add_c(heads - 1, 1)
-    w_add_x(0)
 
     step = half // 2
 
@@ -648,7 +803,8 @@
     for j, ref in enumerate((dq_v, dk_v, dv_v)):
         g = dot_0(x_v[...], d_cat(ref, slice(None)))
         p_q[:, :, :, j] = g.astype(BF).reshape(p_q.shape[:3] + p_q.shape[4:])
-    q_c().start()
+    Q.c_copy().start()
+    M(2).relay()
     base = small_h.shape[0]
     for n, ref in enumerate((dq_v, dv_v)):
         for p in range(pairs):
@@ -657,6 +813,8 @@
     for at in range(base + 2 * pairs, s_v.shape[0]):
         s_v[at:at + 1, :] = jnp.zeros((1, 128), F32)
     s_c().start()
+    Q.c_add()
+    Q.y_copy().start()
 
     def mine(r, carry):
         at = pl.ds(pl.multiple_of(r * step, step), step)
@@ -665,48 +823,48 @@
         return carry
 
     lax.fori_loop(0, 2, mine, 0)
-    q_c().wait_recv()
-    for i in range(Z):
-        lc_q[i] = lc_q[i] + p_q[i, :, c]
-    q_y().start()
     s_c().wait_recv()
     sc_v[...] = sc_v[...] + s_v[...]
     s_y().start()
-    m_add_y(heads - 2)
-    w_add_x(1)
-    m_end(0)
-    m_end(1)
-    w_add_x(2)
-    m_end(2)
-    m_add_y(heads - 1)
-    m_end(3)
-    w_add_y(0)
-    m_end(4)
-    q_y().wait_recv()
-    for i in range(Z):
-        ly_q[i] = ly_q[i] + lc_q[i, y]
-    for d in zs:
-        q_z(d).start()
+    M(3).y_add()
+    M(3).z_start()
+    WI.x_add()
+    WI.z_start()
+    M(0).z_end()
+    WO.x_add()
+    WO.y_copy().start()
+    M(3).relay()
+    WI.relay()
+    WH.y_add()
+    WH.z_start()
+    M(1).z_end()
+    M(2).z_end()
+    M(4).y_add()
+    M(4).z_start()
+    WH.relay()
+    WI.early_z_end()
+    M(3).z_end()
+    M(4).relay()
+    M(5).y_add()
+    M(5).z_start()
     s_y().wait_recv()
     sy_v[...] = sy_v[...] + sc_v[...]
     sz_v[z] = sy_v[...]
     for d in zs:
         s_z(d).start()
-    m_end(5)
-    w_add_y(1)
-    w_end(0)
-    w_add_y(2)
+    Q.y_add()
+    Q.z_start()
+    WH.z_end()
+    M(5).relay()
+    WO.y_add()
+    WO.z_start()
+    Q.relay()
+    M(4).z_end()
     x_copy().wait_recv()
     dx_v[...] = dx_v[...] + lx_x[...].astype(F32)
     dx_save = pltpu.make_async_copy(dx_v, dx_o, loc.at[23])
     dx_save.start()
-    total = ly_q[z].astype(F32)
-    for d in zs:
-        q_z(d).wait_recv()
-        total = total + lz_q[d - 1].astype(F32)
-    fin_q[...] = total
-    q_save = pltpu.make_async_copy(fin_q, gqkv_o, loc.at[24])
-    q_save.start()
+    WO.relay()
     for d in zs:
         s_z_in(d).wait_recv()
     s_c().wait_send()
@@ -715,42 +873,33 @@
         total = total + sz_v[i]
     s_v[...] = total
     s_x().start()
-    w_end(1)
-    w_end(2)
+    M(5).z_end()
+    WI.early_y_end()
+    Q.z_end()
+    WO.z_end()
     s_x().wait_recv()
     low = sx2_v[...] + s_v[...]
     row = lax.broadcasted_iota(jnp.int32, low.shape, 0)
-    sy_done = s_y()
-    sy_done.wait_send()
+    s_y().wait_send()
     sc_v[...] = jnp.where(row < base, low, s_v[...])
     s_save = pltpu.make_async_copy(sc_v, small_o, loc.at[25])
     s_save.start()
 
     for p in range(pairs):
         dat_copy(p).wait_send()
-    for k in range(3):
-        w_c(k).wait_send()
-        w_x(k).wait_send()
-        w_y(k).wait_send()
-        for d in zs:
-            w_z(k, d).wait_send()
-        pltpu.make_async_copy(fins[k], w_outs[k], wl.at[3 + k]).wait()
+    for w in (WH, WI, WO):
+        w.finish()
+        w.saved().wait()
     for h in range(heads):
-        if h >= heads - 2:
-            m_c(h, h % 2).wait_send()
-        m_y(h).wait_send()
-        for d in zs:
-            m_z(h, d).wait_send()
+        M(h).finish(h < heads - 2)
         gm_save(h).wait()
-    q_c().wait_send()
-    q_y().wait_send()
+    Q.finish()
     for d in zs:
-        q_z(d).wait_send()
         s_z(d).wait_send()
     x_copy().wait_send()
     s_x().wait_send()
     dx_save.wait()
-    q_save.wait()
+    pltpu.make_async_copy(fin_q, gqkv_o, loc.at[24]).wait()
     s_save.wait()
 
 
@@ -772,8 +921,9 @@
     )
     pair = vm((pairs, seq, 128), BF)
 
-    def chain(m):
-        return [vm((Z, Y, r, 2 * m), BF), vm((Z, Y, r, m), BF), vm((Z, r, m), BF), vm((Z - 1, r, m), BF)]
+    def chain(m, early):
+        last = (Y, r, m) if early else (r, m)
+        return [vm((Z, Y, r, 2 * m), BF), vm((Z, Y, r, m), BF), vm((r, m) if early else (Z, r, m), BF), vm((2,) + last, BF), vm((2,) + last, BF)]
 
     three, rq, nq = qkv.shape[3:]
     return pl.pallas_call(
@@ -784,15 +934,15 @@
         scratch_shapes=[
             pair, pair, pair, pair, vm((pairs, seq, 128), F32), vm((2, Z, Y, C, blk, seq), BF), vm((2, Z, Y, C, blk, seq), BF),
             pair, pair, pair, vm((seq, 64), F32), vm((seq, 64), F32),
-            vm((heads, Z, Y, blk, seq), BF), vm((heads, Z, blk, seq), BF), vm((heads, Z - 1, blk, seq), BF), vm((heads, blk, seq), F32),
-            vm((Z, Y, r, n2), BF), *chain(n), *chain(n), *chain(no), vm((r, n), F32), vm((r, n), F32), vm((r, no), F32),
-            vm((Z, Y, C, three, rq, nq), BF), vm((Z, Y, three, rq, nq), BF), vm((Z, three, rq, nq), BF), vm((Z - 1, three, rq, nq), BF), vm((three, rq, nq), F32),
+            vm((heads, Z, Y, blk, seq), BF), vm((heads, Z, blk, seq), BF), vm((heads, 2, blk, seq), BF), vm((heads, 2, blk, seq), BF),
+            vm((heads, blk, seq), F32),
+            vm((Z, Y, r, n2), BF), *chain(n, False), *chain(n, True), *chain(no, False), vm((r, n), F32), vm((r, n), F32), vm((r, no), F32),
+            vm((Z, Y, C, three, rq, nq), BF), vm((Z, Y, three, rq, nq), BF), vm((Z, three, rq, nq), BF),
+            vm((2, three, rq, nq), BF), vm((2, three, rq, nq), BF), vm((three, rq, nq), F32),
             vm((seq, width), BF), vm((Z, Y, C, three, rq, nq), BF), vm((half, width), BF), vm((half, width), BF), vm((half, width), F32), vm((half, width), F32),
             vm((rows_s, 128), F32), vm((rows_s, 128), F32), vm((rows_s, 128), F32), vm((Z, rows_s, 128), F32), vm((rows_s, 128), F32),
             dma((26,)), dma((2,)), dma((pairs,)), dma((pairs,)),
-            dma((6,)), dma((3, 3)), dma((3, 3)), dma((3, Z - 1)), dma((3, Z - 1)),
-            dma((heads, 2)), dma((heads, 2)), dma((heads, Z - 1)), dma((heads, Z - 1)),
-            dma((2,)), dma((2,)), dma((Z - 1,)), dma((Z - 1,)), dma, dma,
+            dma((6,)), dma((3, 8)), dma((3, 7)), dma((heads, 8)), dma((heads, 7)), dma((8,)), dma((7,)), dma, dma,
             dma((3,)), dma((3,)), dma((Z - 1,)), dma((Z - 1,)),
         ],
         compiler_params=pltpu.CompilerParams(collective_id=2, has_side_effects=True, vmem_limit_bytes=62 << 20),
@@ -1156,7 +1306,7 @@
 
     def run(*args):
         w_rows, m_rows = args[8].shape[0], args[14].shape[1]
-        tiled = w_rows % 16 == 0 and m_rows % 16 == 0 and args[0].shape[0] == 1
+        tiled = w_rows % 16 == 0 and m_rows % 16 == 0 and args[0].shape[0] == 1 and mesh.shape["dp"] == 16
         return (body if tiled else plain_body)(*args)
 
     return jax.shard_map(

time: 377 us -> 342 us (0.907)
  Pallas kernels: 304 us -> 269 us
    pallas_call x1, Pallas kernels: 159 us -> 135 us  [backward(): pl.pallas_call(functools.partial(bwd_kernel, deep), out_shape=out_shape,...]
    pallas_call x1, Pallas kernels: 145 us -> 134 us  [forward(): pl.pallas_call(functools.partial(fwd_kernel, deep), out_shape=out_shape,...]
where the time goes in v2:
time: 342 us
  Pallas kernels  269 us (79%)
  matrix products  49 us (14%)
  local copies, waits for them, and re-layouts  11.8 us (3%)
  other arithmetic  10.2 us (3%)
    pallas_call x1, Pallas kernels, backward(): pl.pallas_call(functools.partial(bwd_kernel, deep), out_shape=out_shape,...  135 us
    pallas_call x1, Pallas kernels, forward(): pl.pallas_call(functools.partial(fwd_kernel, deep), out_shape=out_shape,...  134 us
    dot_general x3, matrix products, dot(): return jnp.dot(a, b, preferred_element_type=F32)  29.2 us
    dot_general x3, matrix products, dot_0(): lax.dot_general(a, b, (((0,), (0,)), ((), ())), preferred_element_type=F32)  11.3 us
    dot_general x3, matrix products, dot_t(): lax.dot_general(a, b, (((1,), (1,)), ((), ())), preferred_element_type=F32)  8.51 us
    unnamed x72, local copies, waits for them, and re-layouts  7.16 us

profile of v2, /device:TPU:0, one launch (start us, length us, event | category | flops | bytes accessed | tf_op | source)
XLA Modules:
  0.0 341.9 jit_solution(2109216512193336937)
XLA Ops:
  1.3 0.6 compare_select_fusion.1.bias
  1.9 4.5 %add_divide_fusion = (f32[6,64,1024]{2,1,0:T(8,128)}, bf16[6,64,1024]{2,1,0:T(8,128)(2,1)}) fusion(f32[6,64,1024]{2,1,0:T(8,128)} %param.31, f32[6,64,1024]{2,1,0:T(8,128)} %param.32), kind=kLoop, calls=%fused_computation.26 | loop fusion | flops 4718592 | bytes 5505024 | tf_op jit(solution)/shard_map/div | solution.py:1234
  6.4 0.0 copy-done.12
  6.4 0.6 broadcast_in_dim.14.bin_sh
  7.0 133.7 %forward_attention.1 = (bf16[512,768]{1,0:T(8,128)(2,1)}, bf16[3,1024,128]{2,1,0:T(8,128)(2,1)}, bf16[3,1024,128]{2,1,0:T(8,128)(2,1)}, bf16[3,1024,128]{2,1,0:T...) custom-call(bf16[512,768]{1,0:T(8,128)(2,1)} %bitcast.65, ...), custom_call_target="tpu_custom_call" | custom-call | tf_op jit(solution)/shard_map/forward_attention/pallas_call | solution.py:415
  140.7 0.0 copy-start.13
  140.8 0.0 slice-start.2
  140.8 2.6 fusion.27
  143.4 0.3 multiply_reduce_fusion.5
  143.7 0.0 slice-start.3
  143.7 0.0 copy-start.20
  143.7 19.3 %multiply_convert_fusion = (bf16[512,3072]{1,0:T(8,128)(2,1)S(1)}, f32[512,3072]{1,0:T(8,128)}, f32[512,3072]{1,0:T(8,128)}) fusion(f32[3072]{0:T(1024)} %bitcast.81, bf16[768,3072]{1,0:T(8,128)(2,1)S(1)} %bitcast.71, f32[512,768]{1,0:T(8,128)S(1)} %get-tuple-element.78, f32[768]{0:T(1024)S(1)} %copy-done.21, f32[768]{0:T(1024)S(1)} %copy-done.13, ...), kind=kOutput, calls=%fused_computation.4 | convolution fusion | flops 2521694208 | bytes 22042624 | tf_op jit(solution)/shard_map/dot_general | solution.py:68
  163.0 0.0 copy-start.11
  163.0 2.8 fusion.28
  165.9 0.3 multiply_reduce_fusion.4
  166.2 0.0 copy-start.14
  166.2 0.0 copy-start.1
  166.3 0.0 copy-done.11
  166.3 0.0 copy-start.16
  166.3 0.0 copy-start.18
  166.3 2.4 multiply_reduce_fusion
  168.7 0.0 slice-start
  168.7 1.6 fusion.24
  170.3 8.2 %convert_reduce_fusion = (f32[3072]{0:T(1024)S(1)}, bf16[512,3072]{1,0:T(8,128)(2,1)S(1)}) fusion(f32[512,3072]{1,0:T(8,128)} %get-tuple-element.66, bf16[768,3072]{1,0:T(8,128)(2,1)S(1)} %bitcast.78, f32[512,768]{1,0:T(8,128)S(1)} %get-tuple-element.62, f32[512,3072]{1,0:T(8,128)} %get-tuple-element.79, f32[3072]{0:T(1024)S(1)} %bitcast.82), kind=kOutput, calls=%fused_computation.2 | convolution fusion | flops 2443047936 | bytes 22044672 | tf_op jit(solution)/shard_map/dot_general | solution.py:68
  178.6 0.0 copy-start.24
  178.6 0.0 copy-done.3
  178.6 0.0 slice-done
  178.6 0.0 slice-done.1
  178.6 3.1 multiply_reduce_fusion.1
  181.8 0.0 copy-start.6
  181.8 0.5 fusion.25
  182.4 0.7 pad.4.small_h
  183.1 1.9 convolution_convert_fusion.2
  185.0 0.3 copy-done.25
  185.3 4.8 %convolution_convert_fusion = bf16[768,3072]{1,0:T(8,128)(2,1)} fusion(bf16[512,3072]{1,0:T(8,128)(2,1)S(1)} %copy-done.25, f32[512,768]{1,0:T(8,128)S(1)} %get-tuple-element.78, f32[768]{0:T(1024)S(1)} %copy-done.21, f32[768]{0:T(1024)S(1)} %copy-done.13, f32[512]{0:T(512)S(1)} %add_rsqrt_fusion.1, f32[512]{0:T(512)S(1)} %broadcast_multiply_fusion.5), kind=kOutput, calls=%fused_computation.18 | convolution fusion | flops 2420244480 | bytes 9447424 | tf_op jit(solution)/shard_map/dot_general | solution.py:76
  190.1 4.6 %convolution_convert_fusion.1 = bf16[768,3072]{1,0:T(8,128)(2,1)} fusion(bf16[512,3072]{1,0:T(8,128)(2,1)S(1)} %copy-done.23, f32[512,768]{1,0:T(8,128)S(1)} %copy-done.4), kind=kOutput, calls=%fused_computation.19 | convolution fusion | flops 2418671616 | bytes 9437184 | tf_op jit(solution)/shard_map/dot_general | solution.py:76
  194.7 1.7 convolution_convert_fusion.3.dat
  196.4 135.3 %backward_attention.1 = (f32[512,768]{1,0:T(8,128)}, f32[3,48,384]{2,1,0:T(8,128)}, f32[48,1536]{1,0:T(8,128)}, f32[48,1536]{1,0:T(8,128)}, f32[48,384]{1,0:T(8,...) custom-call(bf16[512,768]{1,0:T(8,128)(2,1)} %convolution_convert_fusion.3.dat, ...), custom_call_target="tpu_custom_call" | custom-call | tf_op jit(solution)/shard_map/backward_attention/pallas_call | solution.py:929
  331.8 1.4 slice_bitcast_fusion.1
  333.2 0.6 reshape.140
  333.7 0.7 slice_bitcast_fusion
  334.5 0.7 dynamic_slice.3
  335.1 2.8 copy.46
  338.0 0.7 copy.47
  338.6 0.6 copy.48
  339.3 0.7 copy.49
  340.0 0.7 copy.50
  340.7 1.1 copy.51
  (60 shorter events, 0.2 us)
Async XLA Ops:
  1.9 4.5 %copy-start.12 = (f32[1536]{0:T(1024)S(1)}, f32[1536]{0:T(1024)}, u32[]{:S(2)}) copy-start(f32[1536]{0:T(1024)} %param.26) | copy-start | bytes 18436
  6.4 134.3 %copy-start.5 = (bf16[1,512,768]{2,1,0:T(8,128)(2,1)S(1)}, bf16[1,512,768]{2,1,0:T(8,128)(2,1)}, u32[]{:S(2)}) copy-start(bf16[1,512,768]{2,1,0:T(8,128)(2,1)} %param.17) | copy-start | bytes 2359300
  6.4 134.3 %copy-start.19 = (f32[768]{0:T(1024)S(1)}, f32[768]{0:T(1024)}, u32[]{:S(2)}) copy-start(f32[768]{0:T(1024)} %param.22) | copy-start | bytes 9220
  7.0 136.7 %copy-start.21 = (f32[768]{0:T(1024)S(1)}, f32[768]{0:T(1024)}, u32[]{:S(2)}) copy-start(f32[768]{0:T(1024)} %param.24) | copy-start | bytes 9220
  140.7 2.9 copy-start.13
  140.8 2.9 copy-start.15
  140.8 22.2 %slice-start.2 = ((s8[4718592]{0:T(1024)(128)(4,1)}), s8[4194304]{0:T(1024)(128)(4,1)S(1)}, s32[]{:S(2)}) async-start(s8[4718592]{0:T(1024)(128)(4,1)} %bitcast.75), calls=%async_computation.2 | async-start | bytes 8388608
  143.7 19.3 %slice-start.3 = ((s8[4718592]{0:T(1024)(128)(4,1)}), s8[524288]{0:T(1024)(128)(4,1)S(1)}, s32[]{:S(2)}) async-start(s8[4718592]{0:T(1024)(128)(4,1)} %bitcast.75), calls=%async_computation.3 | async-start | bytes 1048576
  143.7 19.3 %copy-start.20 = (f32[768]{0:T(1024)S(1)}, f32[768]{0:T(1024)}, u32[]{:S(2)}) copy-start(f32[768]{0:T(1024)} %param.28) | copy-start | bytes 9220
  163.0 2.9 copy-start.22
  163.0 3.2 copy-start.11
  166.2 2.5 copy-start.14
  166.2 2.5 copy-start.1
  166.3 4.1 %copy-start.16 = (bf16[4,2,2,48,3072]{4,3,2,1,0:T(8,128)(2,1)S(1)}, bf16[4,2,2,48,3072]{4,3,2,1,0:T(8,128)(2,1)}, u32[]{:S(2)}) copy-start(bf16[4,2,2,48,3072]{4,3,2,1,0:T(8,128)(2,1)} %get-tuple-element.38) | copy-start | bytes 14155780
  166.3 4.0 %copy-start.18 = (f32[2,1,1536]{2,1,0:T(1,128)S(1)}, f32[2,1,1536]{2,1,0:T(1,128)}, u32[]{:S(2)}) copy-start(f32[2,1,1536]{2,1,0:T(1,128)} %get-tuple-element.37) | copy-start | bytes 36868
  168.7 9.9 %slice-start = ((s8[4718592]{0:T(1024)(128)(4,1)}), s8[4194304]{0:T(1024)(128)(4,1)S(1)}, s32[]{:S(2)}) async-start(s8[4718592]{0:T(1024)(128)(4,1)} %bitcast.72), calls=%async_computation | async-start | bytes 8388608
  170.3 8.3 %copy-start.3 = (f32[512,768]{1,0:T(8,128)}, f32[512,768]{1,0:T(8,128)S(1)}, u32[]{:S(2)}) copy-start(f32[512,768]{1,0:T(8,128)S(1)} %get-tuple-element.62) | copy-start | bytes 4718596
  170.3 8.3 %slice-start.1 = ((s8[4718592]{0:T(1024)(128)(4,1)}), s8[524288]{0:T(1024)(128)(4,1)S(1)}, s32[]{:S(2)}) async-start(s8[4718592]{0:T(1024)(128)(4,1)} %bitcast.72), calls=%async_computation.1 | async-start | bytes 1048576
  178.6 3.2 copy-start.24
  181.8 1.3 copy-start.6
  182.3 12.4 %copy-start = (f32[512,768]{1,0:T(8,128)}, f32[512,768]{1,0:T(8,128)S(1)}, u32[]{:S(2)}) copy-start(f32[512,768]{1,0:T(8,128)S(1)} %get-tuple-element.64.dz1_h) | copy-start | bytes 4718596
  183.1 2.2 copy-start.25
  185.3 4.8 %copy-start.4 = (f32[512,768]{1,0:T(8,128)S(1)}, f32[512,768]{1,0:T(8,128)}, u32[]{:S(2)}) copy-start(f32[512,768]{1,0:T(8,128)} %copy-done.3) | copy-start | bytes 4718596
  185.3 4.8 %copy-start.23 = (bf16[512,3072]{1,0:T(8,128)(2,1)S(1)}, bf16[512,3072]{1,0:T(8,128)(2,1)}, u32[]{:S(2)}) copy-start(bf16[512,3072]{1,0:T(8,128)(2,1)} %copy-done.22) | copy-start | bytes 9437188
  190.1 4.7 %copy-start.17 = (bf16[4,2,2,48,768]{4,3,2,1,0:T(8,128)(2,1)S(1)}, bf16[4,2,2,48,768]{4,3,2,1,0:T(8,128)(2,1)}, u32[]{:S(2)}) copy-start(bf16[4,2,2,48,768]{4,3,2,1,0:T(8,128)(2,1)} %get-tuple-element.35) | copy-start | bytes 3538948
  331.7 6.2 %copy-start.9 = (f32[3,48,384]{2,1,0:T(8,128)S(1)}, f32[3,48,384]{2,1,0:T(8,128)}, u32[]{:S(2)}) copy-start(f32[3,48,384]{2,1,0:T(8,128)} %get-tuple-element.104) | copy-start | bytes 663556
  335.1 3.5 %copy-start.10 = (f32[48,384]{1,0:T(8,128)S(1)}, f32[48,384]{1,0:T(8,128)}, u32[]{:S(2)}) copy-start(f32[48,384]{1,0:T(8,128)} %get-tuple-element.49) | copy-start | bytes 221188
  335.1 4.1 %copy-start.8 = (f32[48,1536]{1,0:T(8,128)S(1)}, f32[48,1536]{1,0:T(8,128)}, u32[]{:S(2)}) copy-start(f32[48,1536]{1,0:T(8,128)} %get-tuple-element.110) | copy-start | bytes 884740
  335.1 4.9 %copy-start.7 = (f32[48,1536]{1,0:T(8,128)S(1)}, f32[48,1536]{1,0:T(8,128)}, u32[]{:S(2)}) copy-start(f32[48,1536]{1,0:T(8,128)} %get-tuple-element.51) | copy-start | bytes 884740
  335.1 5.6 %copy-start.2 = (f32[6,64,1024]{2,1,0:T(8,128)S(1)}, f32[6,64,1024]{2,1,0:T(8,128)}, u32[]{:S(2)}) copy-start(f32[6,64,1024]{2,1,0:T(8,128)} %get-tuple-element.116) | copy-start | bytes 4718596

commit v3 on v2

--- a/solution.py
+++ b/solution.py
@@ -76,6 +76,112 @@
     return lax.dot_general(a, b, (((0,), (0,)), ((), ())), preferred_element_type=F32)
 
 
+def norm_stats(rows):
+    centre = rows - jnp.mean(rows, axis=-1, keepdims=True)
+    scale = lax.rsqrt(jnp.mean(centre * centre, axis=-1, keepdims=True) + EPS)
+    return centre * scale, scale
+
+
+def norm_back(e, hat, scale):
+    return (e - jnp.mean(e, axis=-1, keepdims=True) - hat * jnp.mean(e * hat, axis=-1, keepdims=True)) * scale
+
+
+def middle_math(attn, x, wo, wi, wh, b_out, b_in, b_hid, g1, c1, g2, c2, cot, length, first,
+                out, dz1, gout, dat, small, hat1_v, s1_v, h1b_v, ht_v, act_v, dg_v, z_v, hat2_v, zt_v,
+                put_hid, put_in, ready, turned):
+    half, width = hat1_v.shape
+    wide = act_v.shape[1]
+    rb, step = half // 2, 512
+
+    def by_rows(body):
+        def one(r, carry):
+            body(pl.ds(pl.multiple_of(r * rb, rb), rb), r)
+            return carry
+
+        lax.fori_loop(0, half // rb, one, 0)
+
+    def by_cols(body):
+        def one(j, carry):
+            body(pl.ds(pl.multiple_of(j * step, step), step), j)
+            return carry
+
+        lax.fori_loop(0, wide // step, one, 0)
+
+    def put(n, vec, add):
+        for i in range(width // 128):
+            at = n * (width // 128) + i
+            piece = vec[:, i * 128:(i + 1) * 128]
+            small[at:at + 1, :] = small[at:at + 1, :] + piece if add else piece
+
+    small[...] = jnp.zeros_like(small)
+
+    def first_norm(rows, r):
+        z1 = x(rows).astype(F32) + dot_t(attn[rows, :], wo()) + b_out[...]
+        hat, scale = norm_stats(z1)
+        hat1_v[rows, :] = hat
+        s1_v[rows, 0:1] = scale
+        h1 = hat * g1[...] + c1[...]
+        h1b_v[rows, :] = h1.astype(BF)
+        z_v[rows, :] = h1 + b_hid[...]
+
+    by_rows(first_norm)
+
+    def up(cols, j):
+        pre = dot(h1b_v[...], wi(cols)) + b_in(j)
+        phi = jnp.exp(pre * pre * -0.5) * 0.3989422804014327
+        cdf = 0.5 + 0.5 * lax.erf(pre * 0.7071067811865476)
+        act = (pre * cdf).astype(BF)
+        act_v[:, cols] = act
+        dg_v[:, cols] = cdf + pre * phi
+        z_v[...] += dot_t(act, wh(cols))
+
+    by_cols(up)
+
+    def second_norm(rows, r):
+        hat, scale = norm_stats(z_v[rows, :])
+        out[rows, :] = (hat * g2[...] + c2[...]).astype(BF)
+        at = first + r * rb + lax.broadcasted_iota(jnp.int32, (rb, width), 0)
+        dy = jnp.where(at < length, cot[rows, :], 0.0)
+        put(2, jnp.sum(dy * hat, axis=0, keepdims=True), True)
+        put(3, jnp.sum(dy, axis=0, keepdims=True), True)
+        dz2 = norm_back(dy * g2[...], hat, scale)
+        put(5, jnp.sum(dz2, axis=0, keepdims=True), True)
+        z_v[rows, :] = dz2
+        hat2_v[rows, :] = dz2.astype(BF)
+
+    by_rows(second_norm)
+    turned()
+    zt_v[...] = hat2_v[...].T
+    ht_v[...] = h1b_v[...].T
+    ready()
+
+    def down(cols, j):
+        put_hid(j, dot(zt_v[...], act_v[:, cols]).astype(BF))
+        dpre = (dot(hat2_v[...], wh(cols)) * dg_v[:, cols]).astype(BF)
+        sums = jnp.sum(dpre.astype(F32), axis=0, keepdims=True)
+        for i in range(step // 128):
+            small[pl.ds(6 * (width // 128) + j * (step // 128) + i, 1), :] = sums[:, i * 128:(i + 1) * 128]
+        put_in(j, dot(ht_v[...], dpre).astype(BF))
+        z_v[...] += dot_t(dpre, wi(cols))
+
+    by_cols(down)
+
+    def first_back(rows, r):
+        dh1, hat = z_v[rows, :], hat1_v[rows, :]
+        put(0, jnp.sum(dh1 * hat, axis=0, keepdims=True), True)
+        put(1, jnp.sum(dh1, axis=0, keepdims=True), True)
+        d = norm_back(dh1 * g1[...], hat, s1_v[rows, 0:1])
+        put(4, jnp.sum(d, axis=0, keepdims=True), True)
+        dz1[rows, :] = d
+        db = d.astype(BF)
+        hat2_v[rows, :] = db
+        dat[rows, :] = dot(db, wo()).astype(BF)
+
+    by_rows(first_back)
+    zt_v[...] = hat2_v[...].T
+    gout[...] = dot(zt_v[...], attn[...]).astype(BF)
+
+
 class Pass:
     def __init__(self, me, own, view, pair, sems, early=False, wide=False):
         self.me, self.own, self.view, self.pair, self.early, self.wide = me, own, view, pair, early, wide
@@ -153,10 +259,15 @@
     return [dma(lead + (2,)), dma(lead + (3,)), dma(lead + (2,))] + [dma(lead or (1,))] * 6
 
 
-def fwd_kernel(deep, x_sh, mask_sh, qkv_sh, out_sh, in_sh, hid_sh, bin_sh, bias, bqv,
-               attn_o, q_o, k_o, v_o, lse_o, x_o, mask_o, qkv_o, out_o, in_o, hid_o, bin_o,
-               x_v, w_v, m_v, q_v, k_v, v_v, a_v, lse_v,
-               loc, xs, xr, as_, ar, *sems):
+def fwd_kernel(deep, x_sh, ml_sh, nz_sh, qkv_sh, out_sh, in_sh, hid_sh, bin_sh, cot_h, bqv, length, *rest):
+    fwd_steps(deep, x_sh, ml_sh, nz_sh, qkv_sh, out_sh, in_sh, hid_sh, bin_sh, cot_h, bqv, length, rest[:6], *rest[6:])
+
+
+def fwd_steps(deep, x_sh, ml_sh, nz_sh, qkv_sh, out_sh, in_sh, hid_sh, bin_sh, cot_h, bqv, length, vec_h,
+               q_o, k_o, v_o, lse_o, x_o, mask_o, qkv_o, gate_o, outs_o, dz1_o, ghid_o, gin_o, gout_o, dat_o, small_o,
+               x_v, w_v, m_v, q_v, k_v, v_v, a_v, lse_v, out_w, in_w, hid_w, bin_v, attn_v, bias,
+               hat1_v, s1_v, h1b_v, ht_v, act_v, dg_v, z_v, hat2_v, zt_v, outs_v, dz1_v, gout_v, dat_v, cot_v, small_v, vec_v,
+               loc, gs, xs, xr, as_, ar, *sems):
     me = Place(deep)
     Z = me.Z
     y, c, z, t = me.y, me.c, me.z, me.t
@@ -176,7 +287,7 @@
                list(q_sems[:3]) + [s.at[0] for s in q_sems[3:]])
 
     def M(h):
-        return Pass(me, mask_sh.at[h], lambda zs, ys, ts: m_v.at[h, zs, ys, c], lambda: m_v.at[h, :, :, c],
+        return Pass(me, m_v.at[h, z, y, c], lambda zs, ys, ts: m_v.at[h, zs, ys, c], lambda: m_v.at[h, :, :, c],
                     [s.at[h] for s in m_sems])
 
     def W(k, shard, whole, early):
@@ -187,15 +298,20 @@
 
         return Pass(me, shard, view, lambda: whole.at[:, :, c], [s.at[k] for s in w_sems], early, True)
 
-    WO, WI, WH = W(0, out_sh, out_o, False), W(1, in_sh, in_o, True), W(2, hid_sh, hid_o, False)
+    WO, WI, WH = W(0, out_sh, out_w, False), W(1, in_sh, in_w, True), W(2, hid_sh, hid_w, False)
 
     locals_ = [
-        pltpu.make_async_copy(qkv_sh, w_v.at[z, y, c], loc.at[0]),
-        pltpu.make_async_copy(x_sh, x_v.at[rows_own], loc.at[1]),
-        pltpu.make_async_copy(mask_sh, m_v.at[:, z, y, c], loc.at[2]),
-        pltpu.make_async_copy(bin_sh, bin_o.at[t], loc.at[3]),
+        pltpu.make_async_copy(qkv_sh, w_v.at[z, y, c], loc.at[17]),
+        pltpu.make_async_copy(x_sh, x_v.at[rows_own], loc.at[16]),
+        pltpu.make_async_copy(bin_sh, bin_v.at[t, 0], loc.at[3]),
     ] + [pltpu.make_async_copy(w.own, w.view(z, y, t), loc.at[4 + k]) for k, w in enumerate((WO, WI, WH))]
-    for cp in locals_:
+    raw = ml_sh.shape
+    mixed = [pltpu.make_async_copy(a, dg_v.at[pl.ds(0, raw[0]), pl.ds(n * raw[1], raw[1])], loc.at[n])
+             for a, n in ((ml_sh, 0), (nz_sh, 1))]
+    late = [pltpu.make_async_copy(cot_h, cot_v, loc.at[2])] + [
+        pltpu.make_async_copy(a, vec_v.at[n], loc.at[18 + n]) for n, a in enumerate(vec_h)]
+    b_out, b_hid, g1, c1, g2, c2 = (vec_v.at[pl.ds(n, 1)] for n in range(6))
+    for cp in mixed + locals_ + late:
         cp.start()
     me.greet()
 
@@ -203,16 +319,16 @@
         return rcopy(x_sh, x_v.at[rows_own], xs.at[0], xr.at[0], me.over_t)
 
     def b_copy():
-        return rcopy(bin_sh, bin_o.at[t], xs.at[1], xr.at[1], me.over_t)
+        return rcopy(bin_sh, bin_v.at[t, 0], xs.at[1], xr.at[1], me.over_t)
 
     def a_cols(p):
         return pl.ds(pl.multiple_of(t * (pairs * 128) + p * 128, 128), 128)
 
     def a_copy(p):
-        return rcopy(a_v.at[p, rows_other], attn_o.at[:, a_cols(p)], as_.at[p], ar.at[p], me.over_t)
+        return rcopy(a_v.at[p, rows_other], attn_v.at[:, a_cols(p)], as_.at[p], ar.at[p], me.over_t)
 
     def a_local(p):
-        return pltpu.make_async_copy(a_v.at[p, rows_own], attn_o.at[:, a_cols(p)], loc.at[7 + p])
+        return pltpu.make_async_copy(a_v.at[p, rows_own], attn_v.at[:, a_cols(p)], loc.at[7 + p])
 
     def mask_save(h):
         return pltpu.make_async_copy(m_v.at[h], mask_o.at[h], loc.at[10 + h])
@@ -221,7 +337,24 @@
     WI.y_copy().start()
     x_copy().start()
     b_copy().start()
+    for cp in mixed:
+        cp.wait()
+    per = raw[0] // heads
+
+    def mask_of(h):
+        rows = pl.ds(pl.multiple_of(h * per, per), per)
+        v = dg_v[rows, 0:raw[1]] + dg_v[rows, raw[1]:2 * raw[1]]
+        m_v[h, z, y, c] = (jnp.minimum(v, 0.0) - jnp.log1p(jnp.exp(-jnp.abs(v)))).astype(BF)
+        dg_v[rows, 2 * raw[1]:3 * raw[1]] = jax.nn.sigmoid(-v)
+
+    mask_of(0)
     M(0).z_start()
+    for h in range(1, heads):
+        mask_of(h)
+    gate_save = pltpu.make_async_copy(dg_v.at[pl.ds(0, raw[0]), pl.ds(2 * raw[1], raw[1])], gate_o, loc.at[0])
+    gate_save.start()
+    key = lax.broadcasted_iota(jnp.int32, bias.shape, 1)
+    bias[...] = jnp.where(key < length[0], 0.0, NEG)
     for cp in locals_:
         cp.wait()
     P_Q.relay()
@@ -263,7 +396,7 @@
 
     lax.fori_loop(0, seq // step, project, 0)
     outs = [
-        pltpu.make_async_copy(q_v, q_o, loc.at[0]),
+        pltpu.make_async_copy(q_v, q_o, loc.at[6]),
         pltpu.make_async_copy(k_v, k_o, loc.at[1]),
         pltpu.make_async_copy(v_v, v_o, loc.at[2]),
         pltpu.make_async_copy(x_v, x_o, loc.at[3]),
@@ -376,60 +509,116 @@
     lse_out.start()
     WO.x_copy().wait_recv()
     WO.c_copy().start()
-    for cp in outs + [lse_out]:
-        cp.wait()
     for p in range(pairs):
         a_local(p).wait()
         a_copy(p).wait()
     b_copy().wait()
+    for cp in late:
+        cp.wait()
+    for w in (WI, WH, WO):
+        w.c_copy().wait_recv()
+
+    quarter = m_v.shape[1:5]
+    deep_w = width // (quarter[0 + 1] * quarter[2] * quarter[3])
+    step = seq // 2
+    flat = width
+
+    def whole(ref, at):
+        return ref[:, :, :, :, at].reshape(flat, -1)
+
+    def slab(j, n):
+        return m_v.at[j, pl.ds(0, deep_w), :, :, :, pl.ds(n * step, step)]
+
+    def save(j, n):
+        out = (ghid_o, gin_o)[n]
+        return pltpu.make_async_copy(slab(j, n), out.at[:, :, :, :, pl.ds(pl.multiple_of(j * step, 128), step)], gs.at[j, n])
+
+    def put(n):
+        def one(j, value):
+            m_v[j, 0:deep_w, :, :, :, n * step:(n + 1) * step] = value.reshape((deep_w,) + quarter[1:] + (step,))
+            save(j, n).start()
+
+        return one
+
+    def ready():
+        for h in range(heads):
+            M(h).finish()
+            mask_save(h).wait()
+
+    outs_save = pltpu.make_async_copy(outs_v, outs_o, loc.at[0])
+    per_t = bin_v.shape[2] // step
+
+    def bin_of(j):
+        return bin_v[j // per_t, :, pl.ds(pl.multiple_of(lax.rem(j, per_t) * step, 128), step)]
+
+    for cp in outs + [lse_out, gate_save]:
+        cp.wait()
+    middle_math(attn_v, lambda rows: x_v[pl.ds(pl.multiple_of(t * half + rows.start, 128), rows.size), :],
+                lambda: whole(out_w, slice(None)), lambda at: whole(in_w, at), lambda at: whole(hid_w, at),
+                b_out, bin_of, b_hid, g1, c1, g2, c2, cot_v, length[0], t * half,
+                outs_v, dz1_v, gout_v, dat_v, small_v, hat1_v, s1_v, h1b_v, ht_v, act_v, dg_v, z_v, hat2_v, zt_v,
+                put(0), put(1), ready, outs_save.start)
+    ends = [pltpu.make_async_copy(a, b, loc.at[1 + n]) for n, (a, b) in enumerate((
+        (dz1_v, dz1_o), (gout_v, gout_o), (dat_v, dat_o), (small_v, small_o)))]
+    for cp in ends:
+        cp.start()
     x_copy().wait_send()
     P_Q.finish()
-    for h in range(heads):
-        M(h).finish()
-        mask_save(h).wait()
     for w in (WO, WI, WH):
         w.finish()
-        w.c_copy().wait_recv()
-
-
-def forward(deep, x, mask, qkv, w_out_t, w_in, w_hid_t, b_in, bias, b_qv):
+    for j in range(heads):
+        for n in range(2):
+            save(j, n).wait()
+    outs_save.wait()
+    for cp in ends:
+        cp.wait()
+
+
+def forward(deep, x, ml, nz, qkv, w_out_t, w_in, w_hid_t, b_in, cot, b_qv, length, vectors):
     half, width = x.shape
     seq = 2 * half
-    heads, blk, _ = mask.shape
+    heads, blk, _ = ml.shape
     pairs = heads // 2
     Z, Y, C = deep // 4, 2, 2
     n_out, n_in = w_out_t.shape[1], w_in.shape[1]
     r = w_in.shape[0]
-    sd = jax.ShapeDtypeStruct
+    wide = 2 * n_in
+    tall = (width // (Y * C * blk), Y, C, blk)
+    rows = 6 * width // 128 + wide // 128
+    rows += -rows % 8
+    sd, vm = jax.ShapeDtypeStruct, pltpu.VMEM
     dma = pltpu.SemaphoreType.DMA
     out_shape = (
-        sd((half, 2 * pairs * 128), BF),
         sd((pairs, seq, 128), BF), sd((pairs, seq, 128), BF), sd((pairs, seq, 128), BF),
         sd((pairs, seq, 128), F32),
         sd((seq, width), BF),
         sd((heads, Z, Y, C, blk, seq), BF),
-        sd((Z, Y, C) + qkv.shape, BF),
-        sd((Z, Y, C, r, 2 * n_out), BF), sd((Z, Y, C, r, 2 * n_in), BF), sd((Z, Y, C, r, 2 * n_in), BF),
-        sd((2,) + b_in.shape, F32),
+        sd((Z, Y, C) + qkv.shape, BF), sd((heads * blk, seq), F32),
+        sd((half, width), BF), sd((half, width), F32), sd(tall + (wide,), BF), sd(tall + (wide,), BF),
+        sd((width, width), BF), sd((half, width), BF), sd((rows, 128), F32),
     )
+    pair = vm((pairs, seq, 128), BF)
     return pl.pallas_call(
         functools.partial(fwd_kernel, deep),
         out_shape=out_shape,
-        in_specs=[ANY] * 7 + [VM, VM],
+        in_specs=[ANY] * 9 + [VM, pl.BlockSpec(memory_space=pltpu.SMEM)] + [ANY] * 6,
         out_specs=[ANY] * len(out_shape),
         scratch_shapes=[
-            pltpu.VMEM((seq, width), BF),
-            pltpu.VMEM((Z, Y, C) + qkv.shape, BF),
-            pltpu.VMEM((heads, Z, Y, C, blk, seq), BF),
-            pltpu.VMEM((pairs, seq, 128), BF), pltpu.VMEM((pairs, seq, 128), BF), pltpu.VMEM((pairs, seq, 128), BF),
-            pltpu.VMEM((pairs, seq, 128), BF),
-            pltpu.VMEM((pairs, seq, 128), F32),
-            dma((16,)), dma((2,)), dma((2,)), dma((pairs,)), dma((pairs,)),
+            vm((seq, width), BF),
+            vm((Z, Y, C) + qkv.shape, BF),
+            vm((heads, Z, Y, C, blk, seq), BF),
+            pair, pair, pair, pair, vm((pairs, seq, 128), F32),
+            vm((Z, Y, C, r, 2 * n_out), BF), vm((Z, Y, C, r, wide), BF), vm((Z, Y, C, r, wide), BF), vm((2, 1) + b_in.shape, F32),
+            vm((half, width), BF), vm((1, seq), F32),
+            vm((half, width), F32), vm((half, 128), F32), vm((half, width), BF), vm((width, half), BF), vm((half, wide), BF), vm((half, wide), F32),
+            vm((half, width), F32), vm((half, width), BF), vm((width, half), BF),
+            vm((half, width), BF), vm((half, width), F32), vm((width, width), BF), vm((half, width), BF), vm((half, width), F32), vm((rows, 128), F32), vm((8, width), F32),
+            dma((24,)), dma((heads, 2)), dma((2,)), dma((2,)), dma((pairs,)), dma((pairs,)),
             *pass_sems(), *pass_sems(heads), *pass_sems(3),
         ],
-        compiler_params=pltpu.CompilerParams(collective_id=1, has_side_effects=True, vmem_limit_bytes=58 << 20),
+        compiler_params=pltpu.CompilerParams(collective_id=1, has_side_effects=True, vmem_limit_bytes=62 << 20),
         name="forward_attention",
-    )(x, mask, qkv, w_out_t, w_in, w_hid_t, b_in, bias, b_qv)
+    )(x, ml.reshape(heads * blk, seq), nz.reshape(heads * blk, seq), qkv, w_out_t, w_in, w_hid_t, b_in, cot, b_qv, length, *vectors)
 
 
 class Fold:
@@ -1209,14 +1398,50 @@
     )
 
 
-def norm_stats(rows):
-    centre = rows - jnp.mean(rows, axis=-1, keepdims=True)
-    scale = lax.rsqrt(jnp.mean(centre * centre, axis=-1, keepdims=True) + EPS)
-    return centre * scale, scale
-
-
-def norm_back(e, hat, scale):
-    return (e - jnp.mean(e, axis=-1, keepdims=True) - hat * jnp.mean(e * hat, axis=-1, keepdims=True)) * scale
+def last_kernel(place, total, *refs):
+    n = (len(refs) - 10) // 3
+    ins, rest = refs[:n], refs[n:]
+    (bqv_o, bin_o), vecs, outs = rest[:2], rest[2:8], rest[8:8 + n]
+    held, tot_v, sems = rest[8 + n:8 + 2 * n], rest[8 + 2 * n], rest[9 + 2 * n]
+    first = pltpu.make_async_copy(total, tot_v, sems.at[n])
+    first.start()
+    loads = [pltpu.make_async_copy(a, b, sems.at[i]) for i, (a, b) in enumerate(zip(ins, held))]
+    saves = [pltpu.make_async_copy(a, b, sems.at[i]) for i, (a, b) in enumerate(zip(held, outs))]
+    for cp in loads:
+        cp.start()
+    for a, b in zip(loads, saves):
+        a.wait()
+        b.start()
+    first.wait()
+    t = place[0]
+    per = vecs[0].shape[0] // 128
+    for k, ref in enumerate(vecs):
+        for i in range(per):
+            ref[pl.ds(i * 128, 128)] = tot_v[k * per + i, :]
+    m = bin_o.shape[0] // 128
+    for i in range(m):
+        bin_o[pl.ds(i * 128, 128)] = tot_v[6 * per + t * m + i, :]
+    base = total.shape[0] - 8
+    nq = bqv_o.shape[1] // 128
+    for j in range(2):
+        for i in range(nq):
+            bqv_o[j:j + 1, i * 128:(i + 1) * 128] = tot_v[base + j * nq + i:base + j * nq + i + 1, :]
+    for cp in saves:
+        cp.wait()
+
+
+def last(t, total, arrays, width, n_bin, bqv_shape):
+    sd, vm = jax.ShapeDtypeStruct, pltpu.VMEM
+    n = len(arrays)
+    return pl.pallas_call(
+        last_kernel,
+        out_shape=(sd(bqv_shape, F32), sd((n_bin,), F32)) + (sd((width,), F32),) * 6 + tuple(sd(a.shape, a.dtype) for a in arrays),
+        in_specs=[pl.BlockSpec(memory_space=pltpu.SMEM)] + [ANY] * (n + 1),
+        out_specs=[VM] * 8 + [ANY] * n,
+        scratch_shapes=[vm(a.shape, a.dtype) for a in arrays] + [vm(total.shape, F32), pltpu.SemaphoreType.DMA((n + 1,))],
+        compiler_params=pltpu.CompilerParams(vmem_limit_bytes=60 << 20),
+        name="hand_over",
+    )(t, total, *arrays)
 
 
 def body(
@@ -1227,60 +1452,18 @@
     x = inputs[0]
     half, width = x.shape
     seq = 2 * half
-    t = lax.axis_index("tensor")
-    length = lengths[0]
-    mixed = mask_logits + noise
-    mask = jax.nn.log_sigmoid(mixed).astype(BF)
-    gate = jax.nn.sigmoid(-mixed)
-    bias = jnp.where(jnp.arange(seq, dtype=jnp.int32) < length, 0.0, NEG).astype(F32)[None]
-    attn, q, k, v, lse, x_all, mask_all, qkv_all, out_all, in_all, hid_all, bin_all = forward(
-        deep, x, mask, w_qkv, w_out.T, w_in, w_hid.T, b_in[None], bias, b_qv)
-    w_out_t = out_all.reshape(width, -1)
-    w_in_all = in_all.reshape(width, -1)
-    w_hid_t = hid_all.reshape(width, -1)
-
-    z1 = x.astype(F32) + dot_t(attn, w_out_t) + b_out
-    hat1, scale1 = norm_stats(z1)
-    h1 = hat1 * ln1_gain + ln1_bias
-    h1b = h1.astype(BF)
-    pre = dot(h1b, w_in_all) + bin_all.reshape(-1)
-    act = gelu_exact(pre).astype(BF)
-    z2 = h1 + dot_t(act, w_hid_t) + b_hid
-    hat2, scale2 = norm_stats(z2)
-    outputs = (hat2 * ln2_gain + ln2_bias).astype(BF)
-
-    rows = t * half + jnp.arange(half, dtype=jnp.int32)
-    dy = cotangent[0] * (rows < length).astype(F32)[:, None]
-    dz2 = norm_back(dy * ln2_gain, hat2, scale2)
-    dz2b = dz2.astype(BF)
-    g_hid = dot_0(dz2b, act).astype(BF)
-    _, pull = jax.vjp(gelu_exact, pre)
-    dpre = pull(dot(dz2b, w_hid_t))[0].astype(BF)
-    g_in = dot_0(h1b, dpre).astype(BF)
-    dh1 = dz2 + dot_t(dpre, w_in_all)
-    dz1 = norm_back(dh1 * ln1_gain, hat1, scale1)
-    dz1b = dz1.astype(BF)
-    g_out = dot_0(dz1b, attn).astype(BF)
-    dattn = dot(dz1b, w_out_t).astype(BF)
-
-    sums = [
-        jnp.sum(dh1 * hat1, axis=0), jnp.sum(dh1, axis=0), jnp.sum(dy * hat2, axis=0), jnp.sum(dy, axis=0),
-        jnp.sum(dz1, axis=0), jnp.sum(dz2, axis=0), jnp.sum(dpre.astype(F32), axis=0),
-    ]
-    flat = jnp.concatenate(sums).reshape(-1, 128)
-    filled = flat.shape[0]
-    small = jnp.pad(flat, ((0, -filled % 8), (0, 0)))
-
+    bias = jnp.where(jnp.arange(seq, dtype=jnp.int32) < lengths[0], 0.0, NEG).astype(F32).reshape(1, seq)
+    vectors = (b_out, b_hid, ln1_gain, ln1_bias, ln2_gain, ln2_bias)
+    q, k, v, lse, x_all, mask_all, qkv_all, gate, outputs, dz1, g_hid, g_in, g_out, dattn, small = forward(
+        deep, x, mask_logits, noise, w_qkv, w_out.T, w_in, w_hid.T, b_in, cotangent[0], b_qv, lengths, vectors)
+    place = (deep // 4, 2, 2, w_in.shape[0])
     dx, gqkv, ghid, gin, gout, gmask, total = backward(
         deep, dattn, q, k, v, mask_all, lse, x_all, qkv_all,
-        g_hid.reshape(hid_all.shape), g_in.reshape(in_all.shape), g_out.reshape(out_all.shape), dz1, gate, small, bias)
-    vec = total[:6 * width // 128].reshape(6, width)
-    g_bin = lax.dynamic_slice_in_dim(total[6 * width // 128:filled].reshape(-1), t * b_in.shape[0], b_in.shape[0])
-    g_bqv = total[small.shape[0]:small.shape[0] + 2 * b_qv.shape[1] // 128].reshape(b_qv.shape)
-    return (
-        outputs[None], dx[None], gqkv, g_bqv, gout.T, vec[4], vec[0], vec[1], gin, g_bin, ghid.T, vec[5],
-        vec[2], vec[3], gmask,
-    )
+        g_hid.reshape(place + (-1,)), g_in.reshape(place + (-1,)), g_out.reshape(place + (-1,)), dz1, gate.reshape(mask_logits.shape), small, bias)
+    t = lax.axis_index("tensor").astype(jnp.int32).reshape(1)
+    g_bqv, g_bin, v0, v1, v2, v3, v4, v5, outputs, dx, gqkv, gout, gin, ghid, gmask = last(
+        t, total, (outputs, dx, gqkv, gout, gin, ghid, gmask), width, b_in.shape[0], b_qv.shape)
+    return (outputs[None], dx[None], gqkv, g_bqv, gout.T, v4, v0, v1, gin, g_bin, ghid.T, v5, v2, v3, gmask)
 
 
 def solution(mesh):

time: 342 us -> 295 us (0.86)
  matrix products: 49 us -> 0 us
  Pallas kernels: 269 us -> 292 us
  local copies, waits for them, and re-layouts: 11.8 us -> 0 us
  other arithmetic: 10.2 us -> 0.6 us
    dot_general x9 -> x0, matrix products: 49 us -> none  [the longest x3 29.2 us: dot(): return jnp.dot(a, b, preferred_element_type=F32)]
    pallas_call x1, Pallas kernels: 134 us -> 152 us  [forward(): pl.pallas_call(functools.partial(fwd_kernel, deep), out_shape=out_shape,...]
    unnamed x72 -> x0, local copies, waits for them, and re-layouts: 7.16 us -> none
    reduce_sum x5 -> x0, other arithmetic: 5.1 us -> none  [the longest x1 2.4 us: body(): jnp.sum(dy * hat2, axis=0)]
    pallas_call x0 -> x1, Pallas kernels: none -> 4.67 us  [last(): pl.pallas_call(last_kernel, out_shape=(sd(bqv_shape, F32), sd((n_bin,), F...]
    div x6 -> x0, other arithmetic: 4.52 us -> none  [the longest x1 4.49 us: body(): gate = jax.nn.sigmoid(-mixed)]
where the time goes in v3:
time: 295 us; the launch traced here: 294 us
  Pallas kernels  292 us (99%)
    pallas_call x1, Pallas kernels, forward(): pl.pallas_call(functools.partial(fwd_kernel, deep), out_shape=out_shape,...  152 us
    pallas_call x1, Pallas kernels, backward(): pl.pallas_call(functools.partial(bwd_kernel, deep), out_shape=out_shape,...  135 us

profile of v3, /device:TPU:0, one launch (start us, length us, event | category | flops | bytes accessed | tf_op | source)
XLA Modules:
  0.0 294.4 jit_solution(15575992604680341652)
XLA Ops:
  1.3 152.2 %forward_attention.1 = (bf16[3,1024,128]{2,1,0:T(8,128)(2,1)}, bf16[3,1024,128]{2,1,0:T(8,128)(2,1)}, bf16[3,1024,128]{2,1,0:T(8,128)(2,1)}, f32[3,1024,128]{2,1...) custom-call(bf16[512,768]{1,0:T(8,128)(2,1)} %bitcast.24, ...), custom_call_target="tpu_custom_call" | custom-call | tf_op jit(solution)/shard_map/forward_attention/pallas_call | solution.py:601
  153.5 0.6 compare_select_fusion.bias
  154.1 135.4 %backward_attention.1 = (f32[512,768]{1,0:T(8,128)}, f32[3,48,384]{2,1,0:T(8,128)}, f32[48,1536]{1,0:T(8,128)}, f32[48,1536]{1,0:T(8,128)}, f32[48,384]{1,0:T(8,...) custom-call(bf16[512,768]{1,0:T(8,128)(2,1)} %get-tuple-element.52.dat, bf16[3,1024,128]{2,1,0:T(8,128)(2,1)} %get-tuple-element.53.q_h, ...), custom_call_target="tpu_custom_call" | custom-call | tf_op jit(solution)/shard_map/backward_attention/pallas_call | solution.py:1118
  289.5 4.7 %hand_over.1 = (f32[2,384]{1,0:T(2,128)}, f32[1536]{0:T(1024)}, f32[768]{0:T(1024)}, f32[768]{0:T(1024)}, f32[768]{0:T(1024)}, /*index=5*/f32[768]{0:T(1024)}, f...) custom-call(s32[1]{0:T(128)} %bitcast.place, ...), custom_call_target="tpu_custom_call" | custom-call | tf_op jit(solution)/shard_map/hand_over/pallas_call | solution.py:1436

commit v4 on v3

--- a/solution.py
+++ b/solution.py
@@ -349,10 +349,7 @@
 
     mask_of(0)
     M(0).z_start()
-    for h in range(1, heads):
-        mask_of(h)
     gate_save = pltpu.make_async_copy(dg_v.at[pl.ds(0, raw[0]), pl.ds(2 * raw[1], raw[1])], gate_o, loc.at[0])
-    gate_save.start()
     key = lax.broadcasted_iota(jnp.int32, bias.shape, 1)
     bias[...] = jnp.where(key < length[0], 0.0, NEG)
     for cp in locals_:
@@ -361,6 +358,7 @@
     P_Q.z_wait()
     P_Q.y_copy().start()
     WH.z_start()
+    mask_of(1)
     M(0).relay()
     M(0).z_wait()
     M(0).y_copy().start()
@@ -370,6 +368,9 @@
     WH.z_wait()
     WH.y_copy().start()
     M(1).z_start()
+    for h in range(2, heads):
+        mask_of(h)
+    gate_save.start()
     P_Q.y_copy().wait_recv()
     P_Q.c_copy().start()
     x_copy().wait_recv()
@@ -410,7 +411,13 @@
         h = 2 * p + u
         sl = slice(64 * u, 64 * u + 64)
 
-        def rows_of(b, carry):
+        def rows_of(n, carry):
+            b = lax.rem((1 - t) * (Z // 2) + n, Z)
+            if u == 1:
+                @pl.when(n == Z // 2)
+                def _():
+                    a_copy(p).start()
+
             rows = pl.ds(pl.multiple_of(b * blk, blk), blk)
             s = dot_t(q_v[p, rows, sl], k_v[p, :, sl])
             s = s + m_v[h, b].reshape(blk, seq).astype(F32) + bias[...]
@@ -500,7 +507,6 @@
             M(h).c_copy().wait_recv()
             mask_save(h).start()
             attend(p, u)
-        a_copy(p).start()
         a_local(p).start()
         return carry
 
@@ -749,7 +755,7 @@
 def bwd_kernel(deep, dat, q_h, k_h, v_h, mask_h, lse_h, x_h, qkv_h, hid_h, in_h, out_h, dz1_h, sg_h, small_h, bias,
                dx_o, gqkv_o, ghid_o, gin_o, gout_o, gmask_o, small_o,
                q_v, k_v, v_v, do_v, lse_v, m_v, p_v, dq_v, dk_v, dv_v, acck, accv,
-               lc_m, ly_m, lz_m, lr_m, gm_v,
+               lc_m, ly_m, lz_m, lr_m, lz_e, lr_e, gm_v,
                own_w, lc_hid, lx_hid, ly_hid, lz_hid, lr_hid, lc_in, lx_in, ly_in, lz_in, lr_in, lc_out, lx_out, ly_out, lz_out, lr_out,
                fin_hid, fin_in, fin_out,
                p_q, lc_q, ly_q, lz_q, lr_q, fin_q,
@@ -787,6 +793,8 @@
         return pltpu.make_async_copy(gm_v.at[h], gmask_o.at[h], loc.at[17 + h])
 
     def M(h, slot=None):
+        early = isinstance(h, int) and h == 1
+
         def own(i, j):
             return p_v[slot, i, j, c]
 
@@ -797,7 +805,8 @@
 
         away = None if slot is None else p_v.at[slot, :, :, 1 - c]
         return Fold(me, own, p_v.at[0, :, :, 1 - c] if away is None else away, lc_m.at[h],
-                    (ly_m.at[h], lz_m.at[h], lr_m.at[h]), (lambda n: m_s.at[h, n], lambda n: m_r.at[h, n]), final)
+                    (ly_m.at[h, 0], lz_e, lr_e) if early else (ly_m.at[h], lz_m.at[h], lr_m.at[h]),
+                    (lambda n: m_s.at[h, n], lambda n: m_r.at[h, n]), final, early=early)
 
     def W(k, part, lc, lx, ly, lz, lr, fin, out, early):
         n = lx.shape[-1]
@@ -859,7 +868,7 @@
         w.c_copy().start()
     for h in range(heads):
         sg_load(h).start()
-    for cp in loads:
+    for cp in loads[:4]:
         cp.wait()
 
     blk = seq // Z
@@ -876,6 +885,20 @@
                 @pl.when(n == Z // 2)
                 def _():
                     dat_copy(p).wait_recv()
+
+                @pl.when(jnp.logical_and(n == Z // 2, p == 0))
+                def _():
+                    WH.own_load().wait()
+                    WH.c_add()
+                    WI.own_load().start()
+                    WH.x_copy().start()
+
+                @pl.when(jnp.logical_and(n == Z // 2 + 1, p == 0))
+                def _():
+                    WI.own_load().wait()
+                    WI.c_add()
+                    WO.own_load().start()
+                    WI.x_copy().start()
 
             rows = pl.ds(pl.multiple_of(b * blk, blk), blk)
             qb, dob = q_v[p, rows, sl], do_v[p, rows, sl]
@@ -897,27 +920,20 @@
         dv_v[p, :, sl] = accv[...].astype(BF)
 
     def after_0():
-        WH.own_load().wait()
-        WH.c_add()
-        WI.own_load().start()
-        WH.x_copy().start()
         M(0, 0).c_add()
-        M(0).y_copy().start()
-
-    def after_1():
-        WI.own_load().wait()
-        WI.c_add()
-        WO.own_load().start()
-        WI.x_copy().start()
-        M(1, 1).c_add()
-        M(1).y_copy().start()
-
-    def after_2():
         WO.own_load().wait()
         WO.c_add()
         WO.x_copy().start()
+        M(0).y_copy().start()
+
+    def after_1():
+        M(1, 1).c_add()
+        M(1).z_start()
+
+    def after_2():
         M(2, 0).c_add()
         M(2).y_copy().start()
+        M(1).relay()
         M(0).y_add()
         M(0).z_start()
 
@@ -929,17 +945,18 @@
         M(0).relay()
 
     def after_4():
-        M(1).y_add()
-        M(1).z_start()
         M(4, 0).c_add()
         M(4).y_copy().start()
-
-    def after_5():
-        M(1).relay()
         M(2).y_add()
         M(2).z_start()
+        M(1).early_z_end()
+
+    def after_5():
         M(5, 1).c_add()
         M(5).y_copy().start()
+        M(2).relay()
+        M(3).y_add()
+        M(3).z_start()
 
     after = (after_0, after_1, after_2, after_3, after_4, after_5)
 
@@ -966,6 +983,8 @@
         return carry
 
     lax.fori_loop(0, pairs, pair_step, 0)
+    for cp in loads[4:]:
+        cp.wait()
 
     step = half // 2
 
@@ -988,12 +1007,18 @@
 
     lax.fori_loop(0, 2, theirs, 0)
     x_copy().start()
+    M(3).relay()
+    WI.x_add()
+    WI.z_start()
+    M(0).z_end()
+    WO.x_add()
+    WO.y_copy().start()
 
     for j, ref in enumerate((dq_v, dk_v, dv_v)):
         g = dot_0(x_v[...], d_cat(ref, slice(None)))
         p_q[:, :, :, j] = g.astype(BF).reshape(p_q.shape[:3] + p_q.shape[4:])
     Q.c_copy().start()
-    M(2).relay()
+    WI.relay()
     base = small_h.shape[0]
     for n, ref in enumerate((dq_v, dv_v)):
         for p in range(pairs):
@@ -1015,18 +1040,8 @@
     s_c().wait_recv()
     sc_v[...] = sc_v[...] + s_v[...]
     s_y().start()
-    M(3).y_add()
-    M(3).z_start()
-    WI.x_add()
-    WI.z_start()
-    M(0).z_end()
-    WO.x_add()
-    WO.y_copy().start()
-    M(3).relay()
-    WI.relay()
     WH.y_add()
     WH.z_start()
-    M(1).z_end()
     M(2).z_end()
     M(4).y_add()
     M(4).z_start()
@@ -1063,6 +1078,7 @@
     s_v[...] = total
     s_x().start()
     M(5).z_end()
+    M(1).early_y_end()
     WI.early_y_end()
     Q.z_end()
     WO.z_end()
@@ -1124,7 +1140,7 @@
             pair, pair, pair, pair, vm((pairs, seq, 128), F32), vm((2, Z, Y, C, blk, seq), BF), vm((2, Z, Y, C, blk, seq), BF),
             pair, pair, pair, vm((seq, 64), F32), vm((seq, 64), F32),
             vm((heads, Z, Y, blk, seq), BF), vm((heads, Z, blk, seq), BF), vm((heads, 2, blk, seq), BF), vm((heads, 2, blk, seq), BF),
-            vm((heads, blk, seq), F32),
+            vm((2, Y, blk, seq), BF), vm((2, Y, blk, seq), BF), vm((heads, blk, seq), F32),
             vm((Z, Y, r, n2), BF), *chain(n, False), *chain(n, True), *chain(no, False), vm((r, n), F32), vm((r, n), F32), vm((r, no), F32),
             vm((Z, Y, C, three, rq, nq), BF), vm((Z, Y, three, rq, nq), BF), vm((Z, three, rq, nq), BF),
             vm((2, three, rq, nq), BF), vm((2, three, rq, nq), BF), vm((three, rq, nq), F32),

time: 295 us -> 289 us (0.980)
  Pallas kernels: 292 us -> 287 us
    pallas_call x1, Pallas kernels: 135 us -> 130 us  [backward(): pl.pallas_call(functools.partial(bwd_kernel, deep), out_shape=out_shape,...]
where the time goes in v4:
time: 289 us
  Pallas kernels  287 us (99%)
    pallas_call x1, Pallas kernels, forward(): pl.pallas_call(functools.partial(fwd_kernel, deep), out_shape=out_shape,...  152 us
    pallas_call x1, Pallas kernels, backward(): pl.pallas_call(functools.partial(bwd_kernel, deep), out_shape=out_shape,...  130 us

profile of v4, /device:TPU:0, one launch (start us, length us, event | category | flops | bytes accessed | tf_op | source)
XLA Modules:
  0.0 289.1 jit_solution(4765050894224893824)
XLA Ops:
  1.3 152.3 %forward_attention.1 = (bf16[3,1024,128]{2,1,0:T(8,128)(2,1)}, bf16[3,1024,128]{2,1,0:T(8,128)(2,1)}, bf16[3,1024,128]{2,1,0:T(8,128)(2,1)}, f32[3,1024,128]{2,1...) custom-call(bf16[512,768]{1,0:T(8,128)(2,1)} %bitcast.24, ...), custom_call_target="tpu_custom_call" | custom-call | tf_op jit(solution)/shard_map/forward_attention/pallas_call | solution.py:607
  153.6 0.6 compare_select_fusion.bias
  154.2 130.0 %backward_attention.1 = (f32[512,768]{1,0:T(8,128)}, f32[3,48,384]{2,1,0:T(8,128)}, f32[48,1536]{1,0:T(8,128)}, f32[48,1536]{1,0:T(8,128)}, f32[48,384]{1,0:T(8,...) custom-call(bf16[512,768]{1,0:T(8,128)(2,1)} %get-tuple-element.52.dat, bf16[3,1024,128]{2,1,0:T(8,128)(2,1)} %get-tuple-element.53.q_h, ...), custom_call_target="tpu_custom_call" | custom-call | tf_op jit(solution)/shard_map/backward_attention/pallas_call | solution.py:1134
  284.2 4.7 %hand_over.1 = (f32[2,384]{1,0:T(2,128)}, f32[1536]{0:T(1024)}, f32[768]{0:T(1024)}, f32[768]{0:T(1024)}, f32[768]{0:T(1024)}, /*index=5*/f32[768]{0:T(1024)}, f...) custom-call(s32[1]{0:T(128)} %bitcast.place, ...), custom_call_target="tpu_custom_call" | custom-call | tf_op jit(solution)/shard_map/hand_over/pallas_call | solution.py:1452

commit v5 on v4

--- a/solution.py
+++ b/solution.py
@@ -91,7 +91,7 @@
                 put_hid, put_in, ready, turned):
     half, width = hat1_v.shape
     wide = act_v.shape[1]
-    rb, step = half // 2, 512
+    rb, step = half, 512
 
     def by_rows(body):
         def one(r, carry):
@@ -105,7 +105,7 @@
             body(pl.ds(pl.multiple_of(j * step, step), step), j)
             return carry
 
-        lax.fori_loop(0, wide // step, one, 0)
+        lax.fori_loop(0, wide // step, one, 0, unroll=3)
 
     def put(n, vec, add):
         for i in range(width // 128):
@@ -429,7 +429,7 @@
             lse_v[p, rows, u:u + 1] = top + jnp.log(total)
             return carry
 
-        lax.fori_loop(0, Z, rows_of, 0)
+        lax.fori_loop(0, Z, rows_of, 0, unroll=2)
 
     def with_0():
         M(1).relay()
@@ -915,7 +915,7 @@
             accv[...] += dot_0(pr.astype(BF), dob)
             return carry
 
-        lax.fori_loop(0, Z, rows_of, 0)
+        lax.fori_loop(0, Z, rows_of, 0, unroll=2)
         dk_v[p, :, sl] = acck[...].astype(BF)
         dv_v[p, :, sl] = accv[...].astype(BF)
 

time: 289 us -> 286 us (0.990)
  Pallas kernels: 287 us -> 283 us
where the time goes in v5:
time: 286 us
  Pallas kernels  283 us (99%)
    pallas_call x1, Pallas kernels, forward(): pl.pallas_call(functools.partial(fwd_kernel, deep), out_shape=out_shape,...  150 us
    pallas_call x1, Pallas kernels, backward(): pl.pallas_call(functools.partial(bwd_kernel, deep), out_shape=out_shape,...  129 us

profile of v5, /device:TPU:0, one launch (start us, length us, event | category | flops | bytes accessed | tf_op | source)
XLA Modules:
  0.0 285.5 jit_solution(5994342254421418430)
XLA Ops:
  1.3 149.9 %forward_attention.1 = (bf16[3,1024,128]{2,1,0:T(8,128)(2,1)}, bf16[3,1024,128]{2,1,0:T(8,128)(2,1)}, bf16[3,1024,128]{2,1,0:T(8,128)(2,1)}, f32[3,1024,128]{2,1...) custom-call(bf16[512,768]{1,0:T(8,128)(2,1)} %bitcast.24, ...), custom_call_target="tpu_custom_call" | custom-call | tf_op jit(solution)/shard_map/forward_attention/pallas_call | solution.py:607
  151.2 0.6 compare_select_fusion.bias
  151.8 128.8 %backward_attention.1 = (f32[512,768]{1,0:T(8,128)}, f32[3,48,384]{2,1,0:T(8,128)}, f32[48,1536]{1,0:T(8,128)}, f32[48,1536]{1,0:T(8,128)}, f32[48,384]{1,0:T(8,...) custom-call(bf16[512,768]{1,0:T(8,128)(2,1)} %get-tuple-element.52.dat, bf16[3,1024,128]{2,1,0:T(8,128)(2,1)} %get-tuple-element.53.q_h, ...), custom_call_target="tpu_custom_call" | custom-call | tf_op jit(solution)/shard_map/backward_attention/pallas_call | solution.py:1134
  280.7 4.7 %hand_over.1 = (f32[2,384]{1,0:T(2,128)}, f32[1536]{0:T(1024)}, f32[768]{0:T(1024)}, f32[768]{0:T(1024)}, f32[768]{0:T(1024)}, /*index=5*/f32[768]{0:T(1024)}, f...) custom-call(s32[1]{0:T(128)} %bitcast.place, ...), custom_call_target="tpu_custom_call" | custom-call | tf_op jit(solution)/shard_map/hand_over/pallas_call | solution.py:1452

commit v6 on v5

--- a/solution.py
+++ b/solution.py
@@ -1030,13 +1030,6 @@
     Q.c_add()
     Q.y_copy().start()
 
-    def mine(r, carry):
-        at = pl.ds(pl.multiple_of(r * step, step), step)
-        rows = pl.ds(pl.multiple_of(t * half + r * step, step), step)
-        dx_v[at, :] = terms(rows) + dz_v[at, :]
-        return carry
-
-    lax.fori_loop(0, 2, mine, 0)
     s_c().wait_recv()
     sc_v[...] = sc_v[...] + s_v[...]
     s_y().start()
@@ -1051,6 +1044,14 @@
     M(4).relay()
     M(5).y_add()
     M(5).z_start()
+
+    def mine(r, carry):
+        at = pl.ds(pl.multiple_of(r * step, step), step)
+        rows = pl.ds(pl.multiple_of(t * half + r * step, step), step)
+        dx_v[at, :] = terms(rows) + dz_v[at, :]
+        return carry
+
+    lax.fori_loop(0, 2, mine, 0)
     s_y().wait_recv()
     sy_v[...] = sy_v[...] + sc_v[...]
     sz_v[z] = sy_v[...]

time: 286 us -> 286 us (level)
  no operation moved by 1% of the time
where the time goes in v6:
time: 286 us
  Pallas kernels  283 us (99%)
    pallas_call x1, Pallas kernels, forward(): pl.pallas_call(functools.partial(fwd_kernel, deep), out_shape=out_shape,...  150 us
    pallas_call x1, Pallas kernels, backward(): pl.pallas_call(functools.partial(bwd_kernel, deep), out_shape=out_shape,...  129 us

profile of v6, /device:TPU:0, one launch (start us, length us, event | category | flops | bytes accessed | tf_op | source)
XLA Modules:
  0.0 285.5 jit_solution(935480402833265169)
XLA Ops:
  1.3 149.9 %forward_attention.1 = (bf16[3,1024,128]{2,1,0:T(8,128)(2,1)}, bf16[3,1024,128]{2,1,0:T(8,128)(2,1)}, bf16[3,1024,128]{2,1,0:T(8,128)(2,1)}, f32[3,1024,128]{2,1...) custom-call(bf16[512,768]{1,0:T(8,128)(2,1)} %bitcast.24, ...), custom_call_target="tpu_custom_call" | custom-call | tf_op jit(solution)/shard_map/forward_attention/pallas_call | solution.py:607
  151.2 0.6 compare_select_fusion.bias
  151.8 128.8 %backward_attention.1 = (f32[512,768]{1,0:T(8,128)}, f32[3,48,384]{2,1,0:T(8,128)}, f32[48,1536]{1,0:T(8,128)}, f32[48,1536]{1,0:T(8,128)}, f32[48,384]{1,0:T(8,...) custom-call(bf16[512,768]{1,0:T(8,128)(2,1)} %get-tuple-element.52.dat, bf16[3,1024,128]{2,1,0:T(8,128)(2,1)} %get-tuple-element.53.q_h, ...), custom_call_target="tpu_custom_call" | custom-call | tf_op jit(solution)/shard_map/backward_attention/pallas_call | solution.py:1135
  280.7 4.7 %hand_over.1 = (f32[2,384]{1,0:T(2,128)}, f32[1536]{0:T(1024)}, f32[768]{0:T(1024)}, f32[768]{0:T(1024)}, f32[768]{0:T(1024)}, /*index=5*/f32[768]{0:T(1024)}, f...) custom-call(s32[1]{0:T(128)} %bitcast.place, ...), custom_call_target="tpu_custom_call" | custom-call | tf_op jit(solution)/shard_map/hand_over/pallas_call | solution.py:1453
